TPU v7x, 256 devices: a whole 4x4x8 slice. The times are simulated.
256 devices in a mesh: fsdp: 16 (over z_hi, x, core), dp: 16 (over z_lo, y).
Axes of the slice: x: 4, y: 4, z: 8 (z_hi: 2, z_lo: 4; z = z_hi * 4 + z_lo), core: 2. Of those that a mesh axis runs over, the one named last changes fastest.
Arguments:
- x_pre: bfloat16 [32768, 4096], P(('fsdp', 'dp')), may hold values from -6 to 6
- x_dec: bfloat16 [1024, 4096], P(('fsdp', 'dp')), may hold values from -6 to 6
- rec_hidden: bfloat16 [81920, 4096], P(('fsdp', 'dp')), may hold values from -6 to 6
- norm_gain: bfloat16 [4096], replicated, may hold values from 0.099609375 to 1.8984375
- w_query: bfloat16 [4096, 2048], P(('fsdp', 'dp')), may hold values from -1 to 1
- key_value_weight: bfloat16 [4096, 512], P(('fsdp', 'dp')), may hold values from -0.09375 to 0.09375
- cache_pool: bfloat16 [21504, 64, 512], P(('fsdp', 'dp')), may hold values from -12 to 12
- shared_kv: bfloat16 [131072, 512], P(('fsdp', 'dp')), may hold values from -12 to 12
- dec_len: int32 [256, 4], P(('fsdp', 'dp')), may hold values from 1 to 3072, as said below
- dec_table: int32 [256, 4, 48], P(('fsdp', 'dp')), may hold values from 0 to 83, as said below
- dec_group: int32 [256, 4], P(('fsdp', 'dp')), may hold values from 0 to 15, as said below
- prefix_len: int32 [16, 16], P('fsdp'), may hold values from 1 to 512, as said below
- pre_start: int32 [256], P(('fsdp', 'dp')), may hold values from 0 to 1024, as said below
- pre_table: int32 [256, 16], P(('fsdp', 'dp')), may hold values from 0 to 83, as said below
- rec_req: int32 [256, 320], P(('fsdp', 'dp')), may hold values from 0 to 3, as said below
- rec_off: int32 [256, 320], P(('fsdp', 'dp')), may hold values from 0 to 3071, as said below
Outputs:
- out_pre: bfloat16 [32768, 2048], P(('fsdp', 'dp'))
- out_dec: bfloat16 [1024, 2048], P(('fsdp', 'dp'))
Inputs may be any that keep to these rules, and one draw needn't show every extreme that they name: `dec_len`: the private lengths of one device's decode requests sum to 4096; each device has one request of length exactly 3072. `dec_table`: the pages of one device's decode requests (the first ceil(dec_len / 64) entries of each row) and of its prefill history (the first pre_start / 64 entries) are all different; later entries are valid page numbers. `pre_table`: same pages as stated for dec_table. `dec_group`: A group names a device with the same fsdp index; a few groups along a line are far more common than the others. `prefix_len`: in every fsdp line some device holds a prefix of length exactly 512. `pre_start`: A multiple of 64; some device starts at exactly 1024. `rec_req`: the recomputed tokens of one device are different tokens of its decode requests. `rec_off`: below the request's dec_len.
All inputs are finite; a program needn't handle non-finite values.
Results may differ from a plain program's by a relative error of at most 0.0073.
Values may be sent and summed in bfloat16 or wider, within the bound.
No kernel may reach another device: no remote copies, remote signals or barrier semaphores. Data moves between devices by JAX's collectives and lax.ppermute only.
A program may use at most 192 MiB of HBM per device.

v0:
```python
import jax
import jax.numpy as jnp
from jax import lax
from jax.sharding import PartitionSpec as P

QUERY_HEADS = 16
KEY_VALUE_HEADS = 2
HEAD_SIZE = 128
PAGE_TOKENS = 64


theta_base = 5000000.0
epsilon = 1e-05
negative_large = -1e30


def rms_scaled(values, gain):
    widened = values.astype(jnp.float32)
    factor = lax.rsqrt(jnp.mean(widened * widened, axis=-1, keepdims=True) + epsilon)
    return (widened * factor * gain.astype(jnp.float32)).astype(jnp.bfloat16)


def rotate_halves(vectors, positions):
    half_dim = vectors.shape[-1] // 2
    frequency = theta_base ** (-jnp.arange(half_dim, dtype=jnp.float32) * 2.0 / vectors.shape[-1])
    angles = positions.astype(jnp.float32)[:, None, None] * frequency
    cosines = jnp.cos(angles)
    sines = jnp.sin(angles)
    first_half = vectors[..., :half_dim]
    second_half = vectors[..., half_dim:]
    return jnp.concatenate(
        [first_half * cosines - second_half * sines, second_half * cosines + first_half * sines],
        axis=-1,
    )


def small_lookup(entries, indices):
    matches = indices[..., None] == jnp.arange(entries.shape[0], dtype=jnp.int32)
    return jnp.sum(jnp.where(matches, entries, 0), axis=-1)


def attend_portion(query, keys, values, visible_mask, per_request):
    if per_request:
        score_form = "qojv,qeov->qoje"
        value_form = "wucm,wmuf->wucf"
    else:
        score_form = "rkgd,tkd->rkgt"
        value_form = "rkgt,tkd->rkgd"
    score_matrix = jnp.einsum(
        score_form, query, keys, preferred_element_type=jnp.float32
    ) * query.shape[-1] ** (-0.5)
    allowed = visible_mask[:, None, None, :]
    masked = jnp.where(allowed, score_matrix, negative_large)
    maxima = jnp.max(masked, axis=-1)
    weight_matrix = jnp.where(allowed, jnp.exp(masked - maxima[..., None]), 0.0)
    totals = jnp.sum(weight_matrix, axis=-1)
    summed_output = jnp.einsum(
        value_form, weight_matrix, values.astype(jnp.float32), precision=lax.Precision.HIGHEST
    )
    return (maxima, totals, summed_output)


def combine(first_part, second_part):
    maxima = jnp.maximum(first_part[0], second_part[0])
    left_scale = jnp.exp(first_part[0] - maxima)
    right_scale = jnp.exp(second_part[0] - maxima)
    totals = first_part[1] * left_scale + second_part[1] * right_scale
    summed_output = first_part[2] * left_scale[..., None] + second_part[2] * right_scale[..., None]
    return (maxima, totals, summed_output)


def on_device(
    x_pre,
    x_dec,
    rec_hidden,
    norm_gain,
    w_query,
    key_value_weight,
    cache_pool,
    shared_kv,
    dec_len,
    dec_table,
    dec_group,
    prefix_len,
    pre_start,
    pre_table,
    rec_req,
    rec_off,
):
    group_share = QUERY_HEADS // KEY_VALUE_HEADS
    key_value_width = KEY_VALUE_HEADS * HEAD_SIZE
    prefill_count = x_pre.shape[0]
    decode_count = x_dec.shape[0]
    lengths = dec_len[0]
    page_table = dec_table[0]
    groups = dec_group[0]
    prefix_line = prefix_len[0]
    request = rec_req[0]
    within = rec_off[0]
    query_rows = jnp.concatenate(
        [rms_scaled(x_pre, norm_gain), rms_scaled(x_dec, norm_gain)], axis=0
    )
    key_value_rows = jnp.concatenate([query_rows, rms_scaled(rec_hidden, norm_gain)], axis=0)
    whole_query, whole_keyval = (
        lax.all_gather(w_query, ("fsdp", "dp"), axis=0, tiled=True),
        lax.all_gather(key_value_weight, ("fsdp", "dp"), axis=0, tiled=True),
    )
    query_proj = jnp.dot(query_rows, whole_query, preferred_element_type=jnp.float32)
    key_value_projected = jnp.dot(key_value_rows, whole_keyval, preferred_element_type=jnp.float32)
    pre_pos = pre_start[0] + jnp.arange(prefill_count, dtype=jnp.int32)
    dec_pos = small_lookup(prefix_line, groups) + lengths
    rec_pos = small_lookup(prefix_line, small_lookup(groups, request)) + within
    query_pos = jnp.concatenate([pre_pos, dec_pos], axis=0)
    query_matrix = rotate_halves(query_proj.reshape(-1, QUERY_HEADS, HEAD_SIZE), query_pos).astype(
        jnp.bfloat16
    )
    key_value_positions = jnp.concatenate([query_pos, rec_pos], axis=0)
    key_value_heads = key_value_projected.reshape(-1, 2 * KEY_VALUE_HEADS, HEAD_SIZE)
    new_key_value = jnp.concatenate(
        [
            rotate_halves(key_value_heads[:, :KEY_VALUE_HEADS], key_value_positions),
            key_value_heads[:, KEY_VALUE_HEADS:],
        ],
        axis=1,
    ).astype(jnp.bfloat16)
    added_rows = new_key_value.reshape(-1, 2 * key_value_width)
    max_pages = page_table.shape[1]
    rec_page = page_table.reshape(-1)[request * max_pages + within // PAGE_TOKENS]
    flattened_pool = cache_pool.reshape(-1, 2 * key_value_width)
    flattened_pool = flattened_pool.at[rec_page * PAGE_TOKENS + within % PAGE_TOKENS].set(
        added_rows[prefill_count + decode_count :]
    )
    slot_range = jnp.arange(PAGE_TOKENS, dtype=jnp.int32)
    private_lookup = (page_table[:, :, None] * PAGE_TOKENS + slot_range).reshape(decode_count, -1)
    private_keys = flattened_pool[private_lookup].reshape(
        decode_count, -1, 2 * KEY_VALUE_HEADS, HEAD_SIZE
    )
    private_seen = jnp.arange(private_keys.shape[1], dtype=jnp.int32)[None, :] < lengths[:, None]
    decode_query = query_matrix[prefill_count:].reshape(
        decode_count, KEY_VALUE_HEADS, group_share, HEAD_SIZE
    )
    private_part = attend_portion(
        decode_query,
        private_keys[:, :, :KEY_VALUE_HEADS],
        private_keys[:, :, KEY_VALUE_HEADS:],
        private_seen,
        True,
    )
    fresh_keys = new_key_value[prefill_count : prefill_count + decode_count][:, None]
    fresh_part = attend_portion(
        decode_query,
        fresh_keys[:, :, :KEY_VALUE_HEADS],
        fresh_keys[:, :, KEY_VALUE_HEADS:],
        jnp.ones((decode_count, 1), dtype=bool),
        True,
    )
    local_part = combine(private_part, fresh_part)
    span = shared_kv.shape[0]
    start_portion = (
        jnp.full((decode_count, KEY_VALUE_HEADS, group_share), negative_large, jnp.float32),
        jnp.zeros((decode_count, KEY_VALUE_HEADS, group_share), jnp.float32),
        jnp.zeros((decode_count, KEY_VALUE_HEADS, group_share, HEAD_SIZE), jnp.float32),
    )
    slice_portion = lax.all_gather(shared_kv, "dp", axis=0, tiled=True)
    row_counter = slice_portion.shape[0]
    row_ids = jnp.arange(row_counter, dtype=jnp.int32)
    owner_ids = row_ids // span
    limits = small_lookup(prefix_line, owner_ids)
    visible_mask = (owner_ids[None, :] == groups[:, None]) & (row_ids % span < limits)[None, :]
    head_groups = slice_portion.reshape(row_counter, 2 * KEY_VALUE_HEADS, HEAD_SIZE)
    shared_part = combine(
        start_portion,
        attend_portion(
            decode_query,
            head_groups[:, :KEY_VALUE_HEADS],
            head_groups[:, KEY_VALUE_HEADS:],
            visible_mask,
            False,
        ),
    )
    final_part = combine(local_part, shared_part)
    out_dec = (
        (final_part[2] / final_part[1][..., None])
        .astype(jnp.bfloat16)
        .reshape(decode_count, QUERY_HEADS * HEAD_SIZE)
    )
    history_lookup = (pre_table[0][:, None] * PAGE_TOKENS + slot_range).reshape(-1)
    cached_count = history_lookup.shape[0]
    prefill_context = jnp.concatenate(
        [flattened_pool[history_lookup], added_rows[:prefill_count]], axis=0
    ).reshape(-1, 2 * KEY_VALUE_HEADS, HEAD_SIZE)
    row_ids = jnp.arange(prefill_count, dtype=jnp.int32)
    pre_visible = jnp.concatenate(
        [
            jnp.broadcast_to(
                jnp.arange(cached_count, dtype=jnp.int32)[None, :] < pre_start[0],
                (prefill_count, cached_count),
            ),
            row_ids[None, :] <= row_ids[:, None],
        ],
        axis=1,
    )
    prefill_query = query_matrix[:prefill_count].reshape(
        prefill_count, KEY_VALUE_HEADS, group_share, HEAD_SIZE
    )
    prefill_scores = jnp.einsum(
        "uwvm,owm->wvuo",
        prefill_query,
        prefill_context[:, :KEY_VALUE_HEADS],
        preferred_element_type=jnp.float32,
    ) * HEAD_SIZE ** (-0.5)
    pre_allowed = pre_visible[None, None]
    pre_masked = jnp.where(pre_allowed, prefill_scores, negative_large)
    pre_max = jnp.max(pre_masked, axis=-1, keepdims=True)
    pre_weights = jnp.where(pre_allowed, jnp.exp(pre_masked - pre_max), 0.0)
    prefill_probabilities = (pre_weights / jnp.sum(pre_weights, axis=-1, keepdims=True)).astype(
        jnp.bfloat16
    )
    out_pre = jnp.einsum(
        "jcse,eji->sjci",
        prefill_probabilities,
        prefill_context[:, KEY_VALUE_HEADS:],
        preferred_element_type=jnp.float32,
    )
    return (out_pre.astype(jnp.bfloat16).reshape(prefill_count, QUERY_HEADS * HEAD_SIZE), out_dec)


def solution(mesh):
    return jax.shard_map(
        on_device,
        mesh=mesh,
        in_specs=(
            P(("fsdp", "dp"), None),
            P(("fsdp", "dp"), None),
            P(("fsdp", "dp"), None),
            P(),
            P(("fsdp", "dp"), None),
            P(("fsdp", "dp"), None),
            P(("fsdp", "dp"), None, None),
            P(("fsdp", "dp"), None),
            P(("fsdp", "dp"), None),
            P(("fsdp", "dp"), None, None),
            P(("fsdp", "dp"), None),
            P("fsdp", None),
            P(("fsdp", "dp")),
            P(("fsdp", "dp"), None),
            P(("fsdp", "dp"), None),
            P(("fsdp", "dp"), None),
        ),
        out_specs=(P(("fsdp", "dp"), None), P(("fsdp", "dp"), None)),
        check_vma=False,
    )
```

profile of v0, /device:TPU:1, one launch (start us, length us, event | category | flops | bytes accessed | tf_op | source)
XLA Modules:
  0.0 1581.3 jit_solution(894209553763811438)
XLA Ops:
  7.3 5.7 copy.216
  13.1 0.7 all-gather.6.cloned.1.call-update
  13.9 1.0 copy.125
  15.9 0.1 fusion.90
  16.0 0.2 select_reduce_fusion.3
  16.5 2.4 gather_fusion
  19.0 0.6 fusion.114
  19.7 0.2 select_reduce_fusion
  20.3 1.6 fusion.28
  21.9 0.6 fusion.8
  22.6 0.3 multiply_cosine_fusion.1
  22.9 0.9 multiply_cosine_fusion
  23.8 0.9 pad_add_fusion
  24.7 0.7 iota_compare_fusion.2
  25.5 1.3 fusion.30
  26.8 2.3 fusion.10
  29.2 695.2 %all-gather.4.cloned.1.call-done = bf16[4096,512]{1,0:T(8,128)(2,1)} async-done(((bf16[16,512]{1,0:T(8,128)(2,1)}), bf16[4096,512]{1,0:T(8,128)(2,1)}) %all-gather.4.cloned.1.call-update) | async-done | bytes 4194320 | tf_op jit(solution)/shard_map/all_gather | solution.py:106
  724.4 5.4 fusion.16
  729.8 0.3 reshape.640
  730.1 0.2 slice.145
  730.4 0.7 subtract_convert_fusion.1
  731.1 0.3 pad_maximum_fusion.2
  731.4 0.7 copy.119
  732.1 0.9 pad_maximum_fusion.1
  733.1 7.9 scatter_custom_fusion
  741.1 7.3 gather_fusion.1
  748.3 0.5 copy.117
  748.9 1.3 copy.118
  750.2 53.4 %gather_fusion.2 = bf16[12288,512]{1,0:T(8,128)(2,1)} fusion(bf16[5376,512]{1,0:T(8,128)(2,1)} %scatter_custom_fusion, s32[12288]{0:T(1024)S(1)} %broadcast_clamp_fusion), kind=kCustom, calls=%fused_computation.2 | custom fusion | bytes 25214976 | tf_op jit(solution)/shard_map/gather | solution.py:135
  803.6 18.2 %reshape.645 = bf16[4,3072,4,128]{3,2,1,0:T(4,128)(2,1)} reshape(bf16[12288,512]{1,0:T(8,128)(2,1)} %gather_fusion.2) | data formatting | bytes 25165824 | tf_op jit(solution)/shard_map/reshape | solution.py:135
  821.9 16.0 %fusion.127 = (bf16[4,3072,2,128]{3,2,1,0:T(2,128)(2,1)}, bf16[4,3072,2,128]{3,2,1,0:T(2,128)(2,1)}) fusion(bf16[4,3072,4,128]{3,2,1,0:T(4,128)(2,1)} %reshape.645), kind=kLoop, calls=%fused_computation.182 | loop fusion | bytes 25165824 | tf_op jit(solution)/shard_map/slice | solution.py:145
  838.0 618.8 %all-gather.6.cloned.1.call-done = bf16[4096,2048]{1,0:T(8,128)(2,1)} async-done(((bf16[16,2048]{1,0:T(8,128)(2,1)}), bf16[4096,2048]{1,0:T(8,128)(2,1)}) %all-gather.6.cloned.1.call-update) | async-done | bytes 16777232 | tf_op jit(solution)/shard_map/all_gather | solution.py:105
  1456.7 8.2 fusion.35
  1465.0 0.2 copy.147
  1465.3 0.6 add_convert_fusion
  1465.9 0.3 fusion.77
  1466.5 6.5 fusion.128
  1472.9 4.7 fusion.34
  1477.6 1.0 copy.133
  1478.8 81.8 %all-gather.8.cloned.1.call-done = bf16[8192,512]{0,1:T(8,128)(2,1)} async-done(((bf16[512,512]{0,1:T(8,128)(2,1)}), bf16[8192,512]{0,1:T(8,128)(2,1)}) %all-gather.8.cloned.1.call-update) | async-done | bytes 8388624 | tf_op jit(solution)/shard_map/all_gather | solution.py:164
  1560.6 3.3 fusion.131
  1563.9 0.7 fusion.126
  1564.7 1.8 fusion.132
  1566.5 0.3 fusion.72
  1566.9 0.5 copy-done.3
  1567.4 4.0 fusion.48
  1571.4 2.7 fusion.69
  1574.1 0.6 copy.212
  (98 shorter events, 2.2 us)
Async XLA Ops:
  7.2 8.7 copy-start.11
  7.2 8.7 copy-start.8
  7.2 6.7 copy-start.5
  7.2 9.2 copy-start.17
  7.2 7.9 copy-start.12
  7.2 8.8 copy-start.15
  7.2 8.8 copy-start.14
  7.2 12.3 copy-start.18
  7.2 7.7 copy-start.13
  7.3 7.7 copy-start.10
  7.3 717.1 %all-gather.4.cloned.1.call-start = ((), (), s32[]{:S(2)}) async-start(), calls=%async_computation | async-start | bytes 4210688 | tf_op jit(solution)/shard_map/all_gather | solution.py:106
  13.1 8.8 copy-start
  13.1 1443.7 %all-gather.6.cloned.1.call-start = ((), (), s32[]{:S(2)}) async-start(), calls=%async_computation.1 | async-start | bytes 16842752 | tf_op jit(solution)/shard_map/all_gather | solution.py:105
  13.8 1546.8 %all-gather.8.cloned.1.call-start = ((), (), s32[]{:S(2)}) async-start(), calls=%async_computation.2 | async-start | bytes 8912896 | tf_op jit(solution)/shard_map/all_gather | solution.py:164
  20.2 5.3 copy-start.2
  22.5 6.6 copy-start.16
  821.9 634.8 %copy-start.1 = (bf16[128,4096]{1,0:T(8,128)(2,1)S(1)}, bf16[128,4096]{1,0:T(8,128)(2,1)}, u32[]{:S(2)}) copy-start(bf16[128,4096]{1,0:T(8,128)(2,1)} %fusion.30) | copy-start | bytes 3145732
  1465.2 1.2 copy-start.4
  1465.2 1.2 copy-start.6
  1465.2 1.2 copy-start.7
  1478.6 86.1 %slice-start = ((s8[6291456]{0:T(1024)(128)(4,1)}), s8[2097152]{0:T(1024)(128)(4,1)S(1)}, s32[]{:S(2)}) async-start(s8[6291456]{0:T(1024)(128)(4,1)} %bitcast.130), calls=%async_computation.3 | async-start | bytes 4194304
  1560.6 4.0 slice-start.1
  1560.6 4.0 copy-start.9
  1563.9 3.4 copy-start.3
  1564.7 6.7 slice-start.2
  1566.9 4.6 slice-start.3
Sparse Core Ops, SparseCore 0:
  13.2 711.1 all-gather.3
  726.2 730.4 all-gather.5
  1458.5 102.0 all-gather.7
where the time goes:
time: 1580 us
  waiting for transfers between devices  1400 us (89%)
  local copies, waits for them, and re-layouts  118 us (7%)
  matrix products  36.7 us (2%)
    all_gather x1, waiting for transfers between devices, on_device(): lax.all_gather(key_value_weight, ('fsdp', 'dp'), axis=0, tiled=True)  695 us
    all_gather x1, waiting for transfers between devices, on_device(): lax.all_gather(w_query, ('fsdp', 'dp'), axis=0, tiled=True)  619 us
    all_gather x1, waiting for transfers between devices, on_device(): slice_portion = lax.all_gather(shared_kv, 'dp', axis=0, tiled=True)  81.8 us
    gather x1, local copies, waits for them, and re-layouts, on_device(): flattened_pool[private_lookup]  53.4 us
  transfers between devices with their start and end apart: 3, of which 3 were waited for; matrix products, arithmetic and copies ran while one was open for 9% of the time, Pallas kernels for 0%

commit v1 on v0

v1 whole, which is shorter than its diff:
```python
import functools

import jax
import jax.numpy as jnp
from jax import lax
from jax.experimental import pallas as pl
from jax.experimental.pallas import tpu as pltpu
from jax.sharding import Mesh
from jax.sharding import PartitionSpec as P

QUERY_HEADS = 16
KEY_VALUE_HEADS = 2
GROUP = QUERY_HEADS // KEY_VALUE_HEADS
HEAD_SIZE = 128
PAGE_TOKENS = 64
PRE = 128
DEC = 4
REC = 320
LINE = 64
ROWS = PRE + LINE + REC
QROWS = PRE + LINE
DEC_SLOTS = 68
HIST_SLOTS = 16
HALF = GROUP * HEAD_SIZE
WIDE = HALF + 2 * HEAD_SIZE
MODEL = 4096
SPAN = 512
STAT = QUERY_HEADS * HEAD_SIZE

AXES = ("zh", "x", "c", "zl", "y")
DP = ("zl", "y")

theta_base = 5000000.0
epsilon = 1e-05
negative_large = -1e30
scale = HEAD_SIZE**-0.5

f32 = jnp.float32
bf16 = jnp.bfloat16
ANY = pl.BlockSpec(memory_space=pl.ANY)
VMEM = pl.BlockSpec(memory_space=pltpu.VMEM)
SMEM = pl.BlockSpec(memory_space=pltpu.SMEM)


def dot_t(a, b):
    return lax.dot_general(a, b, (((1,), (1,)), ((), ())), preferred_element_type=f32)


def dot(a, b):
    return lax.dot_general(a, b, (((1,), (0,)), ((), ())), preferred_element_type=f32)


def project_kernel(w_hbm, own_hbm, other_hbm, tab_own, tab_oth, q_own, kv_own, packed, w, x, w_sem, x_sem):
    copies = [
        pltpu.make_async_copy(own_hbm.at[0:QROWS], x.at[0:QROWS], x_sem.at[0]),
        pltpu.make_async_copy(other_hbm.at[0:QROWS], x.at[QROWS : 2 * QROWS], x_sem.at[1]),
        pltpu.make_async_copy(own_hbm.at[QROWS:ROWS], x.at[2 * QROWS : 2 * QROWS + REC], x_sem.at[2]),
        pltpu.make_async_copy(other_hbm.at[QROWS:ROWS], x.at[2 * QROWS + REC : 2 * ROWS], x_sem.at[3]),
    ]
    groups = [slice(g * 256, (g + 1) * 256) for g in range(WIDE // 256)]
    pieces = []
    for g, cols in enumerate(groups):
        for xi in range(4):
            for yi in range(4):
                pieces.append(
                    pltpu.make_async_copy(
                        w_hbm.at[xi * 4 + yi, :, :, :, :, cols],
                        w.at[:, xi, :, :, yi, :, cols],
                        w_sem.at[g, xi * 4 + yi],
                    )
                )
    for copy in copies[:2]:
        copy.start()
    for copy in pieces[:16]:
        copy.start()
    for copy in copies[2:]:
        copy.start()
    for copy in pieces[16:]:
        copy.start()
    for copy in copies[:2]:
        copy.wait()

    def turned(values, tab):
        return values * tab[:, :HEAD_SIZE] + pltpu.roll(values, HEAD_SIZE // 2, 1) * tab[:, HEAD_SIZE:]

    q_tab_own = tab_own[0:QROWS, :]
    q_tab_oth = tab_oth[0:QROWS, :]
    for g, cols in enumerate(groups):
        for copy in pieces[g * 16 : (g + 1) * 16]:
            copy.wait()
        wg = w[:, :, :, :, :, :, cols].reshape(MODEL, 256)
        if g < HALF // 256:
            acc = dot(x[0 : 2 * QROWS, :], wg)
            for h in range(2):
                at = slice(g * 256 + h * HEAD_SIZE, g * 256 + (h + 1) * HEAD_SIZE)
                part = acc[:, h * HEAD_SIZE : (h + 1) * HEAD_SIZE]
                q_own[:, at] = turned(part[:QROWS], q_tab_own).astype(bf16)
                packed[0:QROWS, at] = turned(part[QROWS:], q_tab_oth).astype(bf16)
        else:
            for copy in copies[2:]:
                copy.wait()
            acc = dot(x[...], wg)
            for own in (True, False):
                tab = (tab_own if own else tab_oth)[...]
                first = acc[0:QROWS] if own else acc[QROWS : 2 * QROWS]
                rest = acc[2 * QROWS : 2 * QROWS + REC] if own else acc[2 * QROWS + REC :]
                both = jnp.concatenate([first, rest], axis=0)
                keys = turned(both[:, :HEAD_SIZE], tab).astype(bf16)
                values = both[:, HEAD_SIZE:].astype(bf16)
                if own:
                    kv_own[:, :HEAD_SIZE] = keys
                    kv_own[:, HEAD_SIZE:] = values
                else:
                    for b in range(4):
                        rows = slice(b * 128, (b + 1) * 128)
                        packed[QROWS:, b * 256 : b * 256 + 128] = keys[rows]
                        packed[QROWS:, b * 256 + 128 : (b + 1) * 256] = values[rows]


def project(weights, own, other, tab_own, tab_oth):
    return pl.pallas_call(
        project_kernel,
        name="project",
        out_shape=(
            jax.ShapeDtypeStruct((QROWS, HALF), bf16),
            jax.ShapeDtypeStruct((ROWS, 2 * HEAD_SIZE), bf16),
            jax.ShapeDtypeStruct((QROWS + 128, HALF), bf16),
        ),
        in_specs=[ANY, ANY, ANY, VMEM, VMEM],
        out_specs=(VMEM, VMEM, VMEM),
        scratch_shapes=[
            pltpu.VMEM((2, 4, 2, 4, 4, 16, WIDE), bf16),
            pltpu.VMEM((2 * ROWS, MODEL), bf16),
            pltpu.SemaphoreType.DMA((WIDE // 256, 16)),
            pltpu.SemaphoreType.DMA((4,)),
        ],
        compiler_params=pltpu.CompilerParams(vmem_limit_bytes=40 << 20),
        cost_estimate=pl.CostEstimate(flops=6 * 10**9, bytes_accessed=20 * 10**6, transcendentals=0),
    )(weights, own, other, tab_own, tab_oth)


def shared_kernel(info, q_own, packed, kv, out, qs):
    core = info[0]
    qs[core] = q_own[PRE:QROWS, :]
    qs[1 - core] = packed[PRE:QROWS, :]
    limit = info[1]
    bias = jnp.where(lax.broadcasted_iota(jnp.int32, (1, SPAN), 1) < limit, 0.0, negative_large)
    lane = lax.broadcasted_iota(jnp.int32, (LINE, HEAD_SIZE), 1)
    stats = jnp.zeros((LINE, HEAD_SIZE), f32)
    for s in range(KEY_VALUE_HEADS):
        keys = kv[:, s * HEAD_SIZE : (s + 1) * HEAD_SIZE]
        values = kv[:, (2 + s) * HEAD_SIZE : (3 + s) * HEAD_SIZE]
        for h in range(GROUP):
            scores = dot_t(qs[s, :, h * HEAD_SIZE : (h + 1) * HEAD_SIZE], keys) + bias
            top = jnp.max(scores, axis=-1, keepdims=True)
            weights = jnp.exp((scores - top) * scale)
            total = jnp.sum(weights, axis=-1, keepdims=True)
            head = s * GROUP + h
            out[:, head * HEAD_SIZE : (head + 1) * HEAD_SIZE] = dot(weights.astype(bf16), values) / total
            stats = jnp.where(lane == head, top * scale + jnp.log(total), stats)
    out[:, STAT:] = stats


def shared_attention(info, q_own, packed, kv):
    return pl.pallas_call(
        shared_kernel,
        name="shared",
        out_shape=jax.ShapeDtypeStruct((LINE, STAT + 128), f32),
        in_specs=[SMEM, VMEM, VMEM, VMEM],
        out_specs=VMEM,
        scratch_shapes=[pltpu.VMEM((2, LINE, HALF), bf16)],
        compiler_params=pltpu.CompilerParams(vmem_limit_bytes=16 << 20),
        cost_estimate=pl.CostEstimate(flops=3 * 10**8, bytes_accessed=10**6, transcendentals=10**6),
    )(info, q_own, packed, kv)


def local_kernel(info, slots, q_own, kv_own, packed, bias_private, bias_new, pool, out_pre, out_dec, stat_dec, pages, qs, ks, sems):
    copies = []
    for i in list(range(DEC_SLOTS, DEC_SLOTS + HIST_SLOTS)) + list(range(DEC_SLOTS)):
        copies.append(pltpu.make_async_copy(pool.at[slots[i]], pages.at[i], sems.at[i]))
    for copy in copies:
        copy.start()
    core = info[0]
    start = info[2]
    place = info[3]
    qs[core] = q_own[...]
    qs[1 - core] = packed[0:QROWS, :]
    ks[core] = kv_own[...]
    for b in range(4):
        ks[1 - core, b * 128 : (b + 1) * 128, :] = packed[QROWS:, b * 256 : (b + 1) * 256]
    for copy in copies[:HIST_SLOTS]:
        copy.wait()
    history = HIST_SLOTS * PAGE_TOKENS
    seen = jnp.where(lax.broadcasted_iota(jnp.int32, (1, history), 1) < start, 0.0, negative_large)
    rows = lax.broadcasted_iota(jnp.int32, (PRE, PRE), 0)
    cols = lax.broadcasted_iota(jnp.int32, (PRE, PRE), 1)
    causal = jnp.where(cols <= rows, 0.0, negative_large)
    for s in range(KEY_VALUE_HEADS):
        old_keys = pages[DEC_SLOTS:, :, s * HEAD_SIZE : (s + 1) * HEAD_SIZE].reshape(history, HEAD_SIZE)
        old_values = pages[DEC_SLOTS:, :, (2 + s) * HEAD_SIZE : (3 + s) * HEAD_SIZE].reshape(history, HEAD_SIZE)
        new_keys = ks[s, 0:PRE, 0:HEAD_SIZE]
        new_values = ks[s, 0:PRE, HEAD_SIZE:]
        for h in range(GROUP):
            query = qs[s, 0:PRE, h * HEAD_SIZE : (h + 1) * HEAD_SIZE]
            first = dot_t(query, old_keys) + seen
            second = dot_t(query, new_keys) + causal
            top = jnp.maximum(jnp.max(first, axis=-1, keepdims=True), jnp.max(second, axis=-1, keepdims=True))
            first = jnp.exp((first - top) * scale)
            second = jnp.exp((second - top) * scale)
            total = jnp.sum(first, axis=-1, keepdims=True) + jnp.sum(second, axis=-1, keepdims=True)
            result = dot(first.astype(bf16), old_values) + dot(second.astype(bf16), new_values)
            head = s * GROUP + h
            out_pre[:, head * HEAD_SIZE : (head + 1) * HEAD_SIZE] = (result / total).astype(bf16)

    for copy in copies[HIST_SLOTS:]:
        copy.wait()
    private = DEC_SLOTS * PAGE_TOKENS
    pick = (
        lax.broadcasted_iota(jnp.int32, (8, LINE), 1)
        == lax.broadcasted_iota(jnp.int32, (8, LINE), 0) + place * DEC
    ) & (lax.broadcasted_iota(jnp.int32, (8, LINE), 0) < DEC)
    pick = jnp.where(pick, 1.0, 0.0).astype(bf16)
    lane = lax.broadcasted_iota(jnp.int32, (8, HEAD_SIZE), 1)
    stats = jnp.zeros((8, HEAD_SIZE), f32)
    for s in range(KEY_VALUE_HEADS):
        old_keys = pages[:DEC_SLOTS, :, s * HEAD_SIZE : (s + 1) * HEAD_SIZE].reshape(private, HEAD_SIZE)
        old_values = pages[:DEC_SLOTS, :, (2 + s) * HEAD_SIZE : (3 + s) * HEAD_SIZE].reshape(private, HEAD_SIZE)
        new_keys = ks[s, :, 0:HEAD_SIZE]
        new_values = ks[s, :, HEAD_SIZE:]
        line = dot(pick, qs[s, PRE:QROWS, :])
        query = jnp.concatenate([line[:, h * HEAD_SIZE : (h + 1) * HEAD_SIZE] for h in range(GROUP)], axis=0)
        query = query.astype(bf16)
        first = dot_t(query, old_keys).reshape(GROUP, 8, private) + bias_private[...][None]
        second = dot_t(query, new_keys).reshape(GROUP, 8, ROWS) + bias_new[...][None]
        first = first.reshape(GROUP * 8, private)
        second = second.reshape(GROUP * 8, ROWS)
        top = jnp.maximum(jnp.max(first, axis=-1, keepdims=True), jnp.max(second, axis=-1, keepdims=True))
        first = jnp.exp((first - top) * scale)
        second = jnp.exp((second - top) * scale)
        total = jnp.sum(first, axis=-1, keepdims=True) + jnp.sum(second, axis=-1, keepdims=True)
        result = dot(first.astype(bf16), old_values) + dot(second.astype(bf16), new_values)
        result = result / total
        level = top * scale + jnp.log(total)
        for h in range(GROUP):
            head = s * GROUP + h
            out_dec[:, head * HEAD_SIZE : (head + 1) * HEAD_SIZE] = result[h * 8 : (h + 1) * 8]
            stats = jnp.where(lane == head, level[h * 8 : (h + 1) * 8], stats)
    stat_dec[...] = stats


def local_attention(info, slots, q_own, kv_own, packed, bias_private, bias_new, pool):
    return pl.pallas_call(
        local_kernel,
        name="local",
        out_shape=(
            jax.ShapeDtypeStruct((PRE, QUERY_HEADS * HEAD_SIZE), bf16),
            jax.ShapeDtypeStruct((8, QUERY_HEADS * HEAD_SIZE), f32),
            jax.ShapeDtypeStruct((8, HEAD_SIZE), f32),
        ),
        in_specs=[SMEM, SMEM, VMEM, VMEM, VMEM, VMEM, VMEM, ANY],
        out_specs=(VMEM, VMEM, VMEM),
        scratch_shapes=[
            pltpu.VMEM((DEC_SLOTS + HIST_SLOTS, PAGE_TOKENS, 4 * HEAD_SIZE), bf16),
            pltpu.VMEM((2, QROWS, HALF), bf16),
            pltpu.VMEM((2, ROWS, 2 * HEAD_SIZE), bf16),
            pltpu.SemaphoreType.DMA((DEC_SLOTS + HIST_SLOTS,)),
        ],
        compiler_params=pltpu.CompilerParams(vmem_limit_bytes=32 << 20),
        cost_estimate=pl.CostEstimate(flops=10**10, bytes_accessed=8 * 10**6, transcendentals=3 * 10**6),
    )(info, slots, q_own, kv_own, packed, bias_private, bias_new, pool)


def finish_kernel(groups, shared, local, local_stat, out):
    for r in range(DEC):
        row = groups[r] * DEC + r
        eight = shared[pl.ds(pl.multiple_of(row // 8 * 8, 8), 8), :]
        hit = lax.broadcasted_iota(jnp.int32, eight.shape, 0) == row % 8
        chosen = jnp.sum(jnp.where(hit, eight, 0.0), axis=0, keepdims=True)
        far_stat = chosen[:, STAT:]
        near_stat = local_stat[r : r + 1, :]
        top = jnp.maximum(far_stat, near_stat)
        far = jnp.exp(far_stat - top)
        near = jnp.exp(near_stat - top)
        whole = far + near
        far = far / whole
        near = near / whole
        for head in range(QUERY_HEADS):
            at = slice(head * HEAD_SIZE, (head + 1) * HEAD_SIZE)
            mixed = chosen[:, at] * far[:, head : head + 1] + local[r : r + 1, at] * near[:, head : head + 1]
            out[r : r + 1, at] = mixed.astype(bf16)


def finish(groups, shared, local, local_stat):
    return pl.pallas_call(
        finish_kernel,
        name="finish",
        out_shape=jax.ShapeDtypeStruct((DEC, QUERY_HEADS * HEAD_SIZE), bf16),
        in_specs=[SMEM, VMEM, VMEM, VMEM],
        out_specs=VMEM,
        compiler_params=pltpu.CompilerParams(vmem_limit_bytes=8 << 20),
    )(groups, shared, local, local_stat)


def small_lookup(entries, indices):
    matches = indices[..., None] == jnp.arange(entries.shape[0], dtype=jnp.int32)
    return jnp.sum(jnp.where(matches, entries, 0), axis=-1)


def rms_scaled(values, gain):
    widened = values.astype(f32)
    factor = lax.rsqrt(jnp.mean(widened * widened, axis=-1, keepdims=True) + epsilon)
    return (widened * factor * gain.astype(f32)).astype(bf16)


def gather_weights(w_query, key_value_weight):
    key_half = key_value_weight.reshape(16, 2, 2, HEAD_SIZE)
    halves = [
        jnp.concatenate([w_query[:, c * HALF : (c + 1) * HALF], key_half[:, 0, c], key_half[:, 1, c]], axis=1)
        for c in range(2)
    ]
    block = jnp.stack(halves, axis=0)
    sent = jnp.broadcast_to(block[None, :, None], (2, 2, 4, 16, WIDE)).reshape(16, 16, WIDE)
    column = lax.all_to_all(sent, ("zh", "c", "zl"), 0, 0, tiled=True)
    whole = lax.all_gather(column.reshape(256, WIDE), ("x", "y"), axis=0, tiled=True)
    return whole.reshape(16, 2, 2, 4, 16, WIDE)


def on_device(
    x_pre, x_dec, rec_hidden, norm_gain, w_query, key_value_weight, cache_pool, shared_kv,
    dec_len, dec_table, dec_group, prefix_len, pre_start, pre_table, rec_req, rec_off,
):
    core = lax.axis_index("c")
    place = lax.axis_index("zl") * 4 + lax.axis_index("y")
    lengths = dec_len[0]
    page_table = dec_table[0]
    groups = dec_group[0]
    prefix_line = prefix_len[0]
    request = rec_req[0]
    within = rec_off[0]

    weights = gather_weights(w_query, key_value_weight)

    dec_pos = small_lookup(prefix_line, groups) + lengths
    parts = jnp.stack([dec_pos // 64, dec_pos % 64], axis=1).astype(bf16)
    extra = jnp.concatenate([x_dec, parts, jnp.zeros((DEC, 126), bf16)], axis=1)
    line = lax.all_to_all(
        jnp.broadcast_to(extra[None], (16, DEC, MODEL + 128)), DP, 0, 0, tiled=True
    ).reshape(LINE, MODEL + 128)
    line_parts = line[:, MODEL : MODEL + 2].astype(jnp.int32)
    line_pos = line_parts[:, 0] * 64 + line_parts[:, 1]

    rows = jnp.concatenate([x_pre, line[:, :MODEL], rec_hidden], axis=0)
    normed = rms_scaled(rows, norm_gain)
    pre_pos = pre_start[0] + jnp.arange(PRE, dtype=jnp.int32)
    rec_pos = small_lookup(prefix_line, small_lookup(groups, request)) + within
    positions = jnp.concatenate([pre_pos, line_pos, rec_pos], axis=0)
    half_dim = HEAD_SIZE // 2
    frequency = theta_base ** (-jnp.arange(half_dim, dtype=f32) * 2.0 / HEAD_SIZE)
    angles = positions.astype(f32)[:, None] * frequency
    cosines = jnp.cos(angles)
    sines = jnp.sin(angles)
    table = jnp.concatenate([cosines, cosines, -sines, sines], axis=1)
    swap = [(0, 1), (1, 0)]
    other = lax.ppermute(normed, "c", swap)
    other_table = lax.ppermute(table, "c", swap)

    counts = (lengths + PAGE_TOKENS - 1) // PAGE_TOKENS
    ends = jnp.cumsum(counts)
    firsts = ends - counts
    slot = jnp.arange(DEC_SLOTS, dtype=jnp.int32)
    slot_request = jnp.sum((slot[:, None] >= ends[None, :]).astype(jnp.int32), axis=1)
    used = slot_request < DEC
    slot_request = jnp.minimum(slot_request, DEC - 1)
    slot_page = jnp.where(used, slot - small_lookup(firsts, slot_request), 0)
    dec_pages = small_lookup(page_table.reshape(-1), slot_request * page_table.shape[1] + slot_page)
    slots = jnp.concatenate([dec_pages, pre_table[0]], axis=0)
    key_pos = slot_page[:, None] * PAGE_TOKENS + jnp.arange(PAGE_TOKENS, dtype=jnp.int32)[None, :]
    valid = used[:, None] & (key_pos < small_lookup(lengths, slot_request)[:, None])
    rec_slot = small_lookup(firsts, request) + within // PAGE_TOKENS
    slot_hot = (rec_slot[None, :] == slot[:, None]).astype(bf16)
    token_hot = (within[:, None] % PAGE_TOKENS == jnp.arange(PAGE_TOKENS, dtype=jnp.int32)[None, :]).astype(bf16)
    replaced = jnp.dot(slot_hot, token_hot, preferred_element_type=f32) > 0.5
    kept = (valid & ~replaced).reshape(-1)
    eight = jnp.arange(8, dtype=jnp.int32)
    key_request = jnp.repeat(slot_request, PAGE_TOKENS)
    junk = eight[:, None] >= DEC
    bias_private = jnp.where(junk | (kept[None, :] & (key_request[None, :] == eight[:, None])), 0.0, negative_large)
    new_request = jnp.concatenate(
        [jnp.full((PRE,), -1, jnp.int32), jnp.arange(LINE, dtype=jnp.int32) - place * DEC, request], axis=0
    )
    bias_new = jnp.where(junk | (new_request[None, :] == eight[:, None]), 0.0, negative_large)
    own_prefix = small_lookup(prefix_line, place[None])[0]
    info = jnp.stack([core, own_prefix, pre_start[0], place]).astype(jnp.int32)

    q_own, kv_own, packed = project(weights, normed, other, table, other_table)
    packed = lax.ppermute(packed, "c", swap)
    shared_part = shared_attention(info, q_own, packed, shared_kv)
    shared_part = lax.all_to_all(shared_part, DP, 0, 0, tiled=True)
    out_pre, dec_part, dec_stat = local_attention(
        info, slots, q_own, kv_own, packed, bias_private, bias_new, cache_pool
    )
    out_dec = finish(groups, shared_part, dec_part, dec_stat)
    return (out_pre, out_dec)


def solution(mesh):
    split = Mesh(mesh.devices.reshape(2, 4, 2, 4, 4), AXES)
    first = P(AXES, None)
    second = P(AXES, None, None)
    return jax.shard_map(
        on_device,
        mesh=split,
        in_specs=(
            first, first, first, P(), first, first, second, first,
            first, second, first, P(("zh", "x", "c"), None), P(AXES), first, first, first,
        ),
        out_specs=(first, first),
        check_vma=False,
    )
```

time: 1580 us -> 182 us (0.12)
  waiting for transfers between devices: 1400 us -> 61 us
  local copies, waits for them, and re-layouts: 118 us -> 9.15 us
  Pallas kernels: 0 us -> 37.4 us
  matrix products: 36.7 us -> 0.31 us
  blocking collectives: 0 us -> 29 us
  starting transfers between devices: 0.12 us -> 16.2 us
    all_gather x3 -> x1, waiting for transfers between devices: 1400 us -> 44.3 us  [gather_weights(): lax.all_gather(column.reshape(256, WIDE), ('x', 'y'), axis=0, tiled=True)]
    gather x4 -> x0, local copies, waits for them, and re-layouts: 63.7 us -> none  [the longest x1 53.4 us: on_device(): flattened_pool[private_lookup]]
    pallas_call x0 -> x4, Pallas kernels: none -> 37.4 us  [the longest x1 17.7 us: local_attention(): pl.pallas_call(local_kernel, name='local', out_shape=(jax.ShapeDtypeStruc...]
    dot_general x8 -> x1, matrix products: 30.3 us -> 0.31 us  [on_device(): replaced = jnp.dot(slot_hot, token_hot, preferred_element_type=f32) > 0.5]
    all_to_all x0 -> x1, blocking collectives: none -> 29 us  [gather_weights(): column = lax.all_to_all(sent, ('zh', 'c', 'zl'), 0, 0, tiled=True)]
    reshape x3 -> x2, local copies, waits for them, and re-layouts: 18.6 us -> 2.05 us  [the longest x1 1.17 us: on_device(): line = lax.all_to_all(jnp.broadcast_to(extra[None], (16, DEC, MODEL + 128...]
    slice x5 -> x3, local copies, waits for them, and re-layouts: 17.2 us -> 0.84 us  [the longest x1 0.78 us: gather_weights(): w_query[:, c * HALF:(c + 1) * HALF]]
  transfers between devices with their start and end apart: 3 -> 6, of which waited for: 3 -> 4; matrix products, arithmetic and copies ran while one was open for 9% -> 9% of each run, Pallas kernels for 0% -> 10%
where the time goes in v1:
time: 182 us; the launch traced here: 181 us
  waiting for transfers between devices  61 us (34%)
  Pallas kernels  37.4 us (21%)
  blocking collectives  29 us (16%)
  starting transfers between devices  16.2 us (9%)
  between operations  15 us (8%)
  other arithmetic  13.2 us (7%)
  local copies, waits for them, and re-layouts  9.15 us (5%)
    all_gather x1, waiting for transfers between devices, gather_weights(): lax.all_gather(column.reshape(256, WIDE), ('x', 'y'), axis=0, tiled=True)  44.3 us
    all_to_all x1, blocking collectives, gather_weights(): column = lax.all_to_all(sent, ('zh', 'c', 'zl'), 0, 0, tiled=True)  29 us
    pallas_call x1, Pallas kernels, local_attention(): pl.pallas_call(local_kernel, name='local', out_shape=(jax.ShapeDtypeStruc...  17.7 us
    pallas_call x1, Pallas kernels, project(): pl.pallas_call(project_kernel, name='project', out_shape=(jax.ShapeDtypeS...  13.5 us
    all_to_all x1, waiting for transfers between devices, on_device(): lax.all_to_all(jnp.broadcast_to(extra[None], (16, DEC, MODEL + 128)), DP,...  12.1 us
    all_to_all x1, starting transfers between devices, on_device(): shared_part = lax.all_to_all(shared_part, DP, 0, 0, tiled=True)  7.04 us
    all_to_all x1, starting transfers between devices, on_device(): lax.all_to_all(jnp.broadcast_to(extra[None], (16, DEC, MODEL + 128)), DP,...  5.77 us
    pallas_call x1, Pallas kernels, shared_attention(): pl.pallas_call(shared_kernel, name='shared', out_shape=jax.ShapeDtypeStru...  4.75 us
  transfers between devices with their start and end apart: 6, of which 4 were waited for; matrix products, arithmetic and copies ran while one was open for 9% of the time, Pallas kernels for 10%

profile of v1, /device:TPU:1, one launch (start us, length us, event | category | flops | bytes accessed | tf_op | source)
XLA Modules:
  0.0 181.2 jit_solution(12383757929954631530)
XLA Ops:
  7.2 0.9 reshape.297
  8.1 0.8 fusion.20
  9.0 29.0 %all_to_all.21 = bf16[16,16,1280]{2,1,0:T(8,128)(2,1)} all-to-all(bf16[16,16,1280]{2,1,0:T(8,128)(2,1)S(1)} %bitcast.48), channel_id=1, replica_groups=mesh['zh'=2,'x'=4,'c'=2,'zl'=4,'y'=4] {'zh','c','zl'}, dimensions={0} | all-to-all | bytes 1310720 | tf_op jit(solution)/shard_map/all_to_all | solution.py:323
  38.1 0.9 select_reduce_fusion.5
  39.0 0.7 fusion.17
  39.6 0.7 fusion.19
  40.3 0.1 copy.42
  40.4 0.1 copy.43
  40.5 0.9 concatenate.34
  41.4 0.9 broadcast_in_dim.134
  42.3 5.8 %all-to-all-start.1 = ((bf16[16,4,4224]{2,1,0:T(4,128)(2,1)}), bf16[16,4,4224]{2,1,0:T(4,128)(2,1)}, u32[]{:S(2)}, u32[]{:S(2)}) async-start(bf16[16,4,4224]{2,1,0:T(4,128)(2,1)} %broadcast_in_dim.134), calls=%async_computation.1 | async-start | bytes 1081344 | tf_op jit(solution)/shard_map/all_to_all | solution.py:346
  48.1 0.2 reduce-window.8
  48.3 0.7 reduce.2
  49.6 0.7 convert_element_type.27
  50.3 0.1 convert_reduce_fusion
  50.4 12.1 %all-to-all-done.1 = bf16[16,4,4224]{2,1,0:T(4,128)(2,1)} async-done(((bf16[16,4,4224]{2,1,0:T(4,128)(2,1)}), bf16[16,4,4224]{2,1,0:T(4,128)(2,1)}, u32[]{:S(2)}, u32[]{:S(2)}) %all-to-all-start.1) | async-done | bytes 540704 | tf_op jit(solution)/shard_map/all_to_all | solution.py:346
  62.5 1.2 reshape.301
  63.8 2.0 %fusion = f32[512]{0:T(512)S(1)} fusion(bf16[320,4096]{1,0:T(8,128)(2,1)S(1)} %copy-done.3, bf16[64,4096]{1,0:T(8,128)(2,1)S(1)} %slice.44, bf16[128,4096]{1,0:T(8,128)(2,1)} %param.16), kind=kLoop, calls=%fused_computation.2 | loop fusion | flops 16776704 | bytes 4196352 | tf_op jit(solution)/shard_map/reduce_sum | solution.py:311
  65.8 3.7 %fusion.2.own_hbm = bf16[512,4096]{1,0:T(8,128)(2,1)} fusion(f32[4096]{0:T(1024)S(1)} %convert_element_type.27, f32[512]{0:T(512)S(1)} %add_rsqrt_fusion, bf16[320,4096]{1,0:T(8,128)(2,1)S(1)} %copy-done.3, bf16[64,4096]{1,0:T(8,128)(2,1)S(1)} %slice.44, bf16[128,4096]{1,0:T(8,128)(2,1)} %param.16), kind=kLoop, calls=%fused_computation.4 | loop fusion | flops 18874368 | bytes 8407040 | tf_op jit(solution)/shard_map/convert_element_type | solution.py:312
  69.5 2.3 %collective-permute-start = (bf16[512,4096]{1,0:T(8,128)(2,1)}, bf16[512,4096]{1,0:T(8,128)(2,1)}, u32[]{:S(2)}, u32[]{:S(2)}) collective-permute-start(bf16[512,4096]{1,0:T(8,128)(2,1)} %fusion.2.own_hbm), channel_id=1, source_target_pairs={{0,16},{16,0},{1,17},{17,1},{2,18},{18,2},{3,19},{19,3},{4,20},{20... | collective-permute-start | bytes 12582920 | tf_op jit(solution)/shard_map/ppermute | solution.py:364
  71.8 0.1 select_reduce_fusion.2
  71.9 0.1 select_reduce_fusion.1
  72.0 0.1 select_reduce_fusion.4
  72.1 0.3 fusion.4
  72.5 0.1 copy.45
  72.6 0.1 and.108
  72.9 0.2 fusion.11
  73.1 1.0 multiply_cosine_fusion
  74.1 0.3 pad_maximum_fusion.1.tab_own
  74.4 0.3 collective-permute-start.1
  74.7 0.1 fusion.7.bias_private
  74.8 0.1 reshape_squeeze.3
  74.9 0.6 fusion.16
  75.5 3.8 %collective-permute-done.1.tab_oth = f32[512,256]{1,0:T(8,128)S(1)} collective-permute-done((f32[512,256]{1,0:T(8,128)S(1)}, f32[512,256]{1,0:T(8,128)S(1)}, u32[]{:S(2)}, u32[]{:S(2)}) %collective-permute-start.1) | collective-permute-done | bytes 524320 | tf_op jit(solution)/shard_map/ppermute | solution.py:365
  79.3 44.3 %all-gather.2.cloned.1.call-done = bf16[4096,1280]{1,0:T(8,128)(2,1)} async-done(((bf16[256,1280]{1,0:T(8,128)(2,1)}), bf16[4096,1280]{1,0:T(8,128)(2,1)}) %all-gather.2.cloned.1.call-update) | async-done | bytes 10485776 | tf_op jit(solution)/shard_map/all_gather | solution.py:324
  123.6 13.5 %project.1 = (bf16[192,1024]{1,0:T(8,128)(2,1)S(1)}, bf16[512,256]{1,0:T(8,128)(2,1)S(1)}, bf16[320,1024]{1,0:T(8,128)(2,1)S(1)}) custom-call(bf16[16,2,2,4,16,1280]{5,4,3,2,1,0:T(8,128)(2,1)} %bitcast.52, bf16[512,4096]{1,0:T(8,128)(2,1)} %fusion.2.own_hbm, bf16[512,4096]{1,0:T(8,128)(2,1)} %collective-permute-done.other_hbm, ...), custom_call_target="tpu_custom_call" | custom-call | flops 6000000000 | bytes 20000000 | tf_op jit(solution)/shard_map/project/pallas_call | solution.py:121
  137.1 0.8 collective-permute-start.2
  137.9 0.6 pad_add_fusion.1.info
  138.5 0.1 pad_add_fusion
  138.6 0.2 select_reduce_fusion
  138.9 0.8 collective-permute-done.2.packed
  139.6 4.7 %shared.1 = f32[64,2176]{1,0:T(8,128)S(1)} custom-call(s32[4]{0:T(128)S(1)} %pad_add_fusion.1.info, bf16[192,1024]{1,0:T(8,128)(2,1)S(1)} %get-tuple-element.8.q_own, bf16[320,1024]{1,0:T(8,128)(2,1)S(1)} %collective-permute-done.2.packed, bf16[512,512]{1,0:T(8,128)(2,1)S(1)} %copy-done), custom_call_target="tpu_custom_call" | custom-call | flops 300000000 | bytes 1000000 | tf_op jit(solution)/shard_map/shared/pallas_call | solution.py:165
  144.4 0.9 all_to_all.15
  145.3 7.0 %all-to-all-start.2 = ((f32[16,4,2176]{2,1,0:T(4,128)}), f32[16,4,2176]{2,1,0:T(4,128)S(1)}, u32[]{:S(2)}, u32[]{:S(2)}) async-start(f32[16,4,2176]{2,1,0:T(4,128)} %all_to_all.15), calls=%async_computation.2 | async-start | bytes 1114112 | tf_op jit(solution)/shard_map/all_to_all | solution.py:398
  152.5 2.6 %copy-done.2 = bf16[84,64,512]{2,1,0:T(8,128)(2,1)S(1)} copy-done((bf16[84,64,512]{2,1,0:T(8,128)(2,1)S(1)}, bf16[84,64,512]{2,1,0:T(8,128)(2,1)}, u32[]{:S(2)}) %copy-start.2) | copy-done | bytes 5505048
  155.0 17.7 %local.1 = (bf16[128,2048]{1,0:T(8,128)(2,1)}, f32[8,2048]{1,0:T(8,128)S(1)}, f32[8,128]{1,0:T(8,128)S(1)}) custom-call(s32[4]{0:T(128)S(1)} %pad_add_fusion.1.info, s32[84]{0:T(128)S(1)} %pad_add_fusion.2.slots, bf16[192,1024]{1,0:T(8,128)(2,1)S(1)} %get-tuple-element.8.q_own, bf16[512,256]{1,0:T(8,128)(2,1)S(1)} %get-tuple-element.9.kv_own, ...), custom_call_target="tpu_custom_call" | custom-call | flops 10000000000 | bytes 8000000 | tf_op jit(solution)/shard_map/local/pallas_call | solution.py:252
  172.7 0.2 all_to_all.17.shared
  172.9 1.5 finish.1
  (48 shorter events, 0.7 us)
Async XLA Ops:
  7.2 56.6 %copy-start.3 = (bf16[320,4096]{1,0:T(8,128)(2,1)S(1)}, bf16[320,4096]{1,0:T(8,128)(2,1)}, u32[]{:S(2)}) copy-start(bf16[320,4096]{1,0:T(8,128)(2,1)} %param.18) | copy-start | bytes 7864324
  7.2 116.4 %all-gather.2.cloned.1.call-start = ((), (), s32[]{:S(2)}) async-start(), calls=%async_computation.3 | async-start | bytes 11141120 | tf_op jit(solution)/shard_map/all_gather | solution.py:324
  38.0 33.7 %copy-start.4 = (s32[1,4]{1,0:T(1,128)S(1)}, s32[1,4]{1,0:T(1,128)}, u32[]{:S(2)}) copy-start(s32[1,4]{1,0:T(1,128)} %param.24) | copy-start | bytes 52
  38.0 33.7 %copy-start.1 = (s32[1,4]{1,0:T(1,128)S(1)}, s32[1,4]{1,0:T(1,128)}, u32[]{:S(2)}) copy-start(s32[1,4]{1,0:T(1,128)} %param.26) | copy-start | bytes 52
  38.0 33.8 %copy-start.7 = (s32[1,16]{1,0:T(1,128)S(1)}, s32[1,16]{1,0:T(1,128)}, u32[]{:S(2)}) copy-start(s32[1,16]{1,0:T(1,128)} %param.27) | copy-start | bytes 196
  38.0 33.9 %copy-start.6 = (s32[1,320]{1,0:T(1,128)S(1)}, s32[1,320]{1,0:T(1,128)}, u32[]{:S(2)}) copy-start(s32[1,320]{1,0:T(1,128)} %param.31) | copy-start | bytes 3844
  42.3 20.2 %all-to-all-start.1 = ((bf16[16,4,4224]{2,1,0:T(4,128)(2,1)}), bf16[16,4,4224]{2,1,0:T(4,128)(2,1)}, u32[]{:S(2)}, u32[]{:S(2)}) async-start(bf16[16,4,4224]{2,1,0:T(4,128)(2,1)} %broadcast_in_dim.134), calls=%async_computation.1 | async-start | bytes 1081344 | tf_op jit(solution)/shard_map/all_to_all | solution.py:346
  63.7 11.1 %copy-start.5 = (s32[1,4,48]{2,1,0:T(4,128)S(1)}, s32[1,4,48]{2,1,0:T(4,128)}, u32[]{:S(2)}) copy-start(s32[1,4,48]{2,1,0:T(4,128)} %param.25) | copy-start | bytes 2308
  69.5 9.8 %collective-permute-start = (bf16[512,4096]{1,0:T(8,128)(2,1)}, bf16[512,4096]{1,0:T(8,128)(2,1)}, u32[]{:S(2)}, u32[]{:S(2)}) collective-permute-start(bf16[512,4096]{1,0:T(8,128)(2,1)} %fusion.2.own_hbm), channel_id=1, source_target_pairs={{0,16},{16,0},{1,17},{17,1},{2,18},{18,2},{3,19},{19,3},{4,20},{20... | collective-permute-start | bytes 12582920 | tf_op jit(solution)/shard_map/ppermute | solution.py:364
  74.4 4.9 %collective-permute-start.1 = (f32[512,256]{1,0:T(8,128)S(1)}, f32[512,256]{1,0:T(8,128)S(1)}, u32[]{:S(2)}, u32[]{:S(2)}) collective-permute-start(f32[512,256]{1,0:T(8,128)S(1)} %pad_maximum_fusion.1.tab_own), channel_id=1, source_target_pairs={{0,16},{16,0},{1,17},{17,1},{2,18},{18,2},{3,19},{19,3},{4,20},{20... | collective-permute-start | bytes 1572872 | tf_op jit(solution)/shard_map/ppermute | solution.py:365
  123.6 16.0 %copy-start = (bf16[512,512]{1,0:T(8,128)(2,1)S(1)}, bf16[512,512]{1,0:T(8,128)(2,1)}, u32[]{:S(2)}) copy-start(bf16[512,512]{1,0:T(8,128)(2,1)} %kv.1) | copy-start | bytes 1572868
  123.6 28.8 %copy-start.8 = (s32[1,16]{1,0:T(1,128)S(1)}, s32[1,16]{1,0:T(1,128)}, u32[]{:S(2)}) copy-start(s32[1,16]{1,0:T(1,128)} %param.29) | copy-start | bytes 196
  137.1 2.5 %collective-permute-start.2 = (bf16[320,1024]{1,0:T(8,128)(2,1)S(1)}, bf16[320,1024]{1,0:T(8,128)(2,1)S(1)}, u32[]{:S(2)}, u32[]{:S(2)}) collective-permute-start(bf16[320,1024]{1,0:T(8,128)(2,1)S(1)} %get-tuple-element.10), channel_id=1, source_target_pairs={{0,16},{16,0},{1,17},{17,1},{2,18},{18,2},{3,19},{19,3},{4,20},{20... | collective-permute-start | bytes 1966088 | tf_op jit(solution)/shard_map/ppermute | solution.py:396
  145.3 27.4 %all-to-all-start.2 = ((f32[16,4,2176]{2,1,0:T(4,128)}), f32[16,4,2176]{2,1,0:T(4,128)S(1)}, u32[]{:S(2)}, u32[]{:S(2)}) async-start(f32[16,4,2176]{2,1,0:T(4,128)} %all_to_all.15), calls=%async_computation.2 | async-start | bytes 1114112 | tf_op jit(solution)/shard_map/all_to_all | solution.py:398
  152.5 2.6 %copy-start.2 = (bf16[84,64,512]{2,1,0:T(8,128)(2,1)S(1)}, bf16[84,64,512]{2,1,0:T(8,128)(2,1)}, u32[]{:S(2)}) copy-start(bf16[84,64,512]{2,1,0:T(8,128)(2,1)} %pool.1) | copy-start | bytes 16515076
Sparse Core Ops, SparseCore 0:
  38.1 85.4 all-gather.1

commit v2 on v1

v2 whole, which is shorter than its diff:
```python
import functools

import jax
import jax.numpy as jnp
from jax import lax
from jax.experimental import pallas as pl
from jax.experimental.pallas import tpu as pltpu
from jax.sharding import Mesh
from jax.sharding import PartitionSpec as P

QUERY_HEADS = 16
KEY_VALUE_HEADS = 2
GROUP = QUERY_HEADS // KEY_VALUE_HEADS
HEAD_SIZE = 128
PAGE_TOKENS = 64
PRE = 128
DEC = 4
REC = 320
LINE = 64
ROWS = PRE + LINE + REC
QROWS = PRE + LINE
DEC_SLOTS = 68
HIST_SLOTS = 16
HALF = GROUP * HEAD_SIZE
WIDE = HALF + 2 * HEAD_SIZE
MODEL = 4096
SPAN = 512
STAT = QUERY_HEADS * HEAD_SIZE
SPLIT = 512
HEADS_AT_ONCE = 2
LOG2E = 1.4426950408889634

AXES = ("zh", "x", "c", "zl", "y")
DP = ("zl", "y")

theta_base = 5000000.0
epsilon = 1e-05
negative_large = -1e30
scale = HEAD_SIZE**-0.5

f32 = jnp.float32
bf16 = jnp.bfloat16
ANY = pl.BlockSpec(memory_space=pl.ANY)
VMEM = pl.BlockSpec(memory_space=pltpu.VMEM)
HBM = pl.BlockSpec(memory_space=pltpu.HBM)
SMEM = pl.BlockSpec(memory_space=pltpu.SMEM)


def dot_t(a, b):
    return lax.dot_general(a, b, (((1,), (1,)), ((), ())), preferred_element_type=f32)


def dot(a, b):
    return lax.dot_general(a, b, (((1,), (0,)), ((), ())), preferred_element_type=f32)


def turned(values, tab):
    return values * tab[:, :HEAD_SIZE] + pltpu.roll(values, HEAD_SIZE // 2, 1) * tab[:, HEAD_SIZE:]

def project_kernel(w_hbm, own_hbm, other_hbm, tab_own, tab_oth, q_own, kv_own, packed, w, x, w_sem, x_sem):
    copies = [
        pltpu.make_async_copy(own_hbm.at[0:QROWS], x.at[0:QROWS], x_sem.at[0]),
        pltpu.make_async_copy(other_hbm.at[0:QROWS], x.at[QROWS : 2 * QROWS], x_sem.at[1]),
        pltpu.make_async_copy(own_hbm.at[QROWS:ROWS], x.at[2 * QROWS : 2 * QROWS + REC], x_sem.at[2]),
        pltpu.make_async_copy(other_hbm.at[QROWS:ROWS], x.at[2 * QROWS + REC : 2 * ROWS], x_sem.at[3]),
    ]
    groups = [(0, SPLIT), (SPLIT, WIDE)]
    pieces=[]
    for k,(lo,hi) in enumerate(groups):
        for xi in range(4):
            for yi in range(4):
                pieces.append(pltpu.make_async_copy(w_hbm.at[xi*4+yi, :, :, :, :, lo:hi], w.at[:, xi, :, :, yi, :, lo:hi], w_sem.at[k, xi*4+yi]))
    for copy in copies[:2]: copy.start()
    for copy in pieces: copy.start()
    for copy in copies[2:]: copy.start()
    for copy in copies[:2]: copy.wait()
    wf = w.reshape(MODEL, WIDE)
    for k,(lo,hi) in enumerate(groups):
        for copy in pieces[k*16:(k+1)*16]: copy.wait()
        for c0 in range(lo,hi,256):
            cols=slice(c0,c0+256)
            if c0<HALF:
                acc = dot(x[0:2*QROWS, :], wf[:, cols])
                for h in range(2):
                    at = slice(c0 + h * HEAD_SIZE, c0 + (h + 1) * HEAD_SIZE)
                    part = acc[:, h * HEAD_SIZE : (h + 1) * HEAD_SIZE]
                    q_own[:, at] = turned(part[:QROWS], tab_own[0:QROWS,:]).astype(bf16)
                    packed[0:QROWS, at] = turned(part[QROWS:], tab_oth[0:QROWS,:]).astype(bf16)
            else:
                for copy in copies[2:]: copy.wait()
                acc = dot(x[...], wf[:, cols])
                for own in (True, False):
                    tab = (tab_own if own else tab_oth)[...]
                    first = acc[0:QROWS] if own else acc[QROWS : 2 * QROWS]
                    rest = acc[2 * QROWS : 2 * QROWS + REC] if own else acc[2 * QROWS + REC :]
                    both = jnp.concatenate([first, rest], axis=0)
                    keys = turned(both[:, :HEAD_SIZE], tab).astype(bf16)
                    values = both[:, HEAD_SIZE:].astype(bf16)
                    if own:
                        kv_own[:, :HEAD_SIZE] = keys
                        kv_own[:, HEAD_SIZE:] = values
                    else:
                        for b in range(4):
                            rows = slice(b * 128, (b + 1) * 128)
                            packed[QROWS:, b * 256 : b * 256 + 128] = keys[rows]
                            packed[QROWS:, b * 256 + 128 : (b + 1) * 256] = values[rows]

def project(weights, own, other, tab_own, tab_oth):
    return pl.pallas_call(
        project_kernel, name="project",
        out_shape=(jax.ShapeDtypeStruct((QROWS, HALF), bf16), jax.ShapeDtypeStruct((ROWS, 2 * HEAD_SIZE), bf16), jax.ShapeDtypeStruct((QROWS + 128, HALF), bf16)),
        in_specs=[ANY, ANY, ANY, VMEM, VMEM], out_specs=(VMEM, VMEM, VMEM),
        scratch_shapes=[pltpu.VMEM((2, 4, 2, 4, 4, 16, WIDE), bf16), pltpu.VMEM((2 * ROWS, MODEL), bf16),
            pltpu.SemaphoreType.DMA((2, 16)), pltpu.SemaphoreType.DMA((4,))],
        compiler_params=pltpu.CompilerParams(vmem_limit_bytes=40 << 20),
        cost_estimate=pl.CostEstimate(flops=6 * 10**9, bytes_accessed=20 * 10**6, transcendentals=0),
    )(weights, own, other, tab_own, tab_oth)


def shared_kernel(info, q_own, packed, kv, out, qs):
    core = info[0]
    qs[core] = q_own[PRE:QROWS, :]
    qs[1 - core] = packed[PRE:QROWS, :]
    limit = info[1]
    bias = jnp.where(lax.broadcasted_iota(jnp.int32, (1, SPAN), 1) < limit, 0.0, negative_large)
    lane = lax.broadcasted_iota(jnp.int32, (LINE, HEAD_SIZE), 1)
    stats = jnp.zeros((LINE, HEAD_SIZE), f32)
    ones = jnp.ones((SPAN, HEAD_SIZE), bf16)
    c2 = scale*LOG2E
    for s in range(KEY_VALUE_HEADS):
        keys = kv[:, s * HEAD_SIZE : (s + 1) * HEAD_SIZE]
        values = jnp.concatenate([kv[:, (2 + s) * HEAD_SIZE : (3 + s) * HEAD_SIZE], ones], axis=1)
        query = jnp.concatenate([qs[s, :, h * HEAD_SIZE : (h + 1) * HEAD_SIZE] for h in range(GROUP)], axis=0)
        scores = dot_t(query, keys) + bias
        top = jnp.max(scores, axis=-1, keepdims=True)
        weights = jnp.exp2((scores - top) * c2)
        result = dot(weights.astype(bf16), values)
        total = result[:, HEAD_SIZE:]
        done = result[:, :HEAD_SIZE] / total
        level = top * scale + jnp.log(total)
        for h in range(GROUP):
            head = s * GROUP + h
            out[:, :, head * HEAD_SIZE : (head + 1) * HEAD_SIZE] = done[h*LINE:(h+1)*LINE].reshape(16,4,HEAD_SIZE)
            stats = jnp.where(lane == head, level[h*LINE:(h+1)*LINE], stats)
    out[:, :, STAT:] = stats.reshape(16,4,HEAD_SIZE)
def shared_attention(info, q_own, packed, kv):
    return pl.pallas_call(shared_kernel, name="shared", out_shape=jax.ShapeDtypeStruct((16,4, STAT + 128), f32),
        in_specs=[SMEM, VMEM, VMEM, VMEM], out_specs=VMEM, scratch_shapes=[pltpu.VMEM((2, LINE, HALF), bf16)],
        compiler_params=pltpu.CompilerParams(vmem_limit_bytes=16 << 20),
        cost_estimate=pl.CostEstimate(flops=3 * 10**8, bytes_accessed=10**6, transcendentals=10**6))(info, q_own, packed, kv)


def pages_kernel(slots, pool, pages, sems):
    copies=[pltpu.make_async_copy(pool.at[slots[i]], pages.at[i], sems.at[i]) for i in range(DEC_SLOTS+HIST_SLOTS)]
    for c in copies: c.start()
    for c in copies: c.wait()
def take_pages(slots,pool):
    return pl.pallas_call(pages_kernel,name="take_pages",out_shape=jax.ShapeDtypeStruct((DEC_SLOTS+HIST_SLOTS,PAGE_TOKENS,4*HEAD_SIZE),bf16),
      in_specs=[SMEM,HBM],out_specs=HBM,scratch_shapes=[pltpu.SemaphoreType.DMA((DEC_SLOTS+HIST_SLOTS,))],
      compiler_params=pltpu.CompilerParams(vmem_limit_bytes=60<<20),
      cost_estimate=pl.CostEstimate(flops=0, bytes_accessed=11 * 10**6, transcendentals=0))(slots,pool)

def local_kernel(info, q_own, kv_own, packed, bias_private, bias_new, pages_hbm, out_pre, out_dec, stat_dec, qs, ks, pages, sems):
    old = pltpu.make_async_copy(pages_hbm.at[DEC_SLOTS:], pages.at[DEC_SLOTS:], sems.at[0])
    old.start()
    cached = pltpu.make_async_copy(pages_hbm.at[:DEC_SLOTS], pages.at[:DEC_SLOTS], sems.at[1])
    cached.start()
    core = info[0]; start = info[2]; place = info[3]
    qs[core] = q_own[...]
    qs[1 - core] = packed[0:QROWS, :]
    ks[core] = kv_own[...]
    for b in range(4):
        ks[1 - core, b * 128 : (b + 1) * 128, :] = packed[QROWS:, b * 256 : (b + 1) * 256]
    history = HIST_SLOTS * PAGE_TOKENS
    seen = jnp.where(lax.broadcasted_iota(jnp.int32, (1, history), 1) < start, 0.0, negative_large)
    rows = lax.broadcasted_iota(jnp.int32, (PRE, PRE), 0)
    cols = lax.broadcasted_iota(jnp.int32, (PRE, PRE), 1)
    causal = jnp.where(cols <= rows, 0.0, negative_large)
    causal = jnp.concatenate([causal]*HEADS_AT_ONCE, axis=0)
    c2 = scale*LOG2E
    ones_h = jnp.ones((history, HEAD_SIZE), bf16)
    ones_n = jnp.ones((PRE, HEAD_SIZE), bf16)
    old.wait()
    for s in range(KEY_VALUE_HEADS):
        old_keys = pages[DEC_SLOTS:, :, s * HEAD_SIZE : (s + 1) * HEAD_SIZE].reshape(history, HEAD_SIZE)
        old_values = pages[DEC_SLOTS:, :, (2 + s) * HEAD_SIZE : (3 + s) * HEAD_SIZE].reshape(history, HEAD_SIZE)
        old_values = jnp.concatenate([old_values, ones_h], axis=1)
        new_keys = ks[s, 0:PRE, 0:HEAD_SIZE]
        new_values = jnp.concatenate([ks[s, 0:PRE, HEAD_SIZE:], ones_n], axis=1)
        for h in range(0, GROUP, HEADS_AT_ONCE):
            query = jnp.concatenate([qs[s, 0:PRE, (h+j) * HEAD_SIZE : (h+j + 1) * HEAD_SIZE] for j in range(HEADS_AT_ONCE)], axis=0)
            first = dot_t(query, old_keys) + seen
            second = dot_t(query, new_keys) + causal
            top = jnp.maximum(jnp.max(first, axis=-1, keepdims=True), jnp.max(second, axis=-1, keepdims=True))
            first = jnp.exp2((first - top) * c2)
            second = jnp.exp2((second - top) * c2)
            result = dot(first.astype(bf16), old_values) + dot(second.astype(bf16), new_values)
            done = (result[:, :HEAD_SIZE] / result[:, HEAD_SIZE:]).astype(bf16)
            for j in range(HEADS_AT_ONCE):
                head = s * GROUP + h + j
                out_pre[:, head * HEAD_SIZE : (head + 1) * HEAD_SIZE] = done[j*PRE:(j+1)*PRE]
    private = DEC_SLOTS * PAGE_TOKENS
    R = GROUP*DEC
    row = lax.broadcasted_iota(jnp.int32, (R, GROUP*LINE), 0)
    col = lax.broadcasted_iota(jnp.int32, (R, GROUP*LINE), 1)
    pick = (row >> 2 == col >> 6) & ((col & 63) == place * DEC + (row & 3))
    pick = jnp.where(pick, 1.0, 0.0).astype(bf16)
    cached.wait()
    for s in range(KEY_VALUE_HEADS):
        old_keys = pages[:DEC_SLOTS, :, s * HEAD_SIZE : (s + 1) * HEAD_SIZE].reshape(private, HEAD_SIZE)
        old_values = pages[:DEC_SLOTS, :, (2 + s) * HEAD_SIZE : (3 + s) * HEAD_SIZE].reshape(private, HEAD_SIZE)
        new_keys = ks[s, :, 0:HEAD_SIZE]
        new_values = ks[s, :, HEAD_SIZE:]
        line = jnp.concatenate([qs[s, PRE:QROWS, h * HEAD_SIZE : (h + 1) * HEAD_SIZE] for h in range(GROUP)], axis=0)
        query = dot(pick, line).astype(bf16)
        first = (dot_t(query, old_keys).reshape(R//8, 8, private) + bias_private[...][None]).reshape(R, private)
        second = (dot_t(query, new_keys).reshape(R//8, 8, ROWS) + bias_new[...][None]).reshape(R, ROWS)
        top = jnp.maximum(jnp.max(first, axis=-1, keepdims=True), jnp.max(second, axis=-1, keepdims=True))
        first = jnp.exp2((first - top) * c2)
        second = jnp.exp2((second - top) * c2)
        total = jnp.sum(first, axis=-1, keepdims=True) + jnp.sum(second, axis=-1, keepdims=True)
        result = dot(first.astype(bf16), old_values) + dot(second.astype(bf16), new_values)
        out_dec[s*R:(s+1)*R, :] = result / total
        stat_dec[s*R:(s+1)*R, :] = jnp.broadcast_to(top * scale + jnp.log(total), (R, HEAD_SIZE))

def local_attention(info, q_own, kv_own, packed, bias_private, bias_new, pages):
    return pl.pallas_call(
        local_kernel, name="local",
        out_shape=(jax.ShapeDtypeStruct((PRE, QUERY_HEADS * HEAD_SIZE), bf16), jax.ShapeDtypeStruct((64, HEAD_SIZE), f32), jax.ShapeDtypeStruct((64, HEAD_SIZE), f32)),
        in_specs=[SMEM, VMEM, VMEM, VMEM, VMEM, VMEM, HBM], out_specs=(VMEM, VMEM, VMEM),
        scratch_shapes=[pltpu.VMEM((2, QROWS, HALF), bf16), pltpu.VMEM((2, ROWS, 2 * HEAD_SIZE), bf16), pltpu.VMEM((DEC_SLOTS + HIST_SLOTS, PAGE_TOKENS, 4 * HEAD_SIZE), bf16), pltpu.SemaphoreType.DMA((2,))],
        compiler_params=pltpu.CompilerParams(vmem_limit_bytes=48 << 20),
        cost_estimate=pl.CostEstimate(flops=10**10, bytes_accessed=8 * 10**6, transcendentals=3 * 10**6),
    )(info, q_own, kv_own, packed, bias_private, bias_new, pages)


def finish_kernel(groups, shared, local, local_stat, out):
    row = lax.broadcasted_iota(jnp.int32, (DEC, STAT + 128), 0)
    chosen = jnp.zeros((DEC, STAT + 128), f32)
    for r in range(DEC):
        chosen = jnp.where(row == r, shared[groups[r]], chosen)
    for head in range(QUERY_HEADS):
        rows = slice(head*DEC,(head+1)*DEC)
        at = slice(head * HEAD_SIZE, (head + 1) * HEAD_SIZE)
        far = chosen[:, STAT+head:STAT+head+1]
        near = local_stat[rows, 0:1]
        top = jnp.maximum(far, near)
        far = jnp.exp(far - top); near = jnp.exp(near - top)
        whole = far + near
        out[:, at] = (chosen[:, at] * (far/whole) + local[rows, :] * (near/whole)).astype(bf16)
def finish(groups, shared, local, local_stat):
    return pl.pallas_call(finish_kernel, name="finish", out_shape=jax.ShapeDtypeStruct((DEC, QUERY_HEADS * HEAD_SIZE), bf16),
        in_specs=[SMEM, VMEM, VMEM, VMEM], out_specs=VMEM, compiler_params=pltpu.CompilerParams(vmem_limit_bytes=8 << 20))(groups, shared, local, local_stat)


def small_lookup(entries, indices):
    matches = indices[..., None] == jnp.arange(entries.shape[0], dtype=jnp.int32)
    return jnp.sum(jnp.where(matches, entries, 0), axis=-1)


def rms_scaled(values, gain):
    widened = values.astype(f32)
    factor = lax.rsqrt(jnp.mean(widened * widened, axis=-1, keepdims=True) + epsilon)
    return (widened * factor * gain.astype(f32)).astype(bf16)


def gather_weights(w_query, key_value_weight):
    key_half = key_value_weight.reshape(16, 2, 2, HEAD_SIZE)
    halves = [
        jnp.concatenate([w_query[:, c * HALF : (c + 1) * HALF], key_half[:, 0, c], key_half[:, 1, c]], axis=1)
        for c in range(2)
    ]
    block = jnp.stack(halves, axis=0)
    sent = jnp.broadcast_to(block[None, :, None], (2, 2, 4, 16, WIDE)).reshape(16, 16, WIDE)
    column = lax.all_to_all(sent, ("zh", "c", "zl"), 0, 0, tiled=True)
    whole = lax.all_gather(column.reshape(256, WIDE), ("x", "y"), axis=0, tiled=True)
    return whole.reshape(16, 2, 2, 4, 16, WIDE)


def on_device(
    x_pre, x_dec, rec_hidden, norm_gain, w_query, key_value_weight, cache_pool, shared_kv,
    dec_len, dec_table, dec_group, prefix_len, pre_start, pre_table, rec_req, rec_off,
):
    core = lax.axis_index("c")
    place = lax.axis_index("zl") * 4 + lax.axis_index("y")
    lengths = dec_len[0]
    page_table = dec_table[0]
    groups = dec_group[0]
    prefix_line = prefix_len[0]
    request = rec_req[0]
    within = rec_off[0]

    weights = gather_weights(w_query, key_value_weight)

    dec_pos = small_lookup(prefix_line, groups) + lengths
    parts = jnp.stack([dec_pos // 64, dec_pos % 64], axis=1).astype(bf16)
    extra = jnp.concatenate([x_dec, parts, jnp.zeros((DEC, 126), bf16)], axis=1)
    line = lax.all_to_all(
        jnp.broadcast_to(extra[None], (16, DEC, MODEL + 128)), DP, 0, 0, tiled=True
    ).reshape(LINE, MODEL + 128)
    line_parts = line[:, MODEL : MODEL + 2].astype(jnp.int32)
    line_pos = line_parts[:, 0] * 64 + line_parts[:, 1]

    rows = jnp.concatenate([x_pre, line[:, :MODEL], rec_hidden], axis=0)
    normed = rms_scaled(rows, norm_gain)
    pre_pos = pre_start[0] + jnp.arange(PRE, dtype=jnp.int32)
    rec_pos = small_lookup(prefix_line, small_lookup(groups, request)) + within
    positions = jnp.concatenate([pre_pos, line_pos, rec_pos], axis=0)
    half_dim = HEAD_SIZE // 2
    frequency = theta_base ** (-jnp.arange(half_dim, dtype=f32) * 2.0 / HEAD_SIZE)
    angles = positions.astype(f32)[:, None] * frequency
    cosines = jnp.cos(angles)
    sines = jnp.sin(angles)
    table = jnp.concatenate([cosines, cosines, -sines, sines], axis=1)
    swap = [(0, 1), (1, 0)]
    other = lax.ppermute(normed, "c", swap)
    other_table = lax.ppermute(table, "c", swap)

    counts = (lengths + PAGE_TOKENS - 1) // PAGE_TOKENS
    ends = jnp.cumsum(counts)
    firsts = ends - counts
    slot = jnp.arange(DEC_SLOTS, dtype=jnp.int32)
    slot_request = jnp.sum((slot[:, None] >= ends[None, :]).astype(jnp.int32), axis=1)
    used = slot_request < DEC
    slot_request = jnp.minimum(slot_request, DEC - 1)
    slot_page = jnp.where(used, slot - small_lookup(firsts, slot_request), 0)
    dec_pages = small_lookup(page_table.reshape(-1), slot_request * page_table.shape[1] + slot_page)
    slots = jnp.concatenate([dec_pages, pre_table[0]], axis=0)
    key_pos = slot_page[:, None] * PAGE_TOKENS + jnp.arange(PAGE_TOKENS, dtype=jnp.int32)[None, :]
    valid = used[:, None] & (key_pos < small_lookup(lengths, slot_request)[:, None])
    rec_slot = small_lookup(firsts, request) + within // PAGE_TOKENS
    slot_hot = (rec_slot[None, :] == slot[:, None]).astype(bf16)
    token_hot = (within[:, None] % PAGE_TOKENS == jnp.arange(PAGE_TOKENS, dtype=jnp.int32)[None, :]).astype(bf16)
    replaced = jnp.dot(slot_hot, token_hot, preferred_element_type=f32) > 0.5
    kept = (valid & ~replaced).reshape(-1)
    eight = jnp.arange(8, dtype=jnp.int32) % DEC
    key_request = jnp.repeat(slot_request, PAGE_TOKENS)
    bias_private = jnp.where(kept[None, :] & (key_request[None, :] == eight[:, None]), 0.0, negative_large)
    new_request = jnp.concatenate(
        [jnp.full((PRE,), -1, jnp.int32), jnp.arange(LINE, dtype=jnp.int32) - place * DEC, request], axis=0
    )
    bias_new = jnp.where(new_request[None, :] == eight[:, None], 0.0, negative_large)
    own_prefix = small_lookup(prefix_line, place[None])[0]
    info = jnp.stack([core, own_prefix, pre_start[0], place]).astype(jnp.int32)

    pages = take_pages(slots, cache_pool)
    weights, pages, bias_private, bias_new, info, slots = lax.optimization_barrier(
        (weights, pages, bias_private, bias_new, info, slots)
    )
    q_own, kv_own, packed = project(weights, normed, other, table, other_table)
    packed = lax.ppermute(packed, "c", swap)
    shared_part = shared_attention(info, q_own, packed, shared_kv)
    shared_part = lax.all_to_all(shared_part, DP, 0, 0, tiled=True)
    out_pre, dec_part, dec_stat = local_attention(
        info, q_own, kv_own, packed, bias_private, bias_new, pages
    )
    out_dec = finish(groups, shared_part, dec_part, dec_stat)
    return (out_pre, out_dec)


def solution(mesh):
    split = Mesh(mesh.devices.reshape(2, 4, 2, 4, 4), AXES)
    first = P(AXES, None)
    second = P(AXES, None, None)
    return jax.shard_map(
        on_device,
        mesh=split,
        in_specs=(
            first, first, first, P(), first, first, second, first,
            first, second, first, P(("zh", "x", "c"), None), P(AXES), first, first, first,
        ),
        out_specs=(first, first),
        check_vma=False,
    )
```

time: 182 us -> 290 us (1.59)
  Pallas kernels: 37.4 us -> 191 us
  waiting for transfers between devices: 61 us -> 17.9 us
  starting transfers between devices: 16.2 us -> 12.9 us
  other arithmetic: 13.2 us -> 16.3 us
  local copies, waits for them, and re-layouts: 9.15 us -> 6.12 us
    pallas_call x0 -> x1, Pallas kernels: none -> 169 us  [take_pages(): pl.pallas_call(pages_kernel, name='take_pages', out_shape=jax.ShapeDtypeS...]
    all_gather x1, waiting for transfers between devices: 44.3 us -> 0.01 us  [gather_weights(): lax.all_gather(column.reshape(256, WIDE), ('x', 'y'), axis=0, tiled=True)]
    pallas_call x1, Pallas kernels: 17.7 us -> 8.42 us  [local_attention(): pl.pallas_call(local_kernel, name='local', out_shape=(jax.ShapeDtypeStruc...]
    all_to_all x1, waiting for transfers between devices: 0.01 us -> 6.41 us  [on_device(): shared_part = lax.all_to_all(shared_part, DP, 0, 0, tiled=True)]
    pallas_call x1, Pallas kernels: 13.5 us -> 9.76 us  [project(): pl.pallas_call(project_kernel, name='project', out_shape=(jax.ShapeDtypeS...]
    all_to_all x1, waiting for transfers between devices: 12.1 us -> 8.45 us  [on_device(): lax.all_to_all(jnp.broadcast_to(extra[None], (16, DEC, MODEL + 128)), DP,...]
  transfers between devices with their start and end apart: 6 -> 6, of which waited for: 4 -> 4; matrix products, arithmetic and copies ran while one was open for 9% -> 7% of each run, Pallas kernels for 10% -> 61%
where the time goes in v2:
time: 290 us; the launch traced here: 289 us
  Pallas kernels  191 us (66%)
  blocking collectives  29 us (10%)
  waiting for transfers between devices  17.9 us (6%)
  other arithmetic  16.3 us (6%)
  between operations  15 us (5%)
  starting transfers between devices  12.9 us (4%)
  local copies, waits for them, and re-layouts  6.12 us (2%)
    pallas_call x1, Pallas kernels, take_pages(): pl.pallas_call(pages_kernel, name='take_pages', out_shape=jax.ShapeDtypeS...  169 us
    all_to_all x1, blocking collectives, gather_weights(): column = lax.all_to_all(sent, ('zh', 'c', 'zl'), 0, 0, tiled=True)  29 us
    pallas_call x1, Pallas kernels, project(): pl.pallas_call(project_kernel, name='project', out_shape=(jax.ShapeDtypeS...  9.76 us
    all_to_all x1, waiting for transfers between devices, on_device(): lax.all_to_all(jnp.broadcast_to(extra[None], (16, DEC, MODEL + 128)), DP,...  8.45 us
    pallas_call x1, Pallas kernels, local_attention(): pl.pallas_call(local_kernel, name='local', out_shape=(jax.ShapeDtypeStruc...  8.42 us
    all_to_all x1, waiting for transfers between devices, on_device(): shared_part = lax.all_to_all(shared_part, DP, 0, 0, tiled=True)  6.41 us
  transfers between devices with their start and end apart: 6, of which 4 were waited for; matrix products, arithmetic and copies ran while one was open for 7% of the time, Pallas kernels for 61%

profile of v2, /device:TPU:1, one launch (start us, length us, event | category | flops | bytes accessed | tf_op | source)
XLA Modules:
  0.0 289.0 jit_solution(6577697551119316025)
XLA Ops:
  7.2 0.9 reshape.298
  8.1 0.8 fusion.15
  9.0 29.0 %all_to_all.15 = bf16[16,16,1280]{2,1,0:T(8,128)(2,1)} all-to-all(bf16[16,16,1280]{2,1,0:T(8,128)(2,1)S(1)} %bitcast.48), channel_id=1, replica_groups=mesh['zh'=2,'x'=4,'c'=2,'zl'=4,'y'=4] {'zh','c','zl'}, dimensions={0} | all-to-all | bytes 1310720 | tf_op jit(solution)/shard_map/all_to_all | solution.py:275
  38.0 0.9 select_reduce_fusion.4
  38.9 0.7 fusion.12
  39.6 0.1 copy.44
  39.7 0.7 fusion.14
  40.3 0.1 copy.43
  40.4 0.9 concatenate.35
  41.3 0.9 broadcast_in_dim.142
  42.2 5.8 %all-to-all-start.1 = ((bf16[16,4,4224]{2,1,0:T(4,128)(2,1)}), bf16[16,4,4224]{2,1,0:T(4,128)(2,1)}, u32[]{:S(2)}, u32[]{:S(2)}) async-start(bf16[16,4,4224]{2,1,0:T(4,128)(2,1)} %broadcast_in_dim.142), calls=%async_computation.1 | async-start | bytes 1081344 | tf_op jit(solution)/shard_map/all_to_all | solution.py:298
  48.7 0.8 reshape_squeeze.3
  49.5 0.2 reduce-window.8
  49.6 0.7 reduce.1
  50.3 0.7 convert_element_type.27
  51.0 0.1 convert_reduce_fusion
  51.1 0.7 fusion.13
  51.8 0.7 select_reduce_fusion.2
  52.5 0.7 select_reduce_fusion.1
  53.3 0.7 add_reduce_fusion
  54.0 8.5 %all-to-all-done.1 = bf16[16,4,4224]{2,1,0:T(4,128)(2,1)} async-done(((bf16[16,4,4224]{2,1,0:T(4,128)(2,1)}), bf16[16,4,4224]{2,1,0:T(4,128)(2,1)}, u32[]{:S(2)}, u32[]{:S(2)}) %all-to-all-start.1) | async-done | bytes 540704 | tf_op jit(solution)/shard_map/all_to_all | solution.py:298
  62.4 1.2 reshape.303
  63.7 2.0 fusion
  65.7 3.5 %fusion.2.own_hbm = bf16[512,4096]{1,0:T(8,128)(2,1)} fusion(f32[4096]{0:T(1024)S(1)} %convert_element_type.27, f32[512]{0:T(512)S(1)} %add_rsqrt_fusion, bf16[320,4096]{1,0:T(8,128)(2,1)S(1)} %copy-done.2, bf16[64,4096]{1,0:T(8,128)(2,1)S(1)} %slice.44, bf16[128,4096]{1,0:T(8,128)(2,1)} %param.16), kind=kLoop, calls=%fused_computation.4 | loop fusion | flops 18874368 | bytes 8407040 | tf_op jit(solution)/shard_map/convert_element_type | solution.py:264
  69.3 2.3 collective-permute-start
  71.6 0.1 select_reduce_fusion.5
  71.7 0.3 fusion.4
  72.0 0.1 copy.42
  72.1 0.1 and.120
  72.4 0.2 select_reduce_fusion
  72.6 0.6 pad_add_fusion.1.slots
  73.1 169.3 %take_pages.1.pages_hbm = bf16[84,64,512]{2,1,0:T(8,128)(2,1)} custom-call(s32[84]{0:T(128)} %pad_add_fusion.1.slots, bf16[84,64,512]{2,1,0:T(8,128)(2,1)} %pool.1), custom_call_target="tpu_custom_call" | custom-call | bytes 11000000 | tf_op jit(solution)/shard_map/take_pages/pallas_call | solution.py:158
  242.5 0.6 fusion.11
  243.2 0.1 and_select_fusion.bias_private
  243.3 0.2 fusion.8
  243.5 1.0 multiply_cosine_fusion
  244.5 0.3 pad_maximum_fusion.1.tab_own
  244.8 0.1 collective-permute-start.1
  244.9 0.6 pad_add_fusion.2.info
  245.7 1.1 collective-permute-done.1.tab_oth
  246.8 9.8 %project.1 = (bf16[192,1024]{1,0:T(8,128)(2,1)S(1)}, bf16[512,256]{1,0:T(8,128)(2,1)S(1)}, bf16[320,1024]{1,0:T(8,128)(2,1)S(1)}) custom-call(bf16[16,2,2,4,16,1280]{5,4,3,2,1,0:T(8,128)(2,1)} %bitcast.52, bf16[512,4096]{1,0:T(8,128)(2,1)} %fusion.2.own_hbm, bf16[512,4096]{1,0:T(8,128)(2,1)} %collective-permute-done.other_hbm, ...), custom_call_target="tpu_custom_call" | custom-call | flops 6000000000 | bytes 20000000 | tf_op jit(solution)/shard_map/project/pallas_call | solution.py:109
  256.6 0.4 collective-permute-start.2
  257.0 2.0 collective-permute-done.2.packed
  258.9 2.4 shared.1
  261.4 4.4 %all-to-all-start.2 = ((f32[16,4,2176]{2,1,0:T(4,128)}), f32[16,4,2176]{2,1,0:T(4,128)S(1)}, u32[]{:S(2)}, u32[]{:S(2)}) async-start(f32[16,4,2176]{2,1,0:T(4,128)} %shared.1), calls=%async_computation.2 | async-start | bytes 1114112 | tf_op jit(solution)/shard_map/all_to_all | solution.py:353
  265.8 8.4 %local.1 = (bf16[128,2048]{1,0:T(8,128)(2,1)}, f32[64,128]{1,0:T(8,128)S(1)}, f32[64,128]{1,0:T(8,128)S(1)}) custom-call(s32[4]{0:T(128)S(1)} %pad_add_fusion.2.info, bf16[192,1024]{1,0:T(8,128)(2,1)S(1)} %get-tuple-element.15.q_own, bf16[512,256]{1,0:T(8,128)(2,1)S(1)} %get-tuple-element.16.kv_own, bf16[320,1024]{1,0:T(8,128)(2,1)S(1)} %collective-permute-done.2.packed, ...), custom_call_target="tpu_custom_call" | custom-call | flops 10000000000 | bytes 8000000 | tf_op jit(solution)/shard_map/local/pallas_call | solution.py:227
  274.2 6.4 %all-to-all-done.2.shared = f32[16,4,2176]{2,1,0:T(4,128)S(1)} async-done(((f32[16,4,2176]{2,1,0:T(4,128)}), f32[16,4,2176]{2,1,0:T(4,128)S(1)}, u32[]{:S(2)}, u32[]{:S(2)}) %all-to-all-start.2) | async-done | bytes 557088 | tf_op jit(solution)/shard_map/all_to_all | solution.py:353
  280.6 1.5 finish.1
  (41 shorter events, 0.7 us)
Async XLA Ops:
  7.2 56.5 %copy-start.2 = (bf16[320,4096]{1,0:T(8,128)(2,1)S(1)}, bf16[320,4096]{1,0:T(8,128)(2,1)}, u32[]{:S(2)}) copy-start(bf16[320,4096]{1,0:T(8,128)(2,1)} %param.18) | copy-start | bytes 7864324
  7.2 238.5 %all-gather.2.cloned.1.call-start = ((), (), s32[]{:S(2)}) async-start(), calls=%async_computation.3 | async-start | bytes 11141120 | tf_op jit(solution)/shard_map/all_gather | solution.py:276
  38.0 33.5 %copy-start.3 = (s32[1,4]{1,0:T(1,128)S(1)}, s32[1,4]{1,0:T(1,128)}, u32[]{:S(2)}) copy-start(s32[1,4]{1,0:T(1,128)} %param.24) | copy-start | bytes 52
  41.3 31.3 %copy-start.5 = (s32[1,16]{1,0:T(1,128)S(1)}, s32[1,16]{1,0:T(1,128)}, u32[]{:S(2)}) copy-start(s32[1,16]{1,0:T(1,128)} %param.29) | copy-start | bytes 196
  42.2 20.2 %all-to-all-start.1 = ((bf16[16,4,4224]{2,1,0:T(4,128)(2,1)}), bf16[16,4,4224]{2,1,0:T(4,128)(2,1)}, u32[]{:S(2)}, u32[]{:S(2)}) async-start(bf16[16,4,4224]{2,1,0:T(4,128)(2,1)} %broadcast_in_dim.142), calls=%async_computation.1 | async-start | bytes 1081344 | tf_op jit(solution)/shard_map/all_to_all | solution.py:298
  65.7 176.8 %copy-start.4 = (s32[1,16]{1,0:T(1,128)S(1)}, s32[1,16]{1,0:T(1,128)}, u32[]{:S(2)}) copy-start(s32[1,16]{1,0:T(1,128)} %param.27) | copy-start | bytes 196
  69.3 177.5 %collective-permute-start = (bf16[512,4096]{1,0:T(8,128)(2,1)}, bf16[512,4096]{1,0:T(8,128)(2,1)}, u32[]{:S(2)}, u32[]{:S(2)}) collective-permute-start(bf16[512,4096]{1,0:T(8,128)(2,1)} %fusion.2.own_hbm), channel_id=1, source_target_pairs={{0,16},{16,0},{1,17},{17,1},{2,18},{18,2},{3,19},{19,3},{4,20},{20... | collective-permute-start | bytes 12582920 | tf_op jit(solution)/shard_map/ppermute | solution.py:316
  244.8 2.0 collective-permute-start.1
  245.7 13.2 %copy-start = (bf16[512,512]{1,0:T(8,128)(2,1)S(1)}, bf16[512,512]{1,0:T(8,128)(2,1)}, u32[]{:S(2)}) copy-start(bf16[512,512]{1,0:T(8,128)(2,1)} %kv.1) | copy-start | bytes 1572868
  256.6 2.4 collective-permute-start.2
  261.4 19.2 %all-to-all-start.2 = ((f32[16,4,2176]{2,1,0:T(4,128)}), f32[16,4,2176]{2,1,0:T(4,128)S(1)}, u32[]{:S(2)}, u32[]{:S(2)}) async-start(f32[16,4,2176]{2,1,0:T(4,128)} %shared.1), calls=%async_computation.2 | async-start | bytes 1114112 | tf_op jit(solution)/shard_map/all_to_all | solution.py:353
  265.7 14.9 %copy-start.1 = (s32[1,4]{1,0:T(1,128)S(1)}, s32[1,4]{1,0:T(1,128)}, u32[]{:S(2)}) copy-start(s32[1,4]{1,0:T(1,128)} %param.26) | copy-start | bytes 52
Sparse Core Ops, SparseCore 0:
  38.1 85.4 all-gather.1

commit v3 on v2

--- a/solution.py
+++ b/solution.py
@@ -150,15 +150,36 @@
         cost_estimate=pl.CostEstimate(flops=3 * 10**8, bytes_accessed=10**6, transcendentals=10**6))(info, q_own, packed, kv)
 
 
-def pages_kernel(slots, pool, pages, sems):
-    copies=[pltpu.make_async_copy(pool.at[slots[i]], pages.at[i], sems.at[i]) for i in range(DEC_SLOTS+HIST_SLOTS)]
-    for c in copies: c.start()
-    for c in copies: c.wait()
-def take_pages(slots,pool):
-    return pl.pallas_call(pages_kernel,name="take_pages",out_shape=jax.ShapeDtypeStruct((DEC_SLOTS+HIST_SLOTS,PAGE_TOKENS,4*HEAD_SIZE),bf16),
-      in_specs=[SMEM,HBM],out_specs=HBM,scratch_shapes=[pltpu.SemaphoreType.DMA((DEC_SLOTS+HIST_SLOTS,))],
-      compiler_params=pltpu.CompilerParams(vmem_limit_bytes=60<<20),
-      cost_estimate=pl.CostEstimate(flops=0, bytes_accessed=11 * 10**6, transcendentals=0))(slots,pool)
+def pages_kernel(slots, pool, pages, held, sems, out_sem):
+    copies = [
+        pltpu.make_async_copy(pool.at[slots[i]], held.at[i], sems.at[i]) for i in range(DEC_SLOTS + HIST_SLOTS)
+    ]
+    for copy in copies:
+        copy.start()
+    for copy in copies:
+        copy.wait()
+    out = pltpu.make_async_copy(held, pages, out_sem)
+    out.start()
+    out.wait()
+
+
+def take_pages(slots, pool):
+    shape = (DEC_SLOTS + HIST_SLOTS, PAGE_TOKENS, 4 * HEAD_SIZE)
+    return pl.pallas_call(
+        pages_kernel,
+        name="take_pages",
+        out_shape=jax.ShapeDtypeStruct(shape, bf16),
+        in_specs=[SMEM, HBM],
+        out_specs=HBM,
+        scratch_shapes=[
+            pltpu.VMEM(shape, bf16),
+            pltpu.SemaphoreType.DMA((DEC_SLOTS + HIST_SLOTS,)),
+            pltpu.SemaphoreType.DMA,
+        ],
+        compiler_params=pltpu.CompilerParams(vmem_limit_bytes=12 << 20),
+        cost_estimate=pl.CostEstimate(flops=0, bytes_accessed=22 * 10**6, transcendentals=0),
+    )(slots, pool)
+
 
 def local_kernel(info, q_own, kv_own, packed, bias_private, bias_new, pages_hbm, out_pre, out_dec, stat_dec, qs, ks, pages, sems):
     old = pltpu.make_async_copy(pages_hbm.at[DEC_SLOTS:], pages.at[DEC_SLOTS:], sems.at[0])

time: 290 us -> 170 us (0.59)
  Pallas kernels: 191 us -> 31.4 us
  waiting for transfers between devices: 17.9 us -> 50 us
  local copies, waits for them, and re-layouts: 6.12 us -> 11.1 us
  starting transfers between devices: 12.9 us -> 16.2 us
    pallas_call x1, Pallas kernels: 169 us -> 9.17 us  [take_pages(): pl.pallas_call(pages_kernel, name='take_pages', out_shape=jax.ShapeDtypeS...]
    all_gather x1, waiting for transfers between devices: 0.01 us -> 33.5 us  [gather_weights(): lax.all_gather(column.reshape(256, WIDE), ('x', 'y'), axis=0, tiled=True)]
    unnamed x12 -> x16, local copies, waits for them, and re-layouts: 0.03 us -> 5.03 us
  transfers between devices with their start and end apart: 6 -> 6, of which waited for: 4 -> 4; matrix products, arithmetic and copies ran while one was open for 7% -> 12% of each run, Pallas kernels for 61% -> 10%
where the time goes in v3:
time: 170 us; the launch traced here: 169 us
  waiting for transfers between devices  50 us (29%)
  Pallas kernels  31.4 us (18%)
  blocking collectives  29 us (17%)
  starting transfers between devices  16.2 us (10%)
  other arithmetic  15.8 us (9%)
  between operations  15 us (9%)
  local copies, waits for them, and re-layouts  11.1 us (7%)
    all_gather x1, waiting for transfers between devices, gather_weights(): lax.all_gather(column.reshape(256, WIDE), ('x', 'y'), axis=0, tiled=True)  33.5 us
    all_to_all x1, blocking collectives, gather_weights(): column = lax.all_to_all(sent, ('zh', 'c', 'zl'), 0, 0, tiled=True)  29 us
    pallas_call x1, Pallas kernels, project(): pl.pallas_call(project_kernel, name='project', out_shape=(jax.ShapeDtypeS...  9.82 us
    pallas_call x1, Pallas kernels, take_pages(): pl.pallas_call(pages_kernel, name='take_pages', out_shape=jax.ShapeDtypeS...  9.17 us
    all_to_all x1, waiting for transfers between devices, on_device(): lax.all_to_all(jnp.broadcast_to(extra[None], (16, DEC, MODEL + 128)), DP,...  8.45 us
    pallas_call x1, Pallas kernels, local_attention(): pl.pallas_call(local_kernel, name='local', out_shape=(jax.ShapeDtypeStruc...  8.42 us
    all_to_all x1, starting transfers between devices, on_device(): shared_part = lax.all_to_all(shared_part, DP, 0, 0, tiled=True)  7.03 us
    all_to_all x1, waiting for transfers between devices, on_device(): shared_part = lax.all_to_all(shared_part, DP, 0, 0, tiled=True)  6.21 us
  transfers between devices with their start and end apart: 6, of which 4 were waited for; matrix products, arithmetic and copies ran while one was open for 12% of the time, Pallas kernels for 10%

profile of v3, /device:TPU:1, one launch (start us, length us, event | category | flops | bytes accessed | tf_op | source)
XLA Modules:
  0.0 168.6 jit_solution(9458922112669786180)
XLA Ops:
  7.2 0.9 reshape.298
  8.1 0.8 fusion.15
  9.0 29.0 %all_to_all.15 = bf16[16,16,1280]{2,1,0:T(8,128)(2,1)} all-to-all(bf16[16,16,1280]{2,1,0:T(8,128)(2,1)S(1)} %bitcast.48), channel_id=1, replica_groups=mesh['zh'=2,'x'=4,'c'=2,'zl'=4,'y'=4] {'zh','c','zl'}, dimensions={0} | all-to-all | bytes 1310720 | tf_op jit(solution)/shard_map/all_to_all | solution.py:296
  38.0 0.9 select_reduce_fusion.4
  38.9 0.7 fusion.12
  39.6 0.1 copy.44
  39.7 0.7 fusion.14
  40.3 0.1 copy.43
  40.4 0.9 concatenate.35
  41.3 0.9 broadcast_in_dim.142
  42.2 5.8 %all-to-all-start.1 = ((bf16[16,4,4224]{2,1,0:T(4,128)(2,1)}), bf16[16,4,4224]{2,1,0:T(4,128)(2,1)}, u32[]{:S(2)}, u32[]{:S(2)}) async-start(bf16[16,4,4224]{2,1,0:T(4,128)(2,1)} %broadcast_in_dim.142), calls=%async_computation.1 | async-start | bytes 1081344 | tf_op jit(solution)/shard_map/all_to_all | solution.py:319
  48.7 0.8 reshape_squeeze.3
  49.5 0.2 reduce-window.8
  49.6 0.7 reduce.1
  50.3 0.7 convert_element_type.27
  51.1 0.7 fusion.13
  51.8 0.7 select_reduce_fusion.2
  52.5 0.7 select_reduce_fusion.1
  53.3 0.7 add_reduce_fusion
  54.0 8.5 %all-to-all-done.1 = bf16[16,4,4224]{2,1,0:T(4,128)(2,1)} async-done(((bf16[16,4,4224]{2,1,0:T(4,128)(2,1)}), bf16[16,4,4224]{2,1,0:T(4,128)(2,1)}, u32[]{:S(2)}, u32[]{:S(2)}) %all-to-all-start.1) | async-done | bytes 540704 | tf_op jit(solution)/shard_map/all_to_all | solution.py:319
  62.4 1.2 reshape.303
  63.7 2.0 %fusion = f32[512]{0:T(512)S(1)} fusion(bf16[320,4096]{1,0:T(8,128)(2,1)S(1)} %copy-done.4, bf16[64,4096]{1,0:T(8,128)(2,1)S(1)} %slice.44, bf16[128,4096]{1,0:T(8,128)(2,1)} %param.16), kind=kLoop, calls=%fused_computation.2 | loop fusion | flops 16776704 | bytes 4196352 | tf_op jit(solution)/shard_map/reduce_sum | solution.py:284
  65.7 3.5 %fusion.2.own_hbm = bf16[512,4096]{1,0:T(8,128)(2,1)} fusion(f32[4096]{0:T(1024)S(1)} %convert_element_type.27, f32[512]{0:T(512)S(1)} %add_rsqrt_fusion, bf16[320,4096]{1,0:T(8,128)(2,1)S(1)} %copy-done.4, bf16[64,4096]{1,0:T(8,128)(2,1)S(1)} %slice.44, bf16[128,4096]{1,0:T(8,128)(2,1)} %param.16), kind=kLoop, calls=%fused_computation.4 | loop fusion | flops 18874368 | bytes 8407040 | tf_op jit(solution)/shard_map/convert_element_type | solution.py:285
  69.3 2.3 %collective-permute-start = (bf16[512,4096]{1,0:T(8,128)(2,1)}, bf16[512,4096]{1,0:T(8,128)(2,1)}, u32[]{:S(2)}, u32[]{:S(2)}) collective-permute-start(bf16[512,4096]{1,0:T(8,128)(2,1)} %fusion.2.own_hbm), channel_id=1, source_target_pairs={{0,16},{16,0},{1,17},{17,1},{2,18},{18,2},{3,19},{19,3},{4,20},{20... | collective-permute-start | bytes 12582920 | tf_op jit(solution)/shard_map/ppermute | solution.py:337
  71.6 0.1 select_reduce_fusion.5
  71.7 0.3 fusion.4
  72.0 0.1 copy.42
  72.1 0.1 and.120
  72.4 0.2 select_reduce_fusion
  72.6 2.6 %copy-done = bf16[84,64,512]{2,1,0:T(8,128)(2,1)S(1)} copy-done((bf16[84,64,512]{2,1,0:T(8,128)(2,1)S(1)}, bf16[84,64,512]{2,1,0:T(8,128)(2,1)}, u32[]{:S(2)}) %copy-start) | copy-done | bytes 5505048
  75.2 9.2 %take_pages.1.pages_hbm = bf16[84,64,512]{2,1,0:T(8,128)(2,1)S(1)} custom-call(s32[84]{0:T(128)S(1)} %pad_add_fusion.1.slots, bf16[84,64,512]{2,1,0:T(8,128)(2,1)S(1)} %copy-done), custom_call_target="tpu_custom_call" | custom-call | bytes 22000000 | tf_op jit(solution)/shard_map/take_pages/pallas_call | solution.py:168
  84.4 2.4 %copy-done.1 = bf16[84,64,512]{2,1,0:T(8,128)(2,1)} copy-done((bf16[84,64,512]{2,1,0:T(8,128)(2,1)}, bf16[84,64,512]{2,1,0:T(8,128)(2,1)S(1)}, u32[]{:S(2)}) %copy-start.1) | copy-done | bytes 5505048
  86.8 0.6 fusion.11
  87.5 0.1 and_select_fusion.bias_private
  87.6 0.2 fusion.8
  87.9 1.0 multiply_cosine_fusion
  88.9 0.3 pad_maximum_fusion.1.tab_own
  89.1 0.1 collective-permute-start.1
  89.3 0.6 pad_add_fusion.2.info
  90.0 33.5 %all-gather.2.cloned.1.call-done = bf16[4096,1280]{1,0:T(8,128)(2,1)} async-done(((bf16[256,1280]{1,0:T(8,128)(2,1)}), bf16[4096,1280]{1,0:T(8,128)(2,1)}) %all-gather.2.cloned.1.call-update) | async-done | bytes 10485776 | tf_op jit(solution)/shard_map/all_gather | solution.py:297
  123.6 9.8 %project.1 = (bf16[192,1024]{1,0:T(8,128)(2,1)S(1)}, bf16[512,256]{1,0:T(8,128)(2,1)S(1)}, bf16[320,1024]{1,0:T(8,128)(2,1)S(1)}) custom-call(bf16[16,2,2,4,16,1280]{5,4,3,2,1,0:T(8,128)(2,1)} %bitcast.52, bf16[512,4096]{1,0:T(8,128)(2,1)} %fusion.2.own_hbm, bf16[512,4096]{1,0:T(8,128)(2,1)} %collective-permute-done.other_hbm, ...), custom_call_target="tpu_custom_call" | custom-call | flops 6000000000 | bytes 20000000 | tf_op jit(solution)/shard_map/project/pallas_call | solution.py:109
  133.4 0.9 collective-permute-start.2
  134.4 1.7 %collective-permute-done.2.packed = bf16[320,1024]{1,0:T(8,128)(2,1)S(1)} collective-permute-done((bf16[320,1024]{1,0:T(8,128)(2,1)S(1)}, bf16[320,1024]{1,0:T(8,128)(2,1)S(1)}, u32[]{:S(2)}, u32[]{:S(2)}) %collective-permute-start.2) | collective-permute-done | bytes 655392 | tf_op jit(solution)/shard_map/ppermute | solution.py:372
  136.1 2.4 %shared.1 = f32[16,4,2176]{2,1,0:T(4,128)} custom-call(s32[4]{0:T(128)S(1)} %pad_add_fusion.2.info, bf16[192,1024]{1,0:T(8,128)(2,1)S(1)} %get-tuple-element.15.q_own, bf16[320,1024]{1,0:T(8,128)(2,1)S(1)} %collective-permute-done.2.packed, bf16[512,512]{1,0:T(8,128)(2,1)S(1)} %copy-done.2), custom_call_target="tpu_custom_call" | custom-call | flops 300000000 | bytes 1000000 | tf_op jit(solution)/shard_map/shared/pallas_call | solution.py:147
  138.5 7.0 %all-to-all-start.2 = ((f32[16,4,2176]{2,1,0:T(4,128)}), f32[16,4,2176]{2,1,0:T(4,128)S(1)}, u32[]{:S(2)}, u32[]{:S(2)}) async-start(f32[16,4,2176]{2,1,0:T(4,128)} %shared.1), calls=%async_computation.2 | async-start | bytes 1114112 | tf_op jit(solution)/shard_map/all_to_all | solution.py:374
  145.6 8.4 %local.1 = (bf16[128,2048]{1,0:T(8,128)(2,1)}, f32[64,128]{1,0:T(8,128)S(1)}, f32[64,128]{1,0:T(8,128)S(1)}) custom-call(s32[4]{0:T(128)S(1)} %pad_add_fusion.2.info, bf16[192,1024]{1,0:T(8,128)(2,1)S(1)} %get-tuple-element.15.q_own, bf16[512,256]{1,0:T(8,128)(2,1)S(1)} %get-tuple-element.16.kv_own, bf16[320,1024]{1,0:T(8,128)(2,1)S(1)} %collective-permute-done.2.packed, ...), custom_call_target="tpu_custom_call" | custom-call | flops 10000000000 | bytes 8000000 | tf_op jit(solution)/shard_map/local/pallas_call | solution.py:248
  154.0 6.2 %all-to-all-done.2.shared = f32[16,4,2176]{2,1,0:T(4,128)S(1)} async-done(((f32[16,4,2176]{2,1,0:T(4,128)}), f32[16,4,2176]{2,1,0:T(4,128)S(1)}, u32[]{:S(2)}, u32[]{:S(2)}) %all-to-all-start.2) | async-done | bytes 557088 | tf_op jit(solution)/shard_map/all_to_all | solution.py:374
  160.2 1.5 finish.1
  (45 shorter events, 0.8 us)
Async XLA Ops:
  7.2 56.5 %copy-start.4 = (bf16[320,4096]{1,0:T(8,128)(2,1)S(1)}, bf16[320,4096]{1,0:T(8,128)(2,1)}, u32[]{:S(2)}) copy-start(bf16[320,4096]{1,0:T(8,128)(2,1)} %param.18) | copy-start | bytes 7864324
  7.2 116.4 %all-gather.2.cloned.1.call-start = ((), (), s32[]{:S(2)}) async-start(), calls=%async_computation.3 | async-start | bytes 11141120 | tf_op jit(solution)/shard_map/all_gather | solution.py:297
  38.0 33.5 %copy-start.5 = (s32[1,4]{1,0:T(1,128)S(1)}, s32[1,4]{1,0:T(1,128)}, u32[]{:S(2)}) copy-start(s32[1,4]{1,0:T(1,128)} %param.24) | copy-start | bytes 52
  41.3 31.3 %copy-start.7 = (s32[1,16]{1,0:T(1,128)S(1)}, s32[1,16]{1,0:T(1,128)}, u32[]{:S(2)}) copy-start(s32[1,16]{1,0:T(1,128)} %param.29) | copy-start | bytes 196
  42.2 20.2 %all-to-all-start.1 = ((bf16[16,4,4224]{2,1,0:T(4,128)(2,1)}), bf16[16,4,4224]{2,1,0:T(4,128)(2,1)}, u32[]{:S(2)}, u32[]{:S(2)}) async-start(bf16[16,4,4224]{2,1,0:T(4,128)(2,1)} %broadcast_in_dim.142), calls=%async_computation.1 | async-start | bytes 1081344 | tf_op jit(solution)/shard_map/all_to_all | solution.py:319
  65.7 21.1 %copy-start.6 = (s32[1,16]{1,0:T(1,128)S(1)}, s32[1,16]{1,0:T(1,128)}, u32[]{:S(2)}) copy-start(s32[1,16]{1,0:T(1,128)} %param.27) | copy-start | bytes 196
  69.3 54.3 %collective-permute-start = (bf16[512,4096]{1,0:T(8,128)(2,1)}, bf16[512,4096]{1,0:T(8,128)(2,1)}, u32[]{:S(2)}, u32[]{:S(2)}) collective-permute-start(bf16[512,4096]{1,0:T(8,128)(2,1)} %fusion.2.own_hbm), channel_id=1, source_target_pairs={{0,16},{16,0},{1,17},{17,1},{2,18},{18,2},{3,19},{19,3},{4,20},{20... | collective-permute-start | bytes 12582920 | tf_op jit(solution)/shard_map/ppermute | solution.py:337
  72.6 2.6 %copy-start = (bf16[84,64,512]{2,1,0:T(8,128)(2,1)S(1)}, bf16[84,64,512]{2,1,0:T(8,128)(2,1)}, u32[]{:S(2)}) copy-start(bf16[84,64,512]{2,1,0:T(8,128)(2,1)} %pool.1) | copy-start | bytes 16515076
  84.4 2.4 %copy-start.1 = (bf16[84,64,512]{2,1,0:T(8,128)(2,1)}, bf16[84,64,512]{2,1,0:T(8,128)(2,1)S(1)}, u32[]{:S(2)}) copy-start(bf16[84,64,512]{2,1,0:T(8,128)(2,1)S(1)} %take_pages.1.pages_hbm) | copy-start | bytes 16515076
  89.1 34.5 %collective-permute-start.1 = (f32[512,256]{1,0:T(8,128)S(1)}, f32[512,256]{1,0:T(8,128)S(1)}, u32[]{:S(2)}, u32[]{:S(2)}) collective-permute-start(f32[512,256]{1,0:T(8,128)S(1)} %pad_maximum_fusion.1.tab_own), channel_id=1, source_target_pairs={{0,16},{16,0},{1,17},{17,1},{2,18},{18,2},{3,19},{19,3},{4,20},{20... | collective-permute-start | bytes 1572872 | tf_op jit(solution)/shard_map/ppermute | solution.py:338
  123.6 12.5 %copy-start.2 = (bf16[512,512]{1,0:T(8,128)(2,1)S(1)}, bf16[512,512]{1,0:T(8,128)(2,1)}, u32[]{:S(2)}) copy-start(bf16[512,512]{1,0:T(8,128)(2,1)} %kv.1) | copy-start | bytes 1572868
  133.4 2.7 %collective-permute-start.2 = (bf16[320,1024]{1,0:T(8,128)(2,1)S(1)}, bf16[320,1024]{1,0:T(8,128)(2,1)S(1)}, u32[]{:S(2)}, u32[]{:S(2)}) collective-permute-start(bf16[320,1024]{1,0:T(8,128)(2,1)S(1)} %get-tuple-element.17), channel_id=1, source_target_pairs={{0,16},{16,0},{1,17},{17,1},{2,18},{18,2},{3,19},{19,3},{4,20},{20... | collective-permute-start | bytes 1966088 | tf_op jit(solution)/shard_map/ppermute | solution.py:372
  138.5 21.7 %all-to-all-start.2 = ((f32[16,4,2176]{2,1,0:T(4,128)}), f32[16,4,2176]{2,1,0:T(4,128)S(1)}, u32[]{:S(2)}, u32[]{:S(2)}) async-start(f32[16,4,2176]{2,1,0:T(4,128)} %shared.1), calls=%async_computation.2 | async-start | bytes 1114112 | tf_op jit(solution)/shard_map/all_to_all | solution.py:374
  145.6 14.6 %copy-start.3 = (s32[1,4]{1,0:T(1,128)S(1)}, s32[1,4]{1,0:T(1,128)}, u32[]{:S(2)}) copy-start(s32[1,4]{1,0:T(1,128)} %param.26) | copy-start | bytes 52
Sparse Core Ops, SparseCore 0:
  38.1 85.4 all-gather.1

commit v4 on v3

--- a/solution.py
+++ b/solution.py
@@ -26,7 +26,8 @@
 MODEL = 4096
 SPAN = 512
 STAT = QUERY_HEADS * HEAD_SIZE
-SPLIT = 512
+MAIN = 896
+SIDE = WIDE - MAIN
 HEADS_AT_ONCE = 2
 LOG2E = 1.4426950408889634
 
@@ -57,64 +58,98 @@
 def turned(values, tab):
     return values * tab[:, :HEAD_SIZE] + pltpu.roll(values, HEAD_SIZE // 2, 1) * tab[:, HEAD_SIZE:]
 
-def project_kernel(w_hbm, own_hbm, other_hbm, tab_own, tab_oth, q_own, kv_own, packed, w, x, w_sem, x_sem):
-    copies = [
+
+def project_kernel(
+    info, main_hbm, z0, up1, down1, up2, down2, up3, down3, up4, down4, own_hbm, other_hbm, tab_own, tab_oth,
+    q_own, kv_own, packed, main, side, x, main_sem, side_sem, x_sem,
+):
+    x_copies = [
         pltpu.make_async_copy(own_hbm.at[0:QROWS], x.at[0:QROWS], x_sem.at[0]),
         pltpu.make_async_copy(other_hbm.at[0:QROWS], x.at[QROWS : 2 * QROWS], x_sem.at[1]),
         pltpu.make_async_copy(own_hbm.at[QROWS:ROWS], x.at[2 * QROWS : 2 * QROWS + REC], x_sem.at[2]),
         pltpu.make_async_copy(other_hbm.at[QROWS:ROWS], x.at[2 * QROWS + REC : 2 * ROWS], x_sem.at[3]),
     ]
-    groups = [(0, SPLIT), (SPLIT, WIDE)]
-    pieces=[]
-    for k,(lo,hi) in enumerate(groups):
+    here = info[4]
+    side_copies = []
+    for i, (block, far) in enumerate(zip((z0, up1, down1, up2, down2, up3, down3), (0, -1, 1, -2, 2, -3, 3))):
+        z = (here + far) & 7
+        side_copies.append(pltpu.make_async_copy(block, side.at[z >> 2, :, :, z & 3], side_sem.at[i]))
+    z = (here + 4) & 7
+    side_copies.append(pltpu.make_async_copy(up4, side.at[z >> 2, 0:2, :, z & 3], side_sem.at[7]))
+    side_copies.append(pltpu.make_async_copy(down4, side.at[z >> 2, 2:4, :, z & 3], side_sem.at[8]))
+    groups = [(0, 512), (512, MAIN)]
+    main_copies = []
+    for k, (lo, hi) in enumerate(groups):
         for xi in range(4):
             for yi in range(4):
-                pieces.append(pltpu.make_async_copy(w_hbm.at[xi*4+yi, :, :, :, :, lo:hi], w.at[:, xi, :, :, yi, :, lo:hi], w_sem.at[k, xi*4+yi]))
-    for copy in copies[:2]: copy.start()
-    for copy in pieces: copy.start()
-    for copy in copies[2:]: copy.start()
-    for copy in copies[:2]: copy.wait()
-    wf = w.reshape(MODEL, WIDE)
-    for k,(lo,hi) in enumerate(groups):
-        for copy in pieces[k*16:(k+1)*16]: copy.wait()
-        for c0 in range(lo,hi,256):
-            cols=slice(c0,c0+256)
-            if c0<HALF:
-                acc = dot(x[0:2*QROWS, :], wf[:, cols])
-                for h in range(2):
-                    at = slice(c0 + h * HEAD_SIZE, c0 + (h + 1) * HEAD_SIZE)
-                    part = acc[:, h * HEAD_SIZE : (h + 1) * HEAD_SIZE]
-                    q_own[:, at] = turned(part[:QROWS], tab_own[0:QROWS,:]).astype(bf16)
-                    packed[0:QROWS, at] = turned(part[QROWS:], tab_oth[0:QROWS,:]).astype(bf16)
-            else:
-                for copy in copies[2:]: copy.wait()
-                acc = dot(x[...], wf[:, cols])
-                for own in (True, False):
-                    tab = (tab_own if own else tab_oth)[...]
-                    first = acc[0:QROWS] if own else acc[QROWS : 2 * QROWS]
-                    rest = acc[2 * QROWS : 2 * QROWS + REC] if own else acc[2 * QROWS + REC :]
-                    both = jnp.concatenate([first, rest], axis=0)
-                    keys = turned(both[:, :HEAD_SIZE], tab).astype(bf16)
-                    values = both[:, HEAD_SIZE:].astype(bf16)
-                    if own:
-                        kv_own[:, :HEAD_SIZE] = keys
-                        kv_own[:, HEAD_SIZE:] = values
-                    else:
-                        for b in range(4):
-                            rows = slice(b * 128, (b + 1) * 128)
-                            packed[QROWS:, b * 256 : b * 256 + 128] = keys[rows]
-                            packed[QROWS:, b * 256 + 128 : (b + 1) * 256] = values[rows]
-
-def project(weights, own, other, tab_own, tab_oth):
+                main_copies.append(
+                    pltpu.make_async_copy(
+                        main_hbm.at[xi * 4 + yi, :, :, :, :, lo:hi],
+                        main.at[:, xi, :, :, yi, :, lo:hi],
+                        main_sem.at[k, xi * 4 + yi],
+                    )
+                )
+    for copy in x_copies + side_copies + main_copies:
+        copy.start()
+    for copy in x_copies + side_copies:
+        copy.wait()
+
+    def store_queries(acc, first_head):
+        for h in range(acc.shape[1] // HEAD_SIZE):
+            at = slice((first_head + h) * HEAD_SIZE, (first_head + h + 1) * HEAD_SIZE)
+            part = acc[:, h * HEAD_SIZE : (h + 1) * HEAD_SIZE]
+            q_own[:, at] = turned(part[:QROWS], tab_own[0:QROWS, :]).astype(bf16)
+            packed[0:QROWS, at] = turned(part[QROWS:], tab_oth[0:QROWS, :]).astype(bf16)
+
+    side_flat = side.reshape(MODEL, SIDE)
+    acc = dot(x[...], side_flat[:, SIDE - 256 :])
+    for own in (True, False):
+        tab = (tab_own if own else tab_oth)[...]
+        first = acc[0:QROWS] if own else acc[QROWS : 2 * QROWS]
+        rest = acc[2 * QROWS : 2 * QROWS + REC] if own else acc[2 * QROWS + REC :]
+        both = jnp.concatenate([first, rest], axis=0)
+        keys = turned(both[:, :HEAD_SIZE], tab).astype(bf16)
+        values = both[:, HEAD_SIZE:].astype(bf16)
+        if own:
+            kv_own[:, :HEAD_SIZE] = keys
+            kv_own[:, HEAD_SIZE:] = values
+        else:
+            for b in range(4):
+                rows = slice(b * 128, (b + 1) * 128)
+                packed[QROWS:, b * 256 : b * 256 + 128] = keys[rows]
+                packed[QROWS:, b * 256 + 128 : (b + 1) * 256] = values[rows]
+    store_queries(dot(x[0 : 2 * QROWS, :], side_flat[:, : SIDE - 256]), MAIN // HEAD_SIZE)
+    main_flat = main.reshape(MODEL, MAIN)
+    for k, (lo, hi) in enumerate(groups):
+        for copy in main_copies[k * 16 : (k + 1) * 16]:
+            copy.wait()
+        for c0 in range(lo, hi, 256):
+            c1 = min(c0 + 256, hi)
+            store_queries(dot(x[0 : 2 * QROWS, :], main_flat[:, c0:c1]), c0 // HEAD_SIZE)
+
+
+def project(info, main, side, own, other, tab_own, tab_oth):
     return pl.pallas_call(
-        project_kernel, name="project",
-        out_shape=(jax.ShapeDtypeStruct((QROWS, HALF), bf16), jax.ShapeDtypeStruct((ROWS, 2 * HEAD_SIZE), bf16), jax.ShapeDtypeStruct((QROWS + 128, HALF), bf16)),
-        in_specs=[ANY, ANY, ANY, VMEM, VMEM], out_specs=(VMEM, VMEM, VMEM),
-        scratch_shapes=[pltpu.VMEM((2, 4, 2, 4, 4, 16, WIDE), bf16), pltpu.VMEM((2 * ROWS, MODEL), bf16),
-            pltpu.SemaphoreType.DMA((2, 16)), pltpu.SemaphoreType.DMA((4,))],
+        project_kernel,
+        name="project",
+        out_shape=(
+            jax.ShapeDtypeStruct((QROWS, HALF), bf16),
+            jax.ShapeDtypeStruct((ROWS, 2 * HEAD_SIZE), bf16),
+            jax.ShapeDtypeStruct((QROWS + 128, HALF), bf16),
+        ),
+        in_specs=[SMEM] + [ANY] * 12 + [VMEM, VMEM],
+        out_specs=(VMEM, VMEM, VMEM),
+        scratch_shapes=[
+            pltpu.VMEM((2, 4, 2, 4, 4, 16, MAIN), bf16),
+            pltpu.VMEM((2, 4, 2, 4, 4, 16, SIDE), bf16),
+            pltpu.VMEM((2 * ROWS, MODEL), bf16),
+            pltpu.SemaphoreType.DMA((2, 16)),
+            pltpu.SemaphoreType.DMA((9,)),
+            pltpu.SemaphoreType.DMA((4,)),
+        ],
         compiler_params=pltpu.CompilerParams(vmem_limit_bytes=40 << 20),
         cost_estimate=pl.CostEstimate(flops=6 * 10**9, bytes_accessed=20 * 10**6, transcendentals=0),
-    )(weights, own, other, tab_own, tab_oth)
+    )(info, main, *side, own, other, tab_own, tab_oth)
 
 
 def shared_kernel(info, q_own, packed, kv, out, qs):
@@ -140,11 +175,16 @@
         level = top * scale + jnp.log(total)
         for h in range(GROUP):
             head = s * GROUP + h
-            out[:, :, head * HEAD_SIZE : (head + 1) * HEAD_SIZE] = done[h*LINE:(h+1)*LINE].reshape(16,4,HEAD_SIZE)
+            out[:, :, head * HEAD_SIZE : (head + 1) * HEAD_SIZE] = done[h*LINE:(h+1)*LINE].reshape(16,4,HEAD_SIZE).astype(bf16)
             stats = jnp.where(lane == head, level[h*LINE:(h+1)*LINE], stats)
-    out[:, :, STAT:] = stats.reshape(16,4,HEAD_SIZE)
+    high = stats.astype(bf16).astype(f32)
+    left = stats - high
+    middle = left.astype(bf16).astype(f32)
+    low = left - middle
+    parts = high + pltpu.roll(middle, QUERY_HEADS, 1) + pltpu.roll(low, 2 * QUERY_HEADS, 1)
+    out[:, :, STAT:] = parts.reshape(16, 4, HEAD_SIZE).astype(bf16)
 def shared_attention(info, q_own, packed, kv):
-    return pl.pallas_call(shared_kernel, name="shared", out_shape=jax.ShapeDtypeStruct((16,4, STAT + 128), f32),
+    return pl.pallas_call(shared_kernel, name="shared", out_shape=jax.ShapeDtypeStruct((16, 4, STAT + 128), bf16),
         in_specs=[SMEM, VMEM, VMEM, VMEM], out_specs=VMEM, scratch_shapes=[pltpu.VMEM((2, LINE, HALF), bf16)],
         compiler_params=pltpu.CompilerParams(vmem_limit_bytes=16 << 20),
         cost_estimate=pl.CostEstimate(flops=3 * 10**8, bytes_accessed=10**6, transcendentals=10**6))(info, q_own, packed, kv)
@@ -259,11 +299,16 @@
     row = lax.broadcasted_iota(jnp.int32, (DEC, STAT + 128), 0)
     chosen = jnp.zeros((DEC, STAT + 128), f32)
     for r in range(DEC):
-        chosen = jnp.where(row == r, shared[groups[r]], chosen)
+        chosen = jnp.where(row == r, shared[groups[r]].astype(f32), chosen)
     for head in range(QUERY_HEADS):
         rows = slice(head*DEC,(head+1)*DEC)
         at = slice(head * HEAD_SIZE, (head + 1) * HEAD_SIZE)
-        far = chosen[:, STAT+head:STAT+head+1]
+        at_stat = STAT + head
+        far = (
+            chosen[:, at_stat : at_stat + 1]
+            + chosen[:, at_stat + QUERY_HEADS : at_stat + QUERY_HEADS + 1]
+            + chosen[:, at_stat + 2 * QUERY_HEADS : at_stat + 2 * QUERY_HEADS + 1]
+        )
         near = local_stat[rows, 0:1]
         top = jnp.maximum(far, near)
         far = jnp.exp(far - top); near = jnp.exp(near - top)
@@ -285,17 +330,41 @@
     return (widened * factor * gain.astype(f32)).astype(bf16)
 
 
-def gather_weights(w_query, key_value_weight):
+def along_z(step):
+    pairs = []
+    for i in range(256):
+        z = (i // 128) * 4 + (i // 4) % 4
+        to = (z + step) % 8
+        pairs.append((i, i % 128 - (i // 4) % 4 * 4 + (to // 4) * 128 + (to % 4) * 4))
+    return pairs
+
+
+def start_weights(w_query, key_value_weight):
     key_half = key_value_weight.reshape(16, 2, 2, HEAD_SIZE)
     halves = [
         jnp.concatenate([w_query[:, c * HALF : (c + 1) * HALF], key_half[:, 0, c], key_half[:, 1, c]], axis=1)
         for c in range(2)
     ]
     block = jnp.stack(halves, axis=0)
-    sent = jnp.broadcast_to(block[None, :, None], (2, 2, 4, 16, WIDE)).reshape(16, 16, WIDE)
+    sent = jnp.broadcast_to(block[None, :, None, :, :MAIN], (2, 2, 4, 16, MAIN)).reshape(16, 16, MAIN)
     column = lax.all_to_all(sent, ("zh", "c", "zl"), 0, 0, tiled=True)
-    whole = lax.all_gather(column.reshape(256, WIDE), ("x", "y"), axis=0, tiled=True)
-    return whole.reshape(16, 2, 2, 4, 16, WIDE)
+    rest, column = lax.optimization_barrier((block[:, :, MAIN:], column))
+    main = lax.all_gather(column.reshape(256, MAIN), ("x", "y"), axis=0, tiled=True)
+    main = main.reshape(16, 2, 2, 4, 16, MAIN)
+    sent = jnp.broadcast_to(rest[None, :, None], (4, 2, 4, 16, SIDE)).reshape(32, 16, SIDE)
+    plane = lax.all_to_all(sent, ("x", "c", "y"), 0, 0, tiled=True).reshape(4, 2, 4, 16, SIDE)
+    return main, plane
+
+
+def ring_along_z(plane):
+    side = [plane]
+    up = down = plane
+    for _ in range(3):
+        up = lax.ppermute(up, AXES, along_z(1))
+        down = lax.ppermute(down, AXES, along_z(-1))
+        side += [up, down]
+    side += [lax.ppermute(up[:2], AXES, along_z(1)), lax.ppermute(down[2:], AXES, along_z(-1))]
+    return side
 
 
 def on_device(
@@ -311,11 +380,13 @@
     request = rec_req[0]
     within = rec_off[0]
 
-    weights = gather_weights(w_query, key_value_weight)
+    main, plane = start_weights(w_query, key_value_weight)
 
     dec_pos = small_lookup(prefix_line, groups) + lengths
     parts = jnp.stack([dec_pos // 64, dec_pos % 64], axis=1).astype(bf16)
     extra = jnp.concatenate([x_dec, parts, jnp.zeros((DEC, 126), bf16)], axis=1)
+    plane, extra = lax.optimization_barrier((plane, extra))
+    side = ring_along_z(plane)
     line = lax.all_to_all(
         jnp.broadcast_to(extra[None], (16, DEC, MODEL + 128)), DP, 0, 0, tiled=True
     ).reshape(LINE, MODEL + 128)
@@ -362,13 +433,14 @@
     )
     bias_new = jnp.where(new_request[None, :] == eight[:, None], 0.0, negative_large)
     own_prefix = small_lookup(prefix_line, place[None])[0]
-    info = jnp.stack([core, own_prefix, pre_start[0], place]).astype(jnp.int32)
+    depth = lax.axis_index("zh") * 4 + lax.axis_index("zl")
+    info = jnp.stack([core, own_prefix, pre_start[0], place, depth]).astype(jnp.int32)
 
     pages = take_pages(slots, cache_pool)
-    weights, pages, bias_private, bias_new, info, slots = lax.optimization_barrier(
-        (weights, pages, bias_private, bias_new, info, slots)
+    main, pages, bias_private, bias_new, info = lax.optimization_barrier(
+        (main, pages, bias_private, bias_new, info)
     )
-    q_own, kv_own, packed = project(weights, normed, other, table, other_table)
+    q_own, kv_own, packed = project(info, main, side, normed, other, table, other_table)
     packed = lax.ppermute(packed, "c", swap)
     shared_part = shared_attention(info, q_own, packed, shared_kv)
     shared_part = lax.all_to_all(shared_part, DP, 0, 0, tiled=True)

time: 170 us -> 183 us (1.076)
  blocking collectives: 29 us -> 0 us
  starting transfers between devices: 16.2 us -> 45.1 us
  local copies, waits for them, and re-layouts: 11.1 us -> 19.5 us
  Pallas kernels: 31.4 us -> 36.4 us
  waiting for transfers between devices: 50 us -> 46 us
  other arithmetic: 15.8 us -> 19.5 us
    all_gather x1, waiting for transfers between devices: 33.5 us -> 0.01 us  [start_weights(): lax.all_gather(column.reshape(256, MAIN), ('x', 'y'), axis=0, tiled=True)]
    all_to_all x1 -> x0, blocking collectives: 29 us -> none  [gather_weights(): column = lax.all_to_all(sent, ('zh', 'c', 'zl'), 0, 0, tiled=True)]
    all_to_all x0 -> x2, waiting for transfers between devices: none -> 20.8 us  [the longest x1 13.2 us: start_weights(): column = lax.all_to_all(sent, ('zh', 'c', 'zl'), 0, 0, tiled=True)]
    all_to_all x0 -> x2, starting transfers between devices: none -> 17.3 us  [the longest x1 9.98 us: start_weights(): column = lax.all_to_all(sent, ('zh', 'c', 'zl'), 0, 0, tiled=True)]
    ppermute x0 -> x8, waiting for transfers between devices: none -> 15.7 us  [the longest x3 10.5 us: ring_along_z(): down = lax.ppermute(down, AXES, along_z(-1))]
    ppermute x0 -> x8, starting transfers between devices: none -> 9.01 us  [the longest x3 4.2 us: ring_along_z(): down = lax.ppermute(down, AXES, along_z(-1))]
    all_to_all x1, waiting for transfers between devices: 6.21 us -> 0.01 us  [on_device(): shared_part = lax.all_to_all(shared_part, DP, 0, 0, tiled=True)]
    pallas_call x1, Pallas kernels: 9.82 us -> 14.8 us  [project(): pl.pallas_call(project_kernel, name='project', out_shape=(jax.ShapeDtypeS...]
  transfers between devices with their start and end apart: 6 -> 16, of which waited for: 4 -> 8; matrix products, arithmetic and copies ran while one was open for 12% -> 15% of each run, Pallas kernels for 10% -> 10%
where the time goes in v4:
time: 183 us; the launch traced here: 182 us
  waiting for transfers between devices  46 us (25%)
  starting transfers between devices  45.1 us (25%)
  Pallas kernels  36.4 us (20%)
  local copies, waits for them, and re-layouts  19.5 us (11%)
  other arithmetic  19.5 us (11%)
  between operations  15.1 us (8%)
    pallas_call x1, Pallas kernels, project(): pl.pallas_call(project_kernel, name='project', out_shape=(jax.ShapeDtypeS...  14.8 us
    all_to_all x1, waiting for transfers between devices, start_weights(): column = lax.all_to_all(sent, ('zh', 'c', 'zl'), 0, 0, tiled=True)  13.2 us
    ppermute x3, waiting for transfers between devices, ring_along_z(): down = lax.ppermute(down, AXES, along_z(-1))  10.5 us
    all_to_all x1, starting transfers between devices, start_weights(): column = lax.all_to_all(sent, ('zh', 'c', 'zl'), 0, 0, tiled=True)  9.98 us
    pallas_call x1, Pallas kernels, take_pages(): pl.pallas_call(pages_kernel, name='take_pages', out_shape=jax.ShapeDtypeS...  9.17 us
    unnamed x44, local copies, waits for them, and re-layouts  9.14 us
    pallas_call x1, Pallas kernels, local_attention(): pl.pallas_call(local_kernel, name='local', out_shape=(jax.ShapeDtypeStruc...  8.42 us
    all_to_all x1, waiting for transfers between devices, on_device(): lax.all_to_all(jnp.broadcast_to(extra[None], (16, DEC, MODEL + 128)), DP,...  7.76 us
  transfers between devices with their start and end apart: 16, of which 8 were waited for; matrix products, arithmetic and copies ran while one was open for 15% of the time, Pallas kernels for 10%

profile of v4, /device:TPU:1, one launch (start us, length us, event | category | flops | bytes accessed | tf_op | source)
XLA Modules:
  0.0 182.0 jit_solution(1821771012502401163)
XLA Ops:
  7.2 0.9 reshape.305
  8.1 0.8 fusion.15
  8.9 0.8 broadcast_in_dim.129
  9.7 10.0 %all-to-all-start = ((bf16[16,16,896]{2,1,0:T(8,128)(2,1)}), bf16[16,16,896]{2,1,0:T(8,128)(2,1)S(1)}, u32[]{:S(2)}, u32[]{:S(2)}) async-start(bf16[16,16,896]{2,1,0:T(8,128)(2,1)} %bitcast.54), calls=%async_computation | async-start | bytes 917504 | tf_op jit(solution)/shard_map/all_to_all | solution.py:350
  19.8 13.2 %all-to-all-done = bf16[16,16,896]{2,1,0:T(8,128)(2,1)S(1)} async-done(((bf16[16,16,896]{2,1,0:T(8,128)(2,1)}), bf16[16,16,896]{2,1,0:T(8,128)(2,1)S(1)}, u32[]{:S(2)}, u32[]{:S(2)}) %all-to-all-start) | async-done | bytes 458784 | tf_op jit(solution)/shard_map/all_to_all | solution.py:350
  33.0 0.8 copy-done.9
  33.8 0.9 select_reduce_fusion.4
  34.6 0.8 broadcast_in_dim.145
  35.4 7.3 %all-to-all-start.1 = ((bf16[32,16,384]{2,1,0:T(8,128)(2,1)}), bf16[32,16,384]{2,1,0:T(8,128)(2,1)S(1)}, u32[]{:S(2)}, u32[]{:S(2)}) async-start(bf16[32,16,384]{2,1,0:T(8,128)(2,1)} %bitcast.17), calls=%async_computation.1 | async-start | bytes 786432 | tf_op jit(solution)/shard_map/all_to_all | solution.py:355
  44.3 0.9 concatenate.35
  45.1 7.6 %all-to-all-done.1 = bf16[32,16,384]{2,1,0:T(8,128)(2,1)S(1)} async-done(((bf16[32,16,384]{2,1,0:T(8,128)(2,1)}), bf16[32,16,384]{2,1,0:T(8,128)(2,1)S(1)}, u32[]{:S(2)}, u32[]{:S(2)}) %all-to-all-start.1) | async-done | bytes 393248 | tf_op jit(solution)/shard_map/all_to_all | solution.py:355
  52.7 1.0 broadcast_in_dim.149
  53.7 7.3 %all-to-all-start.2 = ((bf16[16,4,4224]{2,1,0:T(4,128)(2,1)}), bf16[16,4,4224]{2,1,0:T(4,128)(2,1)}, u32[]{:S(2)}, u32[]{:S(2)}) async-start(bf16[16,4,4224]{2,1,0:T(4,128)(2,1)} %broadcast_in_dim.149), calls=%async_computation.2 | async-start | bytes 1081344 | tf_op jit(solution)/shard_map/all_to_all | solution.py:390
  61.9 1.3 convert_element_type.27
  63.9 1.3 select_reduce_fusion.2
  65.2 1.3 add_reduce_fusion
  67.1 7.8 %all-to-all-done.2 = bf16[16,4,4224]{2,1,0:T(4,128)(2,1)} async-done(((bf16[16,4,4224]{2,1,0:T(4,128)(2,1)}), bf16[16,4,4224]{2,1,0:T(4,128)(2,1)}, u32[]{:S(2)}, u32[]{:S(2)}) %all-to-all-start.2) | async-done | bytes 540704 | tf_op jit(solution)/shard_map/all_to_all | solution.py:390
  74.8 1.2 reshape.312
  76.1 2.0 %fusion = f32[512]{0:T(512)S(1)} fusion(bf16[320,4096]{1,0:T(8,128)(2,1)S(1)} %copy-done.8, bf16[64,4096]{1,0:T(8,128)(2,1)S(1)} %slice.62, bf16[128,4096]{1,0:T(8,128)(2,1)} %param.16), kind=kLoop, calls=%fused_computation.2 | loop fusion | flops 16776704 | bytes 4196352 | tf_op jit(solution)/shard_map/reduce_sum | solution.py:329
  78.2 3.6 %fusion.2.own_hbm = bf16[512,4096]{1,0:T(8,128)(2,1)} fusion(f32[4096]{0:T(1024)} %convert_element_type.27, f32[512]{0:T(512)S(1)} %add_rsqrt_fusion, bf16[320,4096]{1,0:T(8,128)(2,1)S(1)} %copy-done.8, bf16[64,4096]{1,0:T(8,128)(2,1)S(1)} %slice.62, bf16[128,4096]{1,0:T(8,128)(2,1)} %param.16), kind=kLoop, calls=%fused_computation.4 | loop fusion | flops 18874368 | bytes 8407040 | tf_op jit(solution)/shard_map/convert_element_type | solution.py:330
  81.8 2.9 %collective-permute-start.8 = (bf16[512,4096]{1,0:T(8,128)(2,1)}, bf16[512,4096]{1,0:T(8,128)(2,1)}, u32[]{:S(2)}, u32[]{:S(2)}) collective-permute-start(bf16[512,4096]{1,0:T(8,128)(2,1)} %fusion.2.own_hbm), channel_id=1, source_target_pairs={{0,16},{16,0},{1,17},{17,1},{2,18},{18,2},{3,19},{19,3},{4,20},{20... | collective-permute-start | bytes 12582920 | tf_op jit(solution)/shard_map/ppermute | solution.py:408
  86.4 1.5 collective-permute-start
  87.9 0.8 reshape_squeeze.3
  88.7 8.5 %collective-permute-done.1.down1 = bf16[4,2,4,16,384]{4,3,2,1,0:T(8,128)(2,1)S(1)} collective-permute-done((bf16[4,2,4,16,384]{4,3,2,1,0:T(8,128)(2,1)S(1)}, bf16[4,2,4,16,384]{4,3,2,1,0:T(8,128)(2,1)S(1)}, u32[]{:S(2)}, u32[]{:S(2)}) %collective-permute-start.1) | collective-permute-done | bytes 393248 | tf_op jit(solution)/shard_map/ppermute | solution.py:364
  97.2 1.4 collective-permute-start.3
  99.5 0.7 pad_add_fusion.1.slots
  100.2 2.6 %copy-done = bf16[84,64,512]{2,1,0:T(8,128)(2,1)S(1)} copy-done((bf16[84,64,512]{2,1,0:T(8,128)(2,1)S(1)}, bf16[84,64,512]{2,1,0:T(8,128)(2,1)}, u32[]{:S(2)}) %copy-start) | copy-done | bytes 5505048
  102.8 9.2 %take_pages.1.pages_hbm = bf16[84,64,512]{2,1,0:T(8,128)(2,1)S(1)} custom-call(s32[84]{0:T(128)S(1)} %pad_add_fusion.1.slots, bf16[84,64,512]{2,1,0:T(8,128)(2,1)S(1)} %copy-done), custom_call_target="tpu_custom_call" | custom-call | bytes 22000000 | tf_op jit(solution)/shard_map/take_pages/pallas_call | solution.py:208
  112.0 2.4 %copy-done.1 = bf16[84,64,512]{2,1,0:T(8,128)(2,1)} copy-done((bf16[84,64,512]{2,1,0:T(8,128)(2,1)}, bf16[84,64,512]{2,1,0:T(8,128)(2,1)S(1)}, u32[]{:S(2)}) %copy-start.1) | copy-done | bytes 5505048
  114.4 2.7 %collective-permute-start.5 = (bf16[4,2,4,16,384]{4,3,2,1,0:T(8,128)(2,1)}, bf16[4,2,4,16,384]{4,3,2,1,0:T(8,128)(2,1)S(1)}, u32[]{:S(2)}, u32[]{:S(2)}) collective-permute-start(bf16[4,2,4,16,384]{4,3,2,1,0:T(8,128)(2,1)} %collective-permute-done.3.down2), channel_id=1, source_target_pairs={{0,140},{1,141},{2,142},{3,143},{4,0},{5,1},{6,2},{7,3},{8,4},{9,5... | collective-permute-start | bytes 1179656 | tf_op jit(solution)/shard_map/ppermute | solution.py:364
  117.4 1.0 multiply_cosine_fusion
  118.7 1.4 collective-permute-start.9
  120.1 1.3 fusion.11
  122.8 1.9 %collective-permute-done.5.down3 = bf16[4,2,4,16,384]{4,3,2,1,0:T(8,128)(2,1)S(1)} collective-permute-done((bf16[4,2,4,16,384]{4,3,2,1,0:T(8,128)(2,1)}, bf16[4,2,4,16,384]{4,3,2,1,0:T(8,128)(2,1)S(1)}, u32[]{:S(2)}, u32[]{:S(2)}) %collective-permute-start.5) | collective-permute-done | bytes 393248 | tf_op jit(solution)/shard_map/ppermute | solution.py:364
  125.5 3.3 %collective-permute-start.7 = (bf16[2,2,4,16,384]{4,3,2,1,0:T(8,128)(2,1)}, bf16[2,2,4,16,384]{4,3,2,1,0:T(8,128)(2,1)S(1)}, u32[]{:S(2)}, u32[]{:S(2)}) collective-permute-start(bf16[2,2,4,16,384]{4,3,2,1,0:T(8,128)(2,1)} %slice.61), channel_id=1, source_target_pairs={{0,140},{1,141},{2,142},{3,143},{4,0},{5,1},{6,2},{7,3},{8,4},{9,5... | collective-permute-start | bytes 589832 | tf_op jit(solution)/shard_map/ppermute | solution.py:366
  129.5 0.8 compare_select_fusion.bias_new
  130.3 1.5 collective-permute-done.7.down4
  131.7 3.8 %collective-permute-done.6.up4 = bf16[2,2,4,16,384]{4,3,2,1,0:T(8,128)(2,1)} collective-permute-done((bf16[2,2,4,16,384]{4,3,2,1,0:T(8,128)(2,1)}, bf16[2,2,4,16,384]{4,3,2,1,0:T(8,128)(2,1)}, u32[]{:S(2)}, u32[]{:S(2)}) %collective-permute-start.6) | collective-permute-done | bytes 196640 | tf_op jit(solution)/shard_map/ppermute | solution.py:366
  135.5 14.8 %project.1 = (bf16[192,1024]{1,0:T(8,128)(2,1)S(1)}, bf16[512,256]{1,0:T(8,128)(2,1)S(1)}, bf16[320,1024]{1,0:T(8,128)(2,1)S(1)}) custom-call(s32[5]{0:T(128)S(1)} %stack.31.info, bf16[16,2,2,4,16,896]{5,4,3,2,1,0:T(8,128)(2,1)} %bitcast.58, bf16[4,2,4,16,384]{4,3,2,1,0:T(8,128)(2,1)S(1)} %bitcast.49, ...), custom_call_target="tpu_custom_call" | custom-call | flops 6000000000 | bytes 20000000 | tf_op jit(solution)/shard_map/project/pallas_call | solution.py:132
  151.1 3.4 %collective-permute-start.10 = (bf16[320,1024]{1,0:T(8,128)(2,1)S(1)}, bf16[320,1024]{1,0:T(8,128)(2,1)S(1)}, u32[]{:S(2)}, u32[]{:S(2)}) collective-permute-start(bf16[320,1024]{1,0:T(8,128)(2,1)S(1)} %get-tuple-element.25), channel_id=1, source_target_pairs={{0,16},{16,0},{1,17},{17,1},{2,18},{18,2},{3,19},{19,3},{4,20},{20... | collective-permute-start | bytes 1966088 | tf_op jit(solution)/shard_map/ppermute | solution.py:444
  154.5 1.7 collective-permute-done.10.packed
  156.2 2.4 %shared.1 = bf16[16,4,2176]{2,1,0:T(4,128)(2,1)} custom-call(s32[5]{0:T(128)S(1)} %stack.31.info, bf16[192,1024]{1,0:T(8,128)(2,1)S(1)} %get-tuple-element.23.q_own, bf16[320,1024]{1,0:T(8,128)(2,1)S(1)} %collective-permute-done.10.packed, bf16[512,512]{1,0:T(8,128)(2,1)S(1)} %copy-done.3), custom_call_target="tpu_custom_call" | custom-call | flops 300000000 | bytes 1000000 | tf_op jit(solution)/shard_map/shared/pallas_call | solution.py:187
  158.7 0.7 copy-done.4
  159.4 3.8 %all-to-all-start.3 = ((bf16[16,4,2176]{2,1,0:T(4,128)(2,1)}), bf16[16,4,2176]{2,1,0:T(4,128)(2,1)S(1)}, u32[]{:S(2)}, u32[]{:S(2)}) async-start(bf16[16,4,2176]{2,1,0:T(4,128)(2,1)} %shared.1), calls=%async_computation.3 | async-start | bytes 557056 | tf_op jit(solution)/shard_map/all_to_all | solution.py:446
  163.2 1.0 copy-done.5
  164.2 0.9 copy-done.7
  165.1 8.4 %local.1 = (bf16[128,2048]{1,0:T(8,128)(2,1)}, f32[64,128]{1,0:T(8,128)S(1)}, f32[64,128]{1,0:T(8,128)S(1)}) custom-call(s32[5]{0:T(128)S(1)} %stack.31.info, bf16[192,1024]{1,0:T(8,128)(2,1)S(1)} %copy-done.5, bf16[512,256]{1,0:T(8,128)(2,1)S(1)} %copy-done.7, bf16[320,1024]{1,0:T(8,128)(2,1)S(1)} %collective-permute-done.10.packed, ...), custom_call_target="tpu_custom_call" | custom-call | flops 10000000000 | bytes 8000000 | tf_op jit(solution)/shard_map/local/pallas_call | solution.py:288
  173.6 1.5 finish.1
  (96 shorter events, 9.9 us)
Async XLA Ops:
  7.2 69.0 %copy-start.8 = (bf16[320,4096]{1,0:T(8,128)(2,1)S(1)}, bf16[320,4096]{1,0:T(8,128)(2,1)}, u32[]{:S(2)}) copy-start(bf16[320,4096]{1,0:T(8,128)(2,1)} %param.18) | copy-start | bytes 7864324
  9.7 23.2 %all-to-all-start = ((bf16[16,16,896]{2,1,0:T(8,128)(2,1)}), bf16[16,16,896]{2,1,0:T(8,128)(2,1)S(1)}, u32[]{:S(2)}, u32[]{:S(2)}) async-start(bf16[16,16,896]{2,1,0:T(8,128)(2,1)} %bitcast.54), calls=%async_computation | async-start | bytes 917504 | tf_op jit(solution)/shard_map/all_to_all | solution.py:350
  19.7 110.5 %all-gather.2.cloned.1.call-start = ((), (), s32[]{:S(2)}) async-start(), calls=%async_computation.4 | async-start | bytes 7798784 | tf_op jit(solution)/shard_map/all_gather | solution.py:352
  33.0 0.8 copy-start.9
  35.4 17.3 %all-to-all-start.1 = ((bf16[32,16,384]{2,1,0:T(8,128)(2,1)}), bf16[32,16,384]{2,1,0:T(8,128)(2,1)S(1)}, u32[]{:S(2)}, u32[]{:S(2)}) async-start(bf16[32,16,384]{2,1,0:T(8,128)(2,1)} %bitcast.17), calls=%async_computation.1 | async-start | bytes 786432 | tf_op jit(solution)/shard_map/all_to_all | solution.py:355
  53.7 21.1 %all-to-all-start.2 = ((bf16[16,4,4224]{2,1,0:T(4,128)(2,1)}), bf16[16,4,4224]{2,1,0:T(4,128)(2,1)}, u32[]{:S(2)}, u32[]{:S(2)}) async-start(bf16[16,4,4224]{2,1,0:T(4,128)(2,1)} %broadcast_in_dim.149), calls=%async_computation.2 | async-start | bytes 1081344 | tf_op jit(solution)/shard_map/all_to_all | solution.py:390
  61.9 5.2 %copy-start.10 = (s32[320]{0:T(512)}, s32[320]{0:T(512)S(1)}, u32[]{:S(2)}) copy-start(s32[320]{0:T(512)S(1)} %reduce.1) | copy-start | bytes 3844
  63.3 3.3 %copy-start.20 = (s32[68]{0:T(128)}, s32[68]{0:T(128)S(1)}, u32[]{:S(2)}) copy-start(s32[68]{0:T(128)S(1)} %convert_reduce_fusion) | copy-start | bytes 820
  63.9 2.6 %copy-start.16 = (s32[4]{0:T(128)}, s32[4]{0:T(128)S(1)}, u32[]{:S(2)}) copy-start(s32[4]{0:T(128)S(1)} %fusion.13) | copy-start | bytes 52
  76.0 8.7 %copy-start.11 = (s32[320]{0:T(512)S(1)}, s32[320]{0:T(512)}, u32[]{:S(2)}) copy-start(s32[320]{0:T(512)} %get-tuple-element.32) | copy-start | bytes 3844
  76.0 8.7 %copy-start.19 = (s32[1,16]{1,0:T(1,128)S(1)}, s32[1,16]{1,0:T(1,128)}, u32[]{:S(2)}) copy-start(s32[1,16]{1,0:T(1,128)} %param.27) | copy-start | bytes 196
  76.0 8.8 %copy-start.13 = (s32[1,4]{1,0:T(1,128)S(1)}, s32[1,4]{1,0:T(1,128)}, u32[]{:S(2)}) copy-start(s32[1,4]{1,0:T(1,128)} %param.24) | copy-start | bytes 52
  76.0 8.8 %copy-start.15 = (s32[68]{0:T(128)S(1)}, s32[68]{0:T(128)}, u32[]{:S(2)}) copy-start(s32[68]{0:T(128)} %broadcast_minimum_fusion) | copy-start | bytes 820
  76.0 8.8 %copy-start.17 = (s32[4]{0:T(128)S(1)}, s32[4]{0:T(128)}, u32[]{:S(2)}) copy-start(s32[4]{0:T(128)} %copy-done.16) | copy-start | bytes 52
  76.1 8.9 %copy-start.21 = (s32[68]{0:T(128)S(1)}, s32[68]{0:T(128)}, u32[]{:S(2)}) copy-start(s32[68]{0:T(128)} %copy-done.20) | copy-start | bytes 820
  76.1 8.9 %copy-start.12 = (s32[320]{0:T(512)S(1)}, s32[320]{0:T(512)}, u32[]{:S(2)}) copy-start(s32[320]{0:T(512)} %get-tuple-element.35) | copy-start | bytes 3844
  76.1 8.9 %copy-start.18 = (s32[320]{0:T(512)S(1)}, s32[320]{0:T(512)}, u32[]{:S(2)}) copy-start(s32[320]{0:T(512)} %get-tuple-element.34) | copy-start | bytes 3844
  81.8 53.8 %collective-permute-start.8 = (bf16[512,4096]{1,0:T(8,128)(2,1)}, bf16[512,4096]{1,0:T(8,128)(2,1)}, u32[]{:S(2)}, u32[]{:S(2)}) collective-permute-start(bf16[512,4096]{1,0:T(8,128)(2,1)} %fusion.2.own_hbm), channel_id=1, source_target_pairs={{0,16},{16,0},{1,17},{17,1},{2,18},{18,2},{3,19},{19,3},{4,20},{20... | collective-permute-start | bytes 12582920 | tf_op jit(solution)/shard_map/ppermute | solution.py:408
  86.3 28.1 %copy-start.14 = (s32[8]{0:T(128)}, s32[8]{0:T(128)S(1)}, u32[]{:S(2)}) copy-start(s32[8]{0:T(128)S(1)} %and_select_fusion.4) | copy-start | bytes 100
  86.3 10.9 %collective-permute-start.1 = (bf16[4,2,4,16,384]{4,3,2,1,0:T(8,128)(2,1)S(1)}, bf16[4,2,4,16,384]{4,3,2,1,0:T(8,128)(2,1)S(1)}, u32[]{:S(2)}, u32[]{:S(2)}) collective-permute-start(bf16[4,2,4,16,384]{4,3,2,1,0:T(8,128)(2,1)S(1)} %bitcast.47), channel_id=1, source_target_pairs={{0,140},{1,141},{2,142},{3,143},{4,0},{5,1},{6,2},{7,3},{8,4},{9,5... | collective-permute-start | bytes 1179656 | tf_op jit(solution)/shard_map/ppermute | solution.py:364
  86.4 12.3 %collective-permute-start = (bf16[4,2,4,16,384]{4,3,2,1,0:T(8,128)(2,1)S(1)}, bf16[4,2,4,16,384]{4,3,2,1,0:T(8,128)(2,1)S(1)}, u32[]{:S(2)}, u32[]{:S(2)}) collective-permute-start(bf16[4,2,4,16,384]{4,3,2,1,0:T(8,128)(2,1)S(1)} %bitcast.48), channel_id=1, source_target_pairs={{0,4},{1,5},{2,6},{3,7},{4,8},{5,9},{6,10},{7,11},{8,12},{9,13},{1... | collective-permute-start | bytes 1179656 | tf_op jit(solution)/shard_map/ppermute | solution.py:363
  97.2 17.2 %collective-permute-start.3 = (bf16[4,2,4,16,384]{4,3,2,1,0:T(8,128)(2,1)S(1)}, bf16[4,2,4,16,384]{4,3,2,1,0:T(8,128)(2,1)}, u32[]{:S(2)}, u32[]{:S(2)}) collective-permute-start(bf16[4,2,4,16,384]{4,3,2,1,0:T(8,128)(2,1)S(1)} %collective-permute-done.1.down1), channel_id=1, source_target_pairs={{0,140},{1,141},{2,142},{3,143},{4,0},{5,1},{6,2},{7,3},{8,4},{9,5... | collective-permute-start | bytes 1179656 | tf_op jit(solution)/shard_map/ppermute | solution.py:364
  98.6 18.5 %collective-permute-start.2 = (bf16[4,2,4,16,384]{4,3,2,1,0:T(8,128)(2,1)S(1)}, bf16[4,2,4,16,384]{4,3,2,1,0:T(8,128)(2,1)}, u32[]{:S(2)}, u32[]{:S(2)}) collective-permute-start(bf16[4,2,4,16,384]{4,3,2,1,0:T(8,128)(2,1)S(1)} %collective-permute-done.up1), channel_id=1, source_target_pairs={{0,4},{1,5},{2,6},{3,7},{4,8},{5,9},{6,10},{7,11},{8,12},{9,13},{1... | collective-permute-start | bytes 1179656 | tf_op jit(solution)/shard_map/ppermute | solution.py:363
  100.2 2.6 %copy-start = (bf16[84,64,512]{2,1,0:T(8,128)(2,1)S(1)}, bf16[84,64,512]{2,1,0:T(8,128)(2,1)}, u32[]{:S(2)}) copy-start(bf16[84,64,512]{2,1,0:T(8,128)(2,1)} %pool.1) | copy-start | bytes 16515076
  112.0 2.4 %copy-start.1 = (bf16[84,64,512]{2,1,0:T(8,128)(2,1)}, bf16[84,64,512]{2,1,0:T(8,128)(2,1)S(1)}, u32[]{:S(2)}) copy-start(bf16[84,64,512]{2,1,0:T(8,128)(2,1)S(1)} %take_pages.1.pages_hbm) | copy-start | bytes 16515076
  114.4 10.4 %collective-permute-start.5 = (bf16[4,2,4,16,384]{4,3,2,1,0:T(8,128)(2,1)}, bf16[4,2,4,16,384]{4,3,2,1,0:T(8,128)(2,1)S(1)}, u32[]{:S(2)}, u32[]{:S(2)}) collective-permute-start(bf16[4,2,4,16,384]{4,3,2,1,0:T(8,128)(2,1)} %collective-permute-done.3.down2), channel_id=1, source_target_pairs={{0,140},{1,141},{2,142},{3,143},{4,0},{5,1},{6,2},{7,3},{8,4},{9,5... | collective-permute-start | bytes 1179656 | tf_op jit(solution)/shard_map/ppermute | solution.py:364
  117.1 11.7 %collective-permute-start.4 = (bf16[4,2,4,16,384]{4,3,2,1,0:T(8,128)(2,1)}, bf16[4,2,4,16,384]{4,3,2,1,0:T(8,128)(2,1)S(1)}, u32[]{:S(2)}, u32[]{:S(2)}) collective-permute-start(bf16[4,2,4,16,384]{4,3,2,1,0:T(8,128)(2,1)} %collective-permute-done.2.up2), channel_id=1, source_target_pairs={{0,4},{1,5},{2,6},{3,7},{4,8},{5,9},{6,10},{7,11},{8,12},{9,13},{1... | collective-permute-start | bytes 1179656 | tf_op jit(solution)/shard_map/ppermute | solution.py:363
  118.7 16.9 %collective-permute-start.9 = (f32[512,256]{1,0:T(8,128)S(1)}, f32[512,256]{1,0:T(8,128)S(1)}, u32[]{:S(2)}, u32[]{:S(2)}) collective-permute-start(f32[512,256]{1,0:T(8,128)S(1)} %pad_maximum_fusion.1.tab_own), channel_id=1, source_target_pairs={{0,16},{16,0},{1,17},{17,1},{2,18},{18,2},{3,19},{19,3},{4,20},{20... | collective-permute-start | bytes 1572872 | tf_op jit(solution)/shard_map/ppermute | solution.py:409
  125.5 6.2 %collective-permute-start.7 = (bf16[2,2,4,16,384]{4,3,2,1,0:T(8,128)(2,1)}, bf16[2,2,4,16,384]{4,3,2,1,0:T(8,128)(2,1)S(1)}, u32[]{:S(2)}, u32[]{:S(2)}) collective-permute-start(bf16[2,2,4,16,384]{4,3,2,1,0:T(8,128)(2,1)} %slice.61), channel_id=1, source_target_pairs={{0,140},{1,141},{2,142},{3,143},{4,0},{5,1},{6,2},{7,3},{8,4},{9,5... | collective-permute-start | bytes 589832 | tf_op jit(solution)/shard_map/ppermute | solution.py:366
  129.5 6.0 %collective-permute-start.6 = (bf16[2,2,4,16,384]{4,3,2,1,0:T(8,128)(2,1)}, bf16[2,2,4,16,384]{4,3,2,1,0:T(8,128)(2,1)}, u32[]{:S(2)}, u32[]{:S(2)}) collective-permute-start(bf16[2,2,4,16,384]{4,3,2,1,0:T(8,128)(2,1)} %slice.60), channel_id=1, source_target_pairs={{0,4},{1,5},{2,6},{3,7},{4,8},{5,9},{6,10},{7,11},{8,12},{9,13},{1... | collective-permute-start | bytes 589832 | tf_op jit(solution)/shard_map/ppermute | solution.py:366
  130.3 26.0 %copy-start.3 = (bf16[512,512]{1,0:T(8,128)(2,1)S(1)}, bf16[512,512]{1,0:T(8,128)(2,1)}, u32[]{:S(2)}) copy-start(bf16[512,512]{1,0:T(8,128)(2,1)} %kv.1) | copy-start | bytes 1572868
  150.4 0.7 copy-start.6
  151.1 5.1 %collective-permute-start.10 = (bf16[320,1024]{1,0:T(8,128)(2,1)S(1)}, bf16[320,1024]{1,0:T(8,128)(2,1)S(1)}, u32[]{:S(2)}, u32[]{:S(2)}) collective-permute-start(bf16[320,1024]{1,0:T(8,128)(2,1)S(1)} %get-tuple-element.25), channel_id=1, source_target_pairs={{0,16},{16,0},{1,17},{17,1},{2,18},{18,2},{3,19},{19,3},{4,20},{20... | collective-permute-start | bytes 1966088 | tf_op jit(solution)/shard_map/ppermute | solution.py:444
  158.7 0.7 copy-start.4
  159.4 14.1 %all-to-all-start.3 = ((bf16[16,4,2176]{2,1,0:T(4,128)(2,1)}), bf16[16,4,2176]{2,1,0:T(4,128)(2,1)S(1)}, u32[]{:S(2)}, u32[]{:S(2)}) async-start(bf16[16,4,2176]{2,1,0:T(4,128)(2,1)} %shared.1), calls=%async_computation.3 | async-start | bytes 557056 | tf_op jit(solution)/shard_map/all_to_all | solution.py:446
  163.2 1.0 copy-start.5
  164.2 0.9 copy-start.7
  165.1 8.4 %copy-start.2 = (s32[1,4]{1,0:T(1,128)S(1)}, s32[1,4]{1,0:T(1,128)}, u32[]{:S(2)}) copy-start(s32[1,4]{1,0:T(1,128)} %param.26) | copy-start | bytes 52
Sparse Core Ops, SparseCore 0:
  33.9 73.0 all-gather.1

commit v5 on v4

--- a/solution.py
+++ b/solution.py
@@ -60,15 +60,9 @@
 
 
 def project_kernel(
-    info, main_hbm, z0, up1, down1, up2, down2, up3, down3, up4, down4, own_hbm, other_hbm, tab_own, tab_oth,
-    q_own, kv_own, packed, main, side, x, main_sem, side_sem, x_sem,
+    info, main_hbm, z0, up1, down1, up2, down2, up3, down3, up4, down4, x, tab_own, tab_oth,
+    q_own, kv_own, packed, main, side, main_sem, side_sem,
 ):
-    x_copies = [
-        pltpu.make_async_copy(own_hbm.at[0:QROWS], x.at[0:QROWS], x_sem.at[0]),
-        pltpu.make_async_copy(other_hbm.at[0:QROWS], x.at[QROWS : 2 * QROWS], x_sem.at[1]),
-        pltpu.make_async_copy(own_hbm.at[QROWS:ROWS], x.at[2 * QROWS : 2 * QROWS + REC], x_sem.at[2]),
-        pltpu.make_async_copy(other_hbm.at[QROWS:ROWS], x.at[2 * QROWS + REC : 2 * ROWS], x_sem.at[3]),
-    ]
     here = info[4]
     side_copies = []
     for i, (block, far) in enumerate(zip((z0, up1, down1, up2, down2, up3, down3), (0, -1, 1, -2, 2, -3, 3))):
@@ -89,9 +83,9 @@
                         main_sem.at[k, xi * 4 + yi],
                     )
                 )
-    for copy in x_copies + side_copies + main_copies:
+    for copy in side_copies + main_copies:
         copy.start()
-    for copy in x_copies + side_copies:
+    for copy in side_copies:
         copy.wait()
 
     def store_queries(acc, first_head):
@@ -128,7 +122,7 @@
             store_queries(dot(x[0 : 2 * QROWS, :], main_flat[:, c0:c1]), c0 // HEAD_SIZE)
 
 
-def project(info, main, side, own, other, tab_own, tab_oth):
+def project(info, main, side, rows, tab_own, tab_oth):
     return pl.pallas_call(
         project_kernel,
         name="project",
@@ -137,19 +131,17 @@
             jax.ShapeDtypeStruct((ROWS, 2 * HEAD_SIZE), bf16),
             jax.ShapeDtypeStruct((QROWS + 128, HALF), bf16),
         ),
-        in_specs=[SMEM] + [ANY] * 12 + [VMEM, VMEM],
+        in_specs=[SMEM] + [ANY] * 10 + [VMEM] * 3,
         out_specs=(VMEM, VMEM, VMEM),
         scratch_shapes=[
             pltpu.VMEM((2, 4, 2, 4, 4, 16, MAIN), bf16),
             pltpu.VMEM((2, 4, 2, 4, 4, 16, SIDE), bf16),
-            pltpu.VMEM((2 * ROWS, MODEL), bf16),
             pltpu.SemaphoreType.DMA((2, 16)),
             pltpu.SemaphoreType.DMA((9,)),
-            pltpu.SemaphoreType.DMA((4,)),
         ],
-        compiler_params=pltpu.CompilerParams(vmem_limit_bytes=40 << 20),
+        compiler_params=pltpu.CompilerParams(vmem_limit_bytes=46 << 20),
         cost_estimate=pl.CostEstimate(flops=6 * 10**9, bytes_accessed=20 * 10**6, transcendentals=0),
-    )(info, main, *side, own, other, tab_own, tab_oth)
+    )(info, main, *side, rows, tab_own, tab_oth)
 
 
 def shared_kernel(info, q_own, packed, kv, out, qs):
@@ -227,9 +219,11 @@
     cached = pltpu.make_async_copy(pages_hbm.at[:DEC_SLOTS], pages.at[:DEC_SLOTS], sems.at[1])
     cached.start()
     core = info[0]; start = info[2]; place = info[3]
-    qs[core] = q_own[...]
+    q_copy = pltpu.make_async_copy(q_own, qs.at[core], sems.at[2])
+    q_copy.start()
+    kv_copy = pltpu.make_async_copy(kv_own, ks.at[core], sems.at[3])
+    kv_copy.start()
     qs[1 - core] = packed[0:QROWS, :]
-    ks[core] = kv_own[...]
     for b in range(4):
         ks[1 - core, b * 128 : (b + 1) * 128, :] = packed[QROWS:, b * 256 : (b + 1) * 256]
     history = HIST_SLOTS * PAGE_TOKENS
@@ -241,6 +235,8 @@
     c2 = scale*LOG2E
     ones_h = jnp.ones((history, HEAD_SIZE), bf16)
     ones_n = jnp.ones((PRE, HEAD_SIZE), bf16)
+    q_copy.wait()
+    kv_copy.wait()
     old.wait()
     for s in range(KEY_VALUE_HEADS):
         old_keys = pages[DEC_SLOTS:, :, s * HEAD_SIZE : (s + 1) * HEAD_SIZE].reshape(history, HEAD_SIZE)
@@ -288,8 +284,8 @@
     return pl.pallas_call(
         local_kernel, name="local",
         out_shape=(jax.ShapeDtypeStruct((PRE, QUERY_HEADS * HEAD_SIZE), bf16), jax.ShapeDtypeStruct((64, HEAD_SIZE), f32), jax.ShapeDtypeStruct((64, HEAD_SIZE), f32)),
-        in_specs=[SMEM, VMEM, VMEM, VMEM, VMEM, VMEM, HBM], out_specs=(VMEM, VMEM, VMEM),
-        scratch_shapes=[pltpu.VMEM((2, QROWS, HALF), bf16), pltpu.VMEM((2, ROWS, 2 * HEAD_SIZE), bf16), pltpu.VMEM((DEC_SLOTS + HIST_SLOTS, PAGE_TOKENS, 4 * HEAD_SIZE), bf16), pltpu.SemaphoreType.DMA((2,))],
+        in_specs=[SMEM, ANY, ANY, VMEM, VMEM, VMEM, HBM], out_specs=(VMEM, VMEM, VMEM),
+        scratch_shapes=[pltpu.VMEM((2, QROWS, HALF), bf16), pltpu.VMEM((2, ROWS, 2 * HEAD_SIZE), bf16), pltpu.VMEM((DEC_SLOTS + HIST_SLOTS, PAGE_TOKENS, 4 * HEAD_SIZE), bf16), pltpu.SemaphoreType.DMA((4,))],
         compiler_params=pltpu.CompilerParams(vmem_limit_bytes=48 << 20),
         cost_estimate=pl.CostEstimate(flops=10**10, bytes_accessed=8 * 10**6, transcendentals=3 * 10**6),
     )(info, q_own, kv_own, packed, bias_private, bias_new, pages)
@@ -339,32 +335,27 @@
     return pairs
 
 
-def start_weights(w_query, key_value_weight):
+def weight_block(w_query, key_value_weight):
     key_half = key_value_weight.reshape(16, 2, 2, HEAD_SIZE)
     halves = [
         jnp.concatenate([w_query[:, c * HALF : (c + 1) * HALF], key_half[:, 0, c], key_half[:, 1, c]], axis=1)
         for c in range(2)
     ]
-    block = jnp.stack(halves, axis=0)
-    sent = jnp.broadcast_to(block[None, :, None, :, :MAIN], (2, 2, 4, 16, MAIN)).reshape(16, 16, MAIN)
-    column = lax.all_to_all(sent, ("zh", "c", "zl"), 0, 0, tiled=True)
-    rest, column = lax.optimization_barrier((block[:, :, MAIN:], column))
-    main = lax.all_gather(column.reshape(256, MAIN), ("x", "y"), axis=0, tiled=True)
-    main = main.reshape(16, 2, 2, 4, 16, MAIN)
-    sent = jnp.broadcast_to(rest[None, :, None], (4, 2, 4, 16, SIDE)).reshape(32, 16, SIDE)
-    plane = lax.all_to_all(sent, ("x", "c", "y"), 0, 0, tiled=True).reshape(4, 2, 4, 16, SIDE)
-    return main, plane
-
-
-def ring_along_z(plane):
-    side = [plane]
-    up = down = plane
-    for _ in range(3):
-        up = lax.ppermute(up, AXES, along_z(1))
-        down = lax.ppermute(down, AXES, along_z(-1))
-        side += [up, down]
-    side += [lax.ppermute(up[:2], AXES, along_z(1)), lax.ppermute(down[2:], AXES, along_z(-1))]
-    return side
+    return jnp.stack(halves, axis=0)
+
+
+def main_column(block):
+    sent = jnp.broadcast_to(block[None, :, None], (2, 2, 4, 16, MAIN)).reshape(16, 16, MAIN)
+    return lax.all_to_all(sent, ("zh", "c", "zl"), 0, 0, tiled=True)
+
+
+def side_plane(block):
+    sent = jnp.broadcast_to(block[None, :, None], (4, 2, 4, 16, SIDE)).reshape(32, 16, SIDE)
+    return lax.all_to_all(sent, ("x", "c", "y"), 0, 0, tiled=True).reshape(4, 2, 4, 16, SIDE)
+
+
+def ring_step(up, down):
+    return lax.ppermute(up, AXES, along_z(1)), lax.ppermute(down, AXES, along_z(-1))
 
 
 def on_device(
@@ -380,21 +371,48 @@
     request = rec_req[0]
     within = rec_off[0]
 
-    main, plane = start_weights(w_query, key_value_weight)
+    block = weight_block(w_query, key_value_weight)
+    column = main_column(block[:, :, :MAIN])
+    rest, column = lax.optimization_barrier((block[:, :, MAIN:], column))
+    main = lax.all_gather(column.reshape(256, MAIN), ("x", "y"), axis=0, tiled=True)
+    main = main.reshape(16, 2, 2, 4, 16, MAIN)
 
     dec_pos = small_lookup(prefix_line, groups) + lengths
     parts = jnp.stack([dec_pos // 64, dec_pos % 64], axis=1).astype(bf16)
     extra = jnp.concatenate([x_dec, parts, jnp.zeros((DEC, 126), bf16)], axis=1)
-    plane, extra = lax.optimization_barrier((plane, extra))
-    side = ring_along_z(plane)
+    normed_pre = rms_scaled(x_pre, norm_gain)
+    normed_rec = rms_scaled(rec_hidden, norm_gain)
+
+    counts = (lengths + PAGE_TOKENS - 1) // PAGE_TOKENS
+    ends = jnp.cumsum(counts)
+    firsts = ends - counts
+    slot = jnp.arange(DEC_SLOTS, dtype=jnp.int32)
+    slot_request = jnp.sum((slot[:, None] >= ends[None, :]).astype(jnp.int32), axis=1)
+    used = slot_request < DEC
+    slot_request = jnp.minimum(slot_request, DEC - 1)
+    slot_page = jnp.where(used, slot - small_lookup(firsts, slot_request), 0)
+    dec_pages = small_lookup(page_table.reshape(-1), slot_request * page_table.shape[1] + slot_page)
+    slots = jnp.concatenate([dec_pages, pre_table[0]], axis=0)
+
+    rest, normed_pre, slots = lax.optimization_barrier((rest, normed_pre, slots))
+    plane = side_plane(rest)
+    pages = take_pages(slots, cache_pool)
+    plane, pages = lax.optimization_barrier((plane, pages))
+    up1, down1 = ring_step(plane, plane)
+    up1, down1, extra = lax.optimization_barrier((up1, down1, extra))
     line = lax.all_to_all(
         jnp.broadcast_to(extra[None], (16, DEC, MODEL + 128)), DP, 0, 0, tiled=True
     ).reshape(LINE, MODEL + 128)
+    up2, down2 = ring_step(up1, down1)
+    up2, down2, line = lax.optimization_barrier((up2, down2, line))
     line_parts = line[:, MODEL : MODEL + 2].astype(jnp.int32)
     line_pos = line_parts[:, 0] * 64 + line_parts[:, 1]
-
-    rows = jnp.concatenate([x_pre, line[:, :MODEL], rec_hidden], axis=0)
-    normed = rms_scaled(rows, norm_gain)
+    normed_line = rms_scaled(line[:, :MODEL], norm_gain)
+    up3, down3 = ring_step(up2, down2)
+    up3, down3, normed_line = lax.optimization_barrier((up3, down3, normed_line))
+    up4, down4 = ring_step(up3[:2], down3[2:])
+    side = (plane, up1, down1, up2, down2, up3, down3, up4, down4)
+
     pre_pos = pre_start[0] + jnp.arange(PRE, dtype=jnp.int32)
     rec_pos = small_lookup(prefix_line, small_lookup(groups, request)) + within
     positions = jnp.concatenate([pre_pos, line_pos, rec_pos], axis=0)
@@ -405,19 +423,11 @@
     sines = jnp.sin(angles)
     table = jnp.concatenate([cosines, cosines, -sines, sines], axis=1)
     swap = [(0, 1), (1, 0)]
-    other = lax.ppermute(normed, "c", swap)
+    own = (normed_pre, normed_line, normed_rec)
+    other = [lax.ppermute(v, "c", swap) for v in own]
     other_table = lax.ppermute(table, "c", swap)
-
-    counts = (lengths + PAGE_TOKENS - 1) // PAGE_TOKENS
-    ends = jnp.cumsum(counts)
-    firsts = ends - counts
-    slot = jnp.arange(DEC_SLOTS, dtype=jnp.int32)
-    slot_request = jnp.sum((slot[:, None] >= ends[None, :]).astype(jnp.int32), axis=1)
-    used = slot_request < DEC
-    slot_request = jnp.minimum(slot_request, DEC - 1)
-    slot_page = jnp.where(used, slot - small_lookup(firsts, slot_request), 0)
-    dec_pages = small_lookup(page_table.reshape(-1), slot_request * page_table.shape[1] + slot_page)
-    slots = jnp.concatenate([dec_pages, pre_table[0]], axis=0)
+    rows = jnp.concatenate([own[0], own[1], other[0], other[1], own[2], other[2]], axis=0)
+
     key_pos = slot_page[:, None] * PAGE_TOKENS + jnp.arange(PAGE_TOKENS, dtype=jnp.int32)[None, :]
     valid = used[:, None] & (key_pos < small_lookup(lengths, slot_request)[:, None])
     rec_slot = small_lookup(firsts, request) + within // PAGE_TOKENS
@@ -436,11 +446,10 @@
     depth = lax.axis_index("zh") * 4 + lax.axis_index("zl")
     info = jnp.stack([core, own_prefix, pre_start[0], place, depth]).astype(jnp.int32)
 
-    pages = take_pages(slots, cache_pool)
-    main, pages, bias_private, bias_new, info = lax.optimization_barrier(
-        (main, pages, bias_private, bias_new, info)
+    main, rows, table, other_table, bias_private, bias_new, info = lax.optimization_barrier(
+        (main, rows, table, other_table, bias_private, bias_new, info)
     )
-    q_own, kv_own, packed = project(info, main, side, normed, other, table, other_table)
+    q_own, kv_own, packed = project(info, main, side, rows, table, other_table)
     packed = lax.ppermute(packed, "c", swap)
     shared_part = shared_attention(info, q_own, packed, shared_kv)
     shared_part = lax.all_to_all(shared_part, DP, 0, 0, tiled=True)

time: 183 us -> 197 us (1.077)
  local copies, waits for them, and re-layouts: 19.5 us -> 29.5 us
  starting transfers between devices: 45.1 us -> 48.4 us
    ppermute x9 -> x11, waiting for transfers between devices: 15.7 us -> 25.4 us  [the longest x4 18.8 us: ring_step(): lax.ppermute(up, AXES, along_z(1))]
    unnamed x44 -> x36, local copies, waits for them, and re-layouts: 9.14 us -> 17.4 us
    all_to_all x2, waiting for transfers between devices: 20.8 us -> 13.2 us  [the longest x1 13.2 us: main_column(): return lax.all_to_all(sent, ('zh', 'c', 'zl'), 0, 0, tiled=True)]
    ppermute x9 -> x11, starting transfers between devices: 12 us -> 16.4 us  [the longest x4 9 us: ring_step(): lax.ppermute(up, AXES, along_z(1))]
    unnamed x1 -> x2, other arithmetic: 0.7 us -> 4.4 us
    concatenate x0 -> x1, local copies, waits for them, and re-layouts: none -> 3.53 us  [on_device(): jnp.concatenate([own[0], own[1], other[0], other[1], own[2], other[2]], a...]
    all_to_all x1, starting transfers between devices: 3.75 us -> 7.17 us  [on_device(): shared_part = lax.all_to_all(shared_part, DP, 0, 0, tiled=True)]
    ppermute x1, starting transfers between devices: 3.39 us -> 1.03 us  [on_device(): packed = lax.ppermute(packed, 'c', swap)]
  transfers between devices with their start and end apart: 16 -> 18, of which waited for: 8 -> 10; matrix products, arithmetic and copies ran while one was open for 15% -> 18% of each run, Pallas kernels for 10% -> 9%
where the time goes in v5:
time: 197 us; the launch traced here: 196 us
  starting transfers between devices  48.4 us (25%)
  waiting for transfers between devices  46.8 us (24%)
  Pallas kernels  36.9 us (19%)
  local copies, waits for them, and re-layouts  29.5 us (15%)
  other arithmetic  19 us (10%)
  between operations  15 us (8%)
    ppermute x4, waiting for transfers between devices, ring_step(): lax.ppermute(up, AXES, along_z(1))  18.8 us
    unnamed x36, local copies, waits for them, and re-layouts  17.4 us
    pallas_call x1, Pallas kernels, project(): pl.pallas_call(project_kernel, name='project', out_shape=(jax.ShapeDtypeS...  15.3 us
    all_to_all x1, waiting for transfers between devices, main_column(): return lax.all_to_all(sent, ('zh', 'c', 'zl'), 0, 0, tiled=True)  13.2 us
    all_to_all x1, starting transfers between devices, main_column(): return lax.all_to_all(sent, ('zh', 'c', 'zl'), 0, 0, tiled=True)  9.98 us
    pallas_call x1, Pallas kernels, take_pages(): pl.pallas_call(pages_kernel, name='take_pages', out_shape=jax.ShapeDtypeS...  9.17 us
    ppermute x4, starting transfers between devices, ring_step(): lax.ppermute(up, AXES, along_z(1))  9 us
    pallas_call x1, Pallas kernels, local_attention(): pl.pallas_call(local_kernel, name='local', out_shape=(jax.ShapeDtypeStruc...  8.43 us
  transfers between devices with their start and end apart: 18, of which 10 were waited for; matrix products, arithmetic and copies ran while one was open for 18% of the time, Pallas kernels for 9%

profile of v5, /device:TPU:1, one launch (start us, length us, event | category | flops | bytes accessed | tf_op | source)
XLA Modules:
  0.0 195.9 jit_solution(10632348082031482439)
XLA Ops:
  7.2 0.9 reshape.321
  8.9 0.8 broadcast_in_dim.133
  9.7 10.0 %all-to-all-start = ((bf16[16,16,896]{2,1,0:T(8,128)(2,1)}), bf16[16,16,896]{2,1,0:T(8,128)(2,1)S(1)}, u32[]{:S(2)}, u32[]{:S(2)}) async-start(bf16[16,16,896]{2,1,0:T(8,128)(2,1)} %bitcast.54), calls=%async_computation | async-start | bytes 917504 | tf_op jit(solution)/shard_map/all_to_all | solution.py:349
  19.8 13.2 %all-to-all-done = bf16[16,16,896]{2,1,0:T(8,128)(2,1)S(1)} async-done(((bf16[16,16,896]{2,1,0:T(8,128)(2,1)}), bf16[16,16,896]{2,1,0:T(8,128)(2,1)S(1)}, u32[]{:S(2)}, u32[]{:S(2)}) %all-to-all-start) | async-done | bytes 458784 | tf_op jit(solution)/shard_map/all_to_all | solution.py:349
  35.2 0.9 select_reduce_fusion.5
  38.5 0.9 concatenate.34
  43.3 1.5 fusion.3
  44.8 2.6 %fusion.5 = bf16[128,4096]{1,0:T(8,128)(2,1)} fusion(bf16[128,4096]{1,0:T(8,128)(2,1)} %param.16, f32[4096]{0:T(1024)S(1)} %convert_element_type.40, f32[128]{0:T(128)S(1)} %add_rsqrt_fusion.2), kind=kLoop, calls=%fused_computation.9 | loop fusion | flops 2097152 | bytes 2114048 | tf_op jit(solution)/shard_map/convert_element_type | solution.py:326
  47.4 0.8 broadcast_in_dim.139
  48.2 7.3 %all-to-all-start.1 = ((bf16[32,16,384]{2,1,0:T(8,128)(2,1)}), bf16[32,16,384]{2,1,0:T(8,128)(2,1)S(1)}, u32[]{:S(2)}, u32[]{:S(2)}) async-start(bf16[32,16,384]{2,1,0:T(8,128)(2,1)} %bitcast.13), calls=%async_computation.1 | async-start | bytes 786432 | tf_op jit(solution)/shard_map/all_to_all | solution.py:354
  56.2 2.6 %copy-done = bf16[84,64,512]{2,1,0:T(8,128)(2,1)S(1)} copy-done((bf16[84,64,512]{2,1,0:T(8,128)(2,1)S(1)}, bf16[84,64,512]{2,1,0:T(8,128)(2,1)}, u32[]{:S(2)}) %copy-start) | copy-done | bytes 5505048
  58.8 9.2 %take_pages.1.pages_hbm = bf16[84,64,512]{2,1,0:T(8,128)(2,1)S(1)} custom-call(s32[84]{0:T(128)S(1)} %pad_add_fusion.1.slots, bf16[84,64,512]{2,1,0:T(8,128)(2,1)S(1)} %copy-done), custom_call_target="tpu_custom_call" | custom-call | bytes 22000000 | tf_op jit(solution)/shard_map/take_pages/pallas_call | solution.py:200
  68.0 2.3 %copy-done.1 = bf16[84,64,512]{2,1,0:T(8,128)(2,1)} copy-done((bf16[84,64,512]{2,1,0:T(8,128)(2,1)}, bf16[84,64,512]{2,1,0:T(8,128)(2,1)S(1)}, u32[]{:S(2)}) %copy-start.1) | copy-done | bytes 5505048
  70.4 2.9 %collective-permute-start = (bf16[4,2,4,16,384]{4,3,2,1,0:T(8,128)(2,1)S(1)}, bf16[4,2,4,16,384]{4,3,2,1,0:T(8,128)(2,1)S(1)}, u32[]{:S(2)}, u32[]{:S(2)}) collective-permute-start(bf16[4,2,4,16,384]{4,3,2,1,0:T(8,128)(2,1)S(1)} %bitcast.47), channel_id=1, source_target_pairs={{0,4},{1,5},{2,6},{3,7},{4,8},{5,9},{6,10},{7,11},{8,12},{9,13},{1... | collective-permute-start | bytes 1179656 | tf_op jit(solution)/shard_map/ppermute | solution.py:358
  73.3 8.8 %collective-permute-done.up1 = bf16[4,2,4,16,384]{4,3,2,1,0:T(8,128)(2,1)S(1)} collective-permute-done((bf16[4,2,4,16,384]{4,3,2,1,0:T(8,128)(2,1)S(1)}, bf16[4,2,4,16,384]{4,3,2,1,0:T(8,128)(2,1)S(1)}, u32[]{:S(2)}, u32[]{:S(2)}) %collective-permute-start) | collective-permute-done | bytes 393248 | tf_op jit(solution)/shard_map/ppermute | solution.py:358
  82.2 1.4 collective-permute-done.1.down1
  83.5 0.9 broadcast_in_dim.143
  84.5 5.9 %all-to-all-start.2 = ((bf16[16,4,4224]{2,1,0:T(4,128)(2,1)}), bf16[16,4,4224]{2,1,0:T(4,128)(2,1)S(1)}, u32[]{:S(2)}, u32[]{:S(2)}) async-start(bf16[16,4,4224]{2,1,0:T(4,128)(2,1)} %broadcast_in_dim.143), calls=%async_computation.2 | async-start | bytes 1081344 | tf_op jit(solution)/shard_map/all_to_all | solution.py:403
  90.7 1.8 collective-permute-start.6
  92.5 1.7 collective-permute-start.2
  94.1 1.0 collective-permute-start.3
  95.1 2.3 %constant_dynamic-update-slice_fusion.5 = bf16[1024,4096]{1,0:T(8,128)(2,1)} fusion(bf16[128,4096]{1,0:T(8,128)(2,1)} %fusion.5), kind=kLoop, calls=%fused_computation.47 | loop fusion | bytes 2097152
  97.4 6.4 %all-to-all-done.2 = bf16[16,4,4224]{2,1,0:T(4,128)(2,1)S(1)} async-done(((bf16[16,4,4224]{2,1,0:T(4,128)(2,1)}), bf16[16,4,4224]{2,1,0:T(4,128)(2,1)S(1)}, u32[]{:S(2)}, u32[]{:S(2)}) %all-to-all-start.2) | async-done | bytes 540704 | tf_op jit(solution)/shard_map/all_to_all | solution.py:403
  104.0 2.3 %collective-permute-done.2.up2 = bf16[4,2,4,16,384]{4,3,2,1,0:T(8,128)(2,1)S(1)} collective-permute-done((bf16[4,2,4,16,384]{4,3,2,1,0:T(8,128)(2,1)S(1)}, bf16[4,2,4,16,384]{4,3,2,1,0:T(8,128)(2,1)S(1)}, u32[]{:S(2)}, u32[]{:S(2)}) %collective-permute-start.2) | collective-permute-done | bytes 393248 | tf_op jit(solution)/shard_map/ppermute | solution.py:358
  106.3 3.3 %collective-permute-done.3.down2 = bf16[4,2,4,16,384]{4,3,2,1,0:T(8,128)(2,1)S(1)} collective-permute-done((bf16[4,2,4,16,384]{4,3,2,1,0:T(8,128)(2,1)S(1)}, bf16[4,2,4,16,384]{4,3,2,1,0:T(8,128)(2,1)S(1)}, u32[]{:S(2)}, u32[]{:S(2)}) %collective-permute-start.3) | collective-permute-done | bytes 393248 | tf_op jit(solution)/shard_map/ppermute | solution.py:358
  109.6 3.8 %collective-permute-start.4 = (bf16[4,2,4,16,384]{4,3,2,1,0:T(8,128)(2,1)S(1)}, bf16[4,2,4,16,384]{4,3,2,1,0:T(8,128)(2,1)S(1)}, u32[]{:S(2)}, u32[]{:S(2)}) collective-permute-start(bf16[4,2,4,16,384]{4,3,2,1,0:T(8,128)(2,1)S(1)} %collective-permute-done.2.up2), channel_id=1, source_target_pairs={{0,4},{1,5},{2,6},{3,7},{4,8},{5,9},{6,10},{7,11},{8,12},{9,13},{1... | collective-permute-start | bytes 1179656 | tf_op jit(solution)/shard_map/ppermute | solution.py:358
  113.8 6.6 %collective-permute-done.4.up3 = bf16[4,2,4,16,384]{4,3,2,1,0:T(8,128)(2,1)S(1)} collective-permute-done((bf16[4,2,4,16,384]{4,3,2,1,0:T(8,128)(2,1)S(1)}, bf16[4,2,4,16,384]{4,3,2,1,0:T(8,128)(2,1)S(1)}, u32[]{:S(2)}, u32[]{:S(2)}) %collective-permute-start.4) | collective-permute-done | bytes 393248 | tf_op jit(solution)/shard_map/ppermute | solution.py:358
  120.4 1.9 collective-permute-done.5.down3
  122.4 2.6 %collective-permute-start.7 = (bf16[64,4096]{1,0:T(8,128)(2,1)S(1)}, bf16[64,4096]{1,0:T(8,128)(2,1)S(1)}, u32[]{:S(2)}, u32[]{:S(2)}) collective-permute-start(bf16[64,4096]{1,0:T(8,128)(2,1)S(1)} %fusion.10), channel_id=1, source_target_pairs={{0,16},{16,0},{1,17},{17,1},{2,18},{18,2},{3,19},{19,3},{4,20},{20... | collective-permute-start | bytes 1572872 | tf_op jit(solution)/shard_map/ppermute | solution.py:427
  124.9 0.8 constant_dynamic-update-slice_fusion.4
  125.8 2.3 %constant_dynamic-update-slice_fusion.3 = bf16[1024,4096]{1,0:T(8,128)(2,1)} fusion(bf16[1024,4096]{1,0:T(8,128)(2,1)} %constant_dynamic-update-slice_fusion.4, bf16[128,4096]{1,0:T(8,128)(2,1)} %collective-permute-done.6), kind=kLoop, calls=%fused_computation.45 | loop fusion | bytes 2097152
  128.1 0.8 constant_dynamic-update-slice_fusion.2
  128.9 3.7 %constant_dynamic-update-slice_fusion.1 = (bf16[1024,4096]{1,0:T(8,128)(2,1)}, bf16[320,4096]{1,0:T(8,128)(2,1)}) fusion(bf16[1024,4096]{1,0:T(8,128)(2,1)} %constant_dynamic-update-slice_fusion.2, f32[4096]{0:T(1024)S(1)} %convert_element_type.40, f32[320]{0:T(512)S(1)} %add_rsqrt_fusion, bf16[320,4096]{1,0:T(8,128)(2,1)S(1)} %copy-done.13), kind=kLoop, calls=%fused_computation.43 | loop fusion | flops 5242880 | bytes 7881984
  134.2 1.0 multiply_cosine_fusion
  139.4 2.0 %collective-permute-start.11 = (bf16[2,2,4,16,384]{4,3,2,1,0:T(8,128)(2,1)}, bf16[2,2,4,16,384]{4,3,2,1,0:T(8,128)(2,1)}, u32[]{:S(2)}, u32[]{:S(2)}) collective-permute-start(bf16[2,2,4,16,384]{4,3,2,1,0:T(8,128)(2,1)} %slice.55), channel_id=1, source_target_pairs={{0,140},{1,141},{2,142},{3,143},{4,0},{5,1},{6,2},{7,3},{8,4},{9,5... | collective-permute-start | bytes 589832 | tf_op jit(solution)/shard_map/ppermute | solution.py:358
  141.4 3.5 %constant_dynamic-update-slice_fusion.x = bf16[1024,4096]{1,0:T(8,128)(2,1)} fusion(bf16[1024,4096]{1,0:T(8,128)(2,1)} %get-tuple-element.66, bf16[320,4096]{1,0:T(8,128)(2,1)} %collective-permute-done.8), kind=kLoop, calls=%fused_computation.42 | loop fusion | bytes 5242880 | tf_op jit(solution)/shard_map/concatenate | solution.py:429
  144.9 1.0 collective-permute-done.10.up4
  146.0 1.0 copy-done.5
  147.0 1.0 copy-done.7
  148.0 15.3 %project.1 = (bf16[192,1024]{1,0:T(8,128)(2,1)S(1)}, bf16[512,256]{1,0:T(8,128)(2,1)S(1)}, bf16[320,1024]{1,0:T(8,128)(2,1)S(1)}) custom-call(s32[5]{0:T(128)S(1)} %stack.31.info, bf16[16,2,2,4,16,896]{5,4,3,2,1,0:T(8,128)(2,1)} %bitcast.58, bf16[4,2,4,16,384]{4,3,2,1,0:T(8,128)(2,1)S(1)} %bitcast.49, ...), custom_call_target="tpu_custom_call" | custom-call | flops 6000000000 | bytes 20000000 | tf_op jit(solution)/shard_map/project/pallas_call | solution.py:126
  164.0 1.0 collective-permute-start.12
  165.0 1.7 collective-permute-done.12.packed
  166.8 2.4 %shared.1 = bf16[16,4,2176]{2,1,0:T(4,128)(2,1)} custom-call(s32[5]{0:T(128)S(1)} %stack.31.info, bf16[192,1024]{1,0:T(8,128)(2,1)S(1)} %get-tuple-element.51.q_own, bf16[320,1024]{1,0:T(8,128)(2,1)S(1)} %collective-permute-done.12.packed, bf16[512,512]{1,0:T(8,128)(2,1)S(1)} %copy-done.3), custom_call_target="tpu_custom_call" | custom-call | flops 300000000 | bytes 1000000 | tf_op jit(solution)/shard_map/shared/pallas_call | solution.py:179
  169.9 7.2 %all-to-all-start.3 = ((bf16[16,4,2176]{2,1,0:T(4,128)(2,1)}), bf16[16,4,2176]{2,1,0:T(4,128)(2,1)S(1)}, u32[]{:S(2)}, u32[]{:S(2)}) async-start(bf16[16,4,2176]{2,1,0:T(4,128)(2,1)} %shared.1), calls=%async_computation.3 | async-start | bytes 557056 | tf_op jit(solution)/shard_map/all_to_all | solution.py:455
  177.1 1.0 copy-done.9
  178.1 0.9 copy-done.11
  179.1 8.4 %local.1 = (bf16[128,2048]{1,0:T(8,128)(2,1)}, f32[64,128]{1,0:T(8,128)S(1)}, f32[64,128]{1,0:T(8,128)S(1)}) custom-call(s32[5]{0:T(128)S(1)} %stack.31.info, bf16[192,1024]{1,0:T(8,128)(2,1)S(1)} %copy-done.9, bf16[512,256]{1,0:T(8,128)(2,1)S(1)} %copy-done.11, bf16[320,1024]{1,0:T(8,128)(2,1)S(1)} %collective-permute-done.12.packed, ...), custom_call_target="tpu_custom_call" | custom-call | flops 10000000000 | bytes 8000000 | tf_op jit(solution)/shard_map/local/pallas_call | solution.py:284
  187.5 1.5 finish.1
  (98 shorter events, 17.6 us)
Async XLA Ops:
  7.2 48.3 %copy-start.15 = (s32[1,16]{1,0:T(1,128)S(1)}, s32[1,16]{1,0:T(1,128)}, u32[]{:S(2)}) copy-start(s32[1,16]{1,0:T(1,128)} %param.27) | copy-start | bytes 196
  7.2 48.4 %copy-start.12 = (bf16[320,4096]{1,0:T(8,128)(2,1)S(1)}, bf16[320,4096]{1,0:T(8,128)(2,1)}, u32[]{:S(2)}) copy-start(bf16[320,4096]{1,0:T(8,128)(2,1)} %param.18) | copy-start | bytes 7864324
  9.7 23.2 %all-to-all-start = ((bf16[16,16,896]{2,1,0:T(8,128)(2,1)}), bf16[16,16,896]{2,1,0:T(8,128)(2,1)S(1)}, u32[]{:S(2)}, u32[]{:S(2)}) async-start(bf16[16,16,896]{2,1,0:T(8,128)(2,1)} %bitcast.54), calls=%async_computation | async-start | bytes 917504 | tf_op jit(solution)/shard_map/all_to_all | solution.py:349
  19.7 125.2 %all-gather.2.cloned.1.call-start = ((), (), s32[]{:S(2)}) async-start(), calls=%async_computation.4 | async-start | bytes 7798784 | tf_op jit(solution)/shard_map/all_gather | solution.py:377
  33.0 0.8 copy-start.14
  48.2 22.2 %all-to-all-start.1 = ((bf16[32,16,384]{2,1,0:T(8,128)(2,1)}), bf16[32,16,384]{2,1,0:T(8,128)(2,1)S(1)}, u32[]{:S(2)}, u32[]{:S(2)}) async-start(bf16[32,16,384]{2,1,0:T(8,128)(2,1)} %bitcast.13), calls=%async_computation.1 | async-start | bytes 786432 | tf_op jit(solution)/shard_map/all_to_all | solution.py:354
  56.2 2.6 %copy-start = (bf16[84,64,512]{2,1,0:T(8,128)(2,1)S(1)}, bf16[84,64,512]{2,1,0:T(8,128)(2,1)}, u32[]{:S(2)}) copy-start(bf16[84,64,512]{2,1,0:T(8,128)(2,1)} %pool.1) | copy-start | bytes 16515076
  68.0 2.3 %copy-start.1 = (bf16[84,64,512]{2,1,0:T(8,128)(2,1)}, bf16[84,64,512]{2,1,0:T(8,128)(2,1)S(1)}, u32[]{:S(2)}) copy-start(bf16[84,64,512]{2,1,0:T(8,128)(2,1)S(1)} %take_pages.1.pages_hbm) | copy-start | bytes 16515076
  70.4 11.8 %collective-permute-start = (bf16[4,2,4,16,384]{4,3,2,1,0:T(8,128)(2,1)S(1)}, bf16[4,2,4,16,384]{4,3,2,1,0:T(8,128)(2,1)S(1)}, u32[]{:S(2)}, u32[]{:S(2)}) collective-permute-start(bf16[4,2,4,16,384]{4,3,2,1,0:T(8,128)(2,1)S(1)} %bitcast.47), channel_id=1, source_target_pairs={{0,4},{1,5},{2,6},{3,7},{4,8},{5,9},{6,10},{7,11},{8,12},{9,13},{1... | collective-permute-start | bytes 1179656 | tf_op jit(solution)/shard_map/ppermute | solution.py:358
  73.3 10.2 %collective-permute-start.1 = (bf16[4,2,4,16,384]{4,3,2,1,0:T(8,128)(2,1)S(1)}, bf16[4,2,4,16,384]{4,3,2,1,0:T(8,128)(2,1)S(1)}, u32[]{:S(2)}, u32[]{:S(2)}) collective-permute-start(bf16[4,2,4,16,384]{4,3,2,1,0:T(8,128)(2,1)S(1)} %bitcast.48), channel_id=1, source_target_pairs={{0,140},{1,141},{2,142},{3,143},{4,0},{5,1},{6,2},{7,3},{8,4},{9,5... | collective-permute-start | bytes 1179656 | tf_op jit(solution)/shard_map/ppermute | solution.py:358
  84.5 19.4 %all-to-all-start.2 = ((bf16[16,4,4224]{2,1,0:T(4,128)(2,1)}), bf16[16,4,4224]{2,1,0:T(4,128)(2,1)S(1)}, u32[]{:S(2)}, u32[]{:S(2)}) async-start(bf16[16,4,4224]{2,1,0:T(4,128)(2,1)} %broadcast_in_dim.143), calls=%async_computation.2 | async-start | bytes 1081344 | tf_op jit(solution)/shard_map/all_to_all | solution.py:403
  90.7 35.1 %collective-permute-start.6 = (bf16[128,4096]{1,0:T(8,128)(2,1)}, bf16[128,4096]{1,0:T(8,128)(2,1)}, u32[]{:S(2)}, u32[]{:S(2)}) collective-permute-start(bf16[128,4096]{1,0:T(8,128)(2,1)} %fusion.5), channel_id=1, source_target_pairs={{0,16},{16,0},{1,17},{17,1},{2,18},{18,2},{3,19},{19,3},{4,20},{20... | collective-permute-start | bytes 3145736 | tf_op jit(solution)/shard_map/ppermute | solution.py:427
  92.5 13.8 %collective-permute-start.2 = (bf16[4,2,4,16,384]{4,3,2,1,0:T(8,128)(2,1)S(1)}, bf16[4,2,4,16,384]{4,3,2,1,0:T(8,128)(2,1)S(1)}, u32[]{:S(2)}, u32[]{:S(2)}) collective-permute-start(bf16[4,2,4,16,384]{4,3,2,1,0:T(8,128)(2,1)S(1)} %collective-permute-done.up1), channel_id=1, source_target_pairs={{0,4},{1,5},{2,6},{3,7},{4,8},{5,9},{6,10},{7,11},{8,12},{9,13},{1... | collective-permute-start | bytes 1179656 | tf_op jit(solution)/shard_map/ppermute | solution.py:358
  94.1 15.5 %collective-permute-start.3 = (bf16[4,2,4,16,384]{4,3,2,1,0:T(8,128)(2,1)S(1)}, bf16[4,2,4,16,384]{4,3,2,1,0:T(8,128)(2,1)S(1)}, u32[]{:S(2)}, u32[]{:S(2)}) collective-permute-start(bf16[4,2,4,16,384]{4,3,2,1,0:T(8,128)(2,1)S(1)} %collective-permute-done.1.down1), channel_id=1, source_target_pairs={{0,140},{1,141},{2,142},{3,143},{4,0},{5,1},{6,2},{7,3},{8,4},{9,5... | collective-permute-start | bytes 1179656 | tf_op jit(solution)/shard_map/ppermute | solution.py:358
  104.0 24.9 %copy-start.13 = (bf16[320,4096]{1,0:T(8,128)(2,1)S(1)}, bf16[320,4096]{1,0:T(8,128)(2,1)}, u32[]{:S(2)}) copy-start(bf16[320,4096]{1,0:T(8,128)(2,1)} %param.18) | copy-start | bytes 7864324
  106.3 26.3 %copy-start.4 = (bf16[4,2,4,16,384]{4,3,2,1,0:T(8,128)(2,1)}, bf16[4,2,4,16,384]{4,3,2,1,0:T(8,128)(2,1)S(1)}, u32[]{:S(2)}) copy-start(bf16[4,2,4,16,384]{4,3,2,1,0:T(8,128)(2,1)S(1)} %collective-permute-done.2.up2) | copy-start | bytes 1179652
  109.6 23.0 %copy-start.6 = (bf16[4,2,4,16,384]{4,3,2,1,0:T(8,128)(2,1)}, bf16[4,2,4,16,384]{4,3,2,1,0:T(8,128)(2,1)S(1)}, u32[]{:S(2)}) copy-start(bf16[4,2,4,16,384]{4,3,2,1,0:T(8,128)(2,1)S(1)} %collective-permute-done.3.down2) | copy-start | bytes 1179652
  109.6 10.8 %collective-permute-start.4 = (bf16[4,2,4,16,384]{4,3,2,1,0:T(8,128)(2,1)S(1)}, bf16[4,2,4,16,384]{4,3,2,1,0:T(8,128)(2,1)S(1)}, u32[]{:S(2)}, u32[]{:S(2)}) collective-permute-start(bf16[4,2,4,16,384]{4,3,2,1,0:T(8,128)(2,1)S(1)} %collective-permute-done.2.up2), channel_id=1, source_target_pairs={{0,4},{1,5},{2,6},{3,7},{4,8},{5,9},{6,10},{7,11},{8,12},{9,13},{1... | collective-permute-start | bytes 1179656 | tf_op jit(solution)/shard_map/ppermute | solution.py:358
  113.4 9.0 %collective-permute-start.5 = (bf16[4,2,4,16,384]{4,3,2,1,0:T(8,128)(2,1)S(1)}, bf16[4,2,4,16,384]{4,3,2,1,0:T(8,128)(2,1)S(1)}, u32[]{:S(2)}, u32[]{:S(2)}) collective-permute-start(bf16[4,2,4,16,384]{4,3,2,1,0:T(8,128)(2,1)S(1)} %collective-permute-done.3.down2), channel_id=1, source_target_pairs={{0,140},{1,141},{2,142},{3,143},{4,0},{5,1},{6,2},{7,3},{8,4},{9,5... | collective-permute-start | bytes 1179656 | tf_op jit(solution)/shard_map/ppermute | solution.py:358
  122.4 5.7 %collective-permute-start.7 = (bf16[64,4096]{1,0:T(8,128)(2,1)S(1)}, bf16[64,4096]{1,0:T(8,128)(2,1)S(1)}, u32[]{:S(2)}, u32[]{:S(2)}) collective-permute-start(bf16[64,4096]{1,0:T(8,128)(2,1)S(1)} %fusion.10), channel_id=1, source_target_pairs={{0,16},{16,0},{1,17},{17,1},{2,18},{18,2},{3,19},{19,3},{4,20},{20... | collective-permute-start | bytes 1572872 | tf_op jit(solution)/shard_map/ppermute | solution.py:427
  132.6 8.8 %collective-permute-start.8 = (bf16[320,4096]{1,0:T(8,128)(2,1)}, bf16[320,4096]{1,0:T(8,128)(2,1)}, u32[]{:S(2)}, u32[]{:S(2)}) collective-permute-start(bf16[320,4096]{1,0:T(8,128)(2,1)} %get-tuple-element.67), channel_id=1, source_target_pairs={{0,16},{16,0},{1,17},{17,1},{2,18},{18,2},{3,19},{19,3},{4,20},{20... | collective-permute-start | bytes 7864328 | tf_op jit(solution)/shard_map/ppermute | solution.py:427
  135.5 9.5 %collective-permute-start.9 = (f32[512,256]{1,0:T(8,128)S(1)}, f32[512,256]{1,0:T(8,128)S(1)}, u32[]{:S(2)}, u32[]{:S(2)}) collective-permute-start(f32[512,256]{1,0:T(8,128)S(1)} %pad_maximum_fusion.tab_own), channel_id=1, source_target_pairs={{0,16},{16,0},{1,17},{17,1},{2,18},{18,2},{3,19},{19,3},{4,20},{20... | collective-permute-start | bytes 1572872 | tf_op jit(solution)/shard_map/ppermute | solution.py:428
  138.0 7.9 %collective-permute-start.10 = (bf16[2,2,4,16,384]{4,3,2,1,0:T(8,128)(2,1)}, bf16[2,2,4,16,384]{4,3,2,1,0:T(8,128)(2,1)S(1)}, u32[]{:S(2)}, u32[]{:S(2)}) collective-permute-start(bf16[2,2,4,16,384]{4,3,2,1,0:T(8,128)(2,1)} %slice.54), channel_id=1, source_target_pairs={{0,4},{1,5},{2,6},{3,7},{4,8},{5,9},{6,10},{7,11},{8,12},{9,13},{1... | collective-permute-start | bytes 589832 | tf_op jit(solution)/shard_map/ppermute | solution.py:358
  139.4 6.6 %collective-permute-start.11 = (bf16[2,2,4,16,384]{4,3,2,1,0:T(8,128)(2,1)}, bf16[2,2,4,16,384]{4,3,2,1,0:T(8,128)(2,1)}, u32[]{:S(2)}, u32[]{:S(2)}) collective-permute-start(bf16[2,2,4,16,384]{4,3,2,1,0:T(8,128)(2,1)} %slice.55), channel_id=1, source_target_pairs={{0,140},{1,141},{2,142},{3,143},{4,0},{5,1},{6,2},{7,3},{8,4},{9,5... | collective-permute-start | bytes 589832 | tf_op jit(solution)/shard_map/ppermute | solution.py:358
  144.9 21.8 %copy-start.3 = (bf16[512,512]{1,0:T(8,128)(2,1)S(1)}, bf16[512,512]{1,0:T(8,128)(2,1)}, u32[]{:S(2)}) copy-start(bf16[512,512]{1,0:T(8,128)(2,1)} %kv.1) | copy-start | bytes 1572868
  146.0 1.0 copy-start.5
  147.0 1.0 copy-start.7
  163.3 0.7 copy-start.10
  164.0 2.8 %collective-permute-start.12 = (bf16[320,1024]{1,0:T(8,128)(2,1)S(1)}, bf16[320,1024]{1,0:T(8,128)(2,1)S(1)}, u32[]{:S(2)}, u32[]{:S(2)}) collective-permute-start(bf16[320,1024]{1,0:T(8,128)(2,1)S(1)} %get-tuple-element.53), channel_id=1, source_target_pairs={{0,16},{16,0},{1,17},{17,1},{2,18},{18,2},{3,19},{19,3},{4,20},{20... | collective-permute-start | bytes 1966088 | tf_op jit(solution)/shard_map/ppermute | solution.py:453
  169.2 0.7 copy-start.8
  169.9 17.6 %all-to-all-start.3 = ((bf16[16,4,2176]{2,1,0:T(4,128)(2,1)}), bf16[16,4,2176]{2,1,0:T(4,128)(2,1)S(1)}, u32[]{:S(2)}, u32[]{:S(2)}) async-start(bf16[16,4,2176]{2,1,0:T(4,128)(2,1)} %shared.1), calls=%async_computation.3 | async-start | bytes 557056 | tf_op jit(solution)/shard_map/all_to_all | solution.py:455
  177.1 1.0 copy-start.9
  178.1 0.9 copy-start.11
  179.1 8.5 %copy-start.2 = (s32[1,4]{1,0:T(1,128)S(1)}, s32[1,4]{1,0:T(1,128)}, u32[]{:S(2)}) copy-start(s32[1,4]{1,0:T(1,128)} %param.26) | copy-start | bytes 52
Sparse Core Ops, SparseCore 0:
  33.9 79.3 all-gather.1

commit v6 on v3

--- a/solution.py
+++ b/solution.py
@@ -57,23 +57,14 @@
 def turned(values, tab):
     return values * tab[:, :HEAD_SIZE] + pltpu.roll(values, HEAD_SIZE // 2, 1) * tab[:, HEAD_SIZE:]
 
-def project_kernel(w_hbm, own_hbm, other_hbm, tab_own, tab_oth, q_own, kv_own, packed, w, x, w_sem, x_sem):
-    copies = [
-        pltpu.make_async_copy(own_hbm.at[0:QROWS], x.at[0:QROWS], x_sem.at[0]),
-        pltpu.make_async_copy(other_hbm.at[0:QROWS], x.at[QROWS : 2 * QROWS], x_sem.at[1]),
-        pltpu.make_async_copy(own_hbm.at[QROWS:ROWS], x.at[2 * QROWS : 2 * QROWS + REC], x_sem.at[2]),
-        pltpu.make_async_copy(other_hbm.at[QROWS:ROWS], x.at[2 * QROWS + REC : 2 * ROWS], x_sem.at[3]),
-    ]
+def project_kernel(w_hbm, x, tab_own, tab_oth, q_own, kv_own, packed, w, w_sem):
     groups = [(0, SPLIT), (SPLIT, WIDE)]
     pieces=[]
     for k,(lo,hi) in enumerate(groups):
         for xi in range(4):
             for yi in range(4):
                 pieces.append(pltpu.make_async_copy(w_hbm.at[xi*4+yi, :, :, :, :, lo:hi], w.at[:, xi, :, :, yi, :, lo:hi], w_sem.at[k, xi*4+yi]))
-    for copy in copies[:2]: copy.start()
     for copy in pieces: copy.start()
-    for copy in copies[2:]: copy.start()
-    for copy in copies[:2]: copy.wait()
     wf = w.reshape(MODEL, WIDE)
     for k,(lo,hi) in enumerate(groups):
         for copy in pieces[k*16:(k+1)*16]: copy.wait()
@@ -87,7 +78,6 @@
                     q_own[:, at] = turned(part[:QROWS], tab_own[0:QROWS,:]).astype(bf16)
                     packed[0:QROWS, at] = turned(part[QROWS:], tab_oth[0:QROWS,:]).astype(bf16)
             else:
-                for copy in copies[2:]: copy.wait()
                 acc = dot(x[...], wf[:, cols])
                 for own in (True, False):
                     tab = (tab_own if own else tab_oth)[...]
@@ -105,16 +95,16 @@
                             packed[QROWS:, b * 256 : b * 256 + 128] = keys[rows]
                             packed[QROWS:, b * 256 + 128 : (b + 1) * 256] = values[rows]
 
-def project(weights, own, other, tab_own, tab_oth):
+def project(weights, rows, tab_own, tab_oth):
     return pl.pallas_call(
         project_kernel, name="project",
         out_shape=(jax.ShapeDtypeStruct((QROWS, HALF), bf16), jax.ShapeDtypeStruct((ROWS, 2 * HEAD_SIZE), bf16), jax.ShapeDtypeStruct((QROWS + 128, HALF), bf16)),
-        in_specs=[ANY, ANY, ANY, VMEM, VMEM], out_specs=(VMEM, VMEM, VMEM),
-        scratch_shapes=[pltpu.VMEM((2, 4, 2, 4, 4, 16, WIDE), bf16), pltpu.VMEM((2 * ROWS, MODEL), bf16),
-            pltpu.SemaphoreType.DMA((2, 16)), pltpu.SemaphoreType.DMA((4,))],
-        compiler_params=pltpu.CompilerParams(vmem_limit_bytes=40 << 20),
+        in_specs=[ANY, VMEM, VMEM, VMEM], out_specs=(VMEM, VMEM, VMEM),
+        scratch_shapes=[pltpu.VMEM((2, 4, 2, 4, 4, 16, WIDE), bf16),
+            pltpu.SemaphoreType.DMA((2, 16))],
+        compiler_params=pltpu.CompilerParams(vmem_limit_bytes=44 << 20),
         cost_estimate=pl.CostEstimate(flops=6 * 10**9, bytes_accessed=20 * 10**6, transcendentals=0),
-    )(weights, own, other, tab_own, tab_oth)
+    )(weights, rows, tab_own, tab_oth)
 
 
 def shared_kernel(info, q_own, packed, kv, out, qs):
@@ -140,11 +130,16 @@
         level = top * scale + jnp.log(total)
         for h in range(GROUP):
             head = s * GROUP + h
-            out[:, :, head * HEAD_SIZE : (head + 1) * HEAD_SIZE] = done[h*LINE:(h+1)*LINE].reshape(16,4,HEAD_SIZE)
+            out[:, :, head * HEAD_SIZE : (head + 1) * HEAD_SIZE] = done[h*LINE:(h+1)*LINE].reshape(16,4,HEAD_SIZE).astype(bf16)
             stats = jnp.where(lane == head, level[h*LINE:(h+1)*LINE], stats)
-    out[:, :, STAT:] = stats.reshape(16,4,HEAD_SIZE)
+    high = stats.astype(bf16).astype(f32)
+    left = stats - high
+    middle = left.astype(bf16).astype(f32)
+    low = left - middle
+    parts = high + pltpu.roll(middle, QUERY_HEADS, 1) + pltpu.roll(low, 2 * QUERY_HEADS, 1)
+    out[:, :, STAT:] = parts.reshape(16, 4, HEAD_SIZE).astype(bf16)
 def shared_attention(info, q_own, packed, kv):
-    return pl.pallas_call(shared_kernel, name="shared", out_shape=jax.ShapeDtypeStruct((16,4, STAT + 128), f32),
+    return pl.pallas_call(shared_kernel, name="shared", out_shape=jax.ShapeDtypeStruct((16, 4, STAT + 128), bf16),
         in_specs=[SMEM, VMEM, VMEM, VMEM], out_specs=VMEM, scratch_shapes=[pltpu.VMEM((2, LINE, HALF), bf16)],
         compiler_params=pltpu.CompilerParams(vmem_limit_bytes=16 << 20),
         cost_estimate=pl.CostEstimate(flops=3 * 10**8, bytes_accessed=10**6, transcendentals=10**6))(info, q_own, packed, kv)
@@ -187,9 +182,11 @@
     cached = pltpu.make_async_copy(pages_hbm.at[:DEC_SLOTS], pages.at[:DEC_SLOTS], sems.at[1])
     cached.start()
     core = info[0]; start = info[2]; place = info[3]
-    qs[core] = q_own[...]
+    q_copy = pltpu.make_async_copy(q_own, qs.at[core], sems.at[2])
+    q_copy.start()
+    kv_copy = pltpu.make_async_copy(kv_own, ks.at[core], sems.at[3])
+    kv_copy.start()
     qs[1 - core] = packed[0:QROWS, :]
-    ks[core] = kv_own[...]
     for b in range(4):
         ks[1 - core, b * 128 : (b + 1) * 128, :] = packed[QROWS:, b * 256 : (b + 1) * 256]
     history = HIST_SLOTS * PAGE_TOKENS
@@ -201,6 +198,8 @@
     c2 = scale*LOG2E
     ones_h = jnp.ones((history, HEAD_SIZE), bf16)
     ones_n = jnp.ones((PRE, HEAD_SIZE), bf16)
+    q_copy.wait()
+    kv_copy.wait()
     old.wait()
     for s in range(KEY_VALUE_HEADS):
         old_keys = pages[DEC_SLOTS:, :, s * HEAD_SIZE : (s + 1) * HEAD_SIZE].reshape(history, HEAD_SIZE)
@@ -248,8 +247,8 @@
     return pl.pallas_call(
         local_kernel, name="local",
         out_shape=(jax.ShapeDtypeStruct((PRE, QUERY_HEADS * HEAD_SIZE), bf16), jax.ShapeDtypeStruct((64, HEAD_SIZE), f32), jax.ShapeDtypeStruct((64, HEAD_SIZE), f32)),
-        in_specs=[SMEM, VMEM, VMEM, VMEM, VMEM, VMEM, HBM], out_specs=(VMEM, VMEM, VMEM),
-        scratch_shapes=[pltpu.VMEM((2, QROWS, HALF), bf16), pltpu.VMEM((2, ROWS, 2 * HEAD_SIZE), bf16), pltpu.VMEM((DEC_SLOTS + HIST_SLOTS, PAGE_TOKENS, 4 * HEAD_SIZE), bf16), pltpu.SemaphoreType.DMA((2,))],
+        in_specs=[SMEM, ANY, ANY, VMEM, VMEM, VMEM, HBM], out_specs=(VMEM, VMEM, VMEM),
+        scratch_shapes=[pltpu.VMEM((2, QROWS, HALF), bf16), pltpu.VMEM((2, ROWS, 2 * HEAD_SIZE), bf16), pltpu.VMEM((DEC_SLOTS + HIST_SLOTS, PAGE_TOKENS, 4 * HEAD_SIZE), bf16), pltpu.SemaphoreType.DMA((4,))],
         compiler_params=pltpu.CompilerParams(vmem_limit_bytes=48 << 20),
         cost_estimate=pl.CostEstimate(flops=10**10, bytes_accessed=8 * 10**6, transcendentals=3 * 10**6),
     )(info, q_own, kv_own, packed, bias_private, bias_new, pages)
@@ -259,11 +258,16 @@
     row = lax.broadcasted_iota(jnp.int32, (DEC, STAT + 128), 0)
     chosen = jnp.zeros((DEC, STAT + 128), f32)
     for r in range(DEC):
-        chosen = jnp.where(row == r, shared[groups[r]], chosen)
+        chosen = jnp.where(row == r, shared[groups[r]].astype(f32), chosen)
     for head in range(QUERY_HEADS):
         rows = slice(head*DEC,(head+1)*DEC)
         at = slice(head * HEAD_SIZE, (head + 1) * HEAD_SIZE)
-        far = chosen[:, STAT+head:STAT+head+1]
+        at_stat = STAT + head
+        far = (
+            chosen[:, at_stat : at_stat + 1]
+            + chosen[:, at_stat + QUERY_HEADS : at_stat + QUERY_HEADS + 1]
+            + chosen[:, at_stat + 2 * QUERY_HEADS : at_stat + 2 * QUERY_HEADS + 1]
+        )
         near = local_stat[rows, 0:1]
         top = jnp.maximum(far, near)
         far = jnp.exp(far - top); near = jnp.exp(near - top)
@@ -285,17 +289,18 @@
     return (widened * factor * gain.astype(f32)).astype(bf16)
 
 
-def gather_weights(w_query, key_value_weight):
+def weight_block(w_query, key_value_weight):
     key_half = key_value_weight.reshape(16, 2, 2, HEAD_SIZE)
     halves = [
         jnp.concatenate([w_query[:, c * HALF : (c + 1) * HALF], key_half[:, 0, c], key_half[:, 1, c]], axis=1)
         for c in range(2)
     ]
-    block = jnp.stack(halves, axis=0)
+    return jnp.stack(halves, axis=0)
+
+
+def main_column(block):
     sent = jnp.broadcast_to(block[None, :, None], (2, 2, 4, 16, WIDE)).reshape(16, 16, WIDE)
-    column = lax.all_to_all(sent, ("zh", "c", "zl"), 0, 0, tiled=True)
-    whole = lax.all_gather(column.reshape(256, WIDE), ("x", "y"), axis=0, tiled=True)
-    return whole.reshape(16, 2, 2, 4, 16, WIDE)
+    return lax.all_to_all(sent, ("zh", "c", "zl"), 0, 0, tiled=True)
 
 
 def on_device(
@@ -311,19 +316,35 @@
     request = rec_req[0]
     within = rec_off[0]
 
-    weights = gather_weights(w_query, key_value_weight)
+    column = main_column(weight_block(w_query, key_value_weight))
+    weights = lax.all_gather(column.reshape(256, WIDE), ("x", "y"), axis=0, tiled=True)
+    weights = weights.reshape(16, 2, 2, 4, 16, WIDE)
 
     dec_pos = small_lookup(prefix_line, groups) + lengths
     parts = jnp.stack([dec_pos // 64, dec_pos % 64], axis=1).astype(bf16)
     extra = jnp.concatenate([x_dec, parts, jnp.zeros((DEC, 126), bf16)], axis=1)
+    normed_pre = rms_scaled(x_pre, norm_gain)
+    normed_rec = rms_scaled(rec_hidden, norm_gain)
+
+    counts = (lengths + PAGE_TOKENS - 1) // PAGE_TOKENS
+    ends = jnp.cumsum(counts)
+    firsts = ends - counts
+    slot = jnp.arange(DEC_SLOTS, dtype=jnp.int32)
+    slot_request = jnp.sum((slot[:, None] >= ends[None, :]).astype(jnp.int32), axis=1)
+    used = slot_request < DEC
+    slot_request = jnp.minimum(slot_request, DEC - 1)
+    slot_page = jnp.where(used, slot - small_lookup(firsts, slot_request), 0)
+    dec_pages = small_lookup(page_table.reshape(-1), slot_request * page_table.shape[1] + slot_page)
+    slots = jnp.concatenate([dec_pages, pre_table[0]], axis=0)
+
+    pages = take_pages(slots, cache_pool)
+
     line = lax.all_to_all(
         jnp.broadcast_to(extra[None], (16, DEC, MODEL + 128)), DP, 0, 0, tiled=True
     ).reshape(LINE, MODEL + 128)
     line_parts = line[:, MODEL : MODEL + 2].astype(jnp.int32)
     line_pos = line_parts[:, 0] * 64 + line_parts[:, 1]
-
-    rows = jnp.concatenate([x_pre, line[:, :MODEL], rec_hidden], axis=0)
-    normed = rms_scaled(rows, norm_gain)
+    normed_line = rms_scaled(line[:, :MODEL], norm_gain)
     pre_pos = pre_start[0] + jnp.arange(PRE, dtype=jnp.int32)
     rec_pos = small_lookup(prefix_line, small_lookup(groups, request)) + within
     positions = jnp.concatenate([pre_pos, line_pos, rec_pos], axis=0)
@@ -334,19 +355,11 @@
     sines = jnp.sin(angles)
     table = jnp.concatenate([cosines, cosines, -sines, sines], axis=1)
     swap = [(0, 1), (1, 0)]
-    other = lax.ppermute(normed, "c", swap)
+    own = (normed_pre, normed_line, normed_rec)
+    other = [lax.ppermute(v, "c", swap) for v in own]
     other_table = lax.ppermute(table, "c", swap)
-
-    counts = (lengths + PAGE_TOKENS - 1) // PAGE_TOKENS
-    ends = jnp.cumsum(counts)
-    firsts = ends - counts
-    slot = jnp.arange(DEC_SLOTS, dtype=jnp.int32)
-    slot_request = jnp.sum((slot[:, None] >= ends[None, :]).astype(jnp.int32), axis=1)
-    used = slot_request < DEC
-    slot_request = jnp.minimum(slot_request, DEC - 1)
-    slot_page = jnp.where(used, slot - small_lookup(firsts, slot_request), 0)
-    dec_pages = small_lookup(page_table.reshape(-1), slot_request * page_table.shape[1] + slot_page)
-    slots = jnp.concatenate([dec_pages, pre_table[0]], axis=0)
+    rows = jnp.concatenate([own[0], own[1], other[0], other[1], own[2], other[2]], axis=0)
+
     key_pos = slot_page[:, None] * PAGE_TOKENS + jnp.arange(PAGE_TOKENS, dtype=jnp.int32)[None, :]
     valid = used[:, None] & (key_pos < small_lookup(lengths, slot_request)[:, None])
     rec_slot = small_lookup(firsts, request) + within // PAGE_TOKENS
@@ -364,11 +377,10 @@
     own_prefix = small_lookup(prefix_line, place[None])[0]
     info = jnp.stack([core, own_prefix, pre_start[0], place]).astype(jnp.int32)
 
-    pages = take_pages(slots, cache_pool)
-    weights, pages, bias_private, bias_new, info, slots = lax.optimization_barrier(
-        (weights, pages, bias_private, bias_new, info, slots)
+    weights, rows, table, other_table, pages, bias_private, bias_new, info = lax.optimization_barrier(
+        (weights, rows, table, other_table, pages, bias_private, bias_new, info)
     )
-    q_own, kv_own, packed = project(weights, normed, other, table, other_table)
+    q_own, kv_own, packed = project(weights, rows, table, other_table)
     packed = lax.ppermute(packed, "c", swap)
     shared_part = shared_attention(info, q_own, packed, shared_kv)
     shared_part = lax.all_to_all(shared_part, DP, 0, 0, tiled=True)

time: 170 us -> 167 us (0.982)
  waiting for transfers between devices: 50 us -> 35.9 us
  local copies, waits for them, and re-layouts: 11.1 us -> 18.2 us
  Pallas kernels: 31.4 us -> 33.5 us
    all_gather x1, waiting for transfers between devices: 33.5 us -> 26.5 us  [on_device(): lax.all_gather(column.reshape(256, WIDE), ('x', 'y'), axis=0, tiled=True)]
    unnamed x1 -> x4, other arithmetic: 0.71 us -> 7.58 us
    all_to_all x1, waiting for transfers between devices: 6.21 us -> 1.73 us  [on_device(): shared_part = lax.all_to_all(shared_part, DP, 0, 0, tiled=True)]
    unnamed x16 -> x24, local copies, waits for them, and re-layouts: 5.03 us -> 9.24 us
    concatenate x0 -> x1, local copies, waits for them, and re-layouts: none -> 3.57 us  [on_device(): jnp.concatenate([own[0], own[1], other[0], other[1], own[2], other[2]], a...]
    convert_element_type x2 -> x1, other arithmetic: 4.25 us -> 0.71 us  [rms_scaled(): return (widened * factor * gain.astype(f32)).astype(bf16)]
    all_to_all x1, waiting for transfers between devices: 8.45 us -> 5.92 us  [on_device(): lax.all_to_all(jnp.broadcast_to(extra[None], (16, DEC, MODEL + 128)), DP,...]
    pallas_call x1, Pallas kernels: 9.82 us -> 12 us  [project(): pl.pallas_call(project_kernel, name='project', out_shape=(jax.ShapeDtypeS...]
  transfers between devices with their start and end apart: 6 -> 8, of which waited for: 4 -> 4; matrix products, arithmetic and copies ran while one was open for 12% -> 17% of each run, Pallas kernels for 10% -> 11%
where the time goes in v6:
time: 167 us; the launch traced here: 166 us
  waiting for transfers between devices  35.9 us (21%)
  Pallas kernels  33.5 us (20%)
  blocking collectives  29 us (17%)
  local copies, waits for them, and re-layouts  18.2 us (11%)
  starting transfers between devices  17.4 us (10%)
  other arithmetic  16.9 us (10%)
  between operations  15 us (9%)
    all_to_all x1, blocking collectives, main_column(): return lax.all_to_all(sent, ('zh', 'c', 'zl'), 0, 0, tiled=True)  29 us
    all_gather x1, waiting for transfers between devices, on_device(): lax.all_gather(column.reshape(256, WIDE), ('x', 'y'), axis=0, tiled=True)  26.5 us
    pallas_call x1, Pallas kernels, project(): pl.pallas_call(project_kernel, name='project', out_shape=(jax.ShapeDtypeS...  12 us
    unnamed x24, local copies, waits for them, and re-layouts  9.24 us
    pallas_call x1, Pallas kernels, take_pages(): pl.pallas_call(pages_kernel, name='take_pages', out_shape=jax.ShapeDtypeS...  9.17 us
    pallas_call x1, Pallas kernels, local_attention(): pl.pallas_call(local_kernel, name='local', out_shape=(jax.ShapeDtypeStruc...  8.44 us
    unnamed x4, other arithmetic  7.58 us
    all_to_all x1, starting transfers between devices, on_device(): shared_part = lax.all_to_all(shared_part, DP, 0, 0, tiled=True)  7.03 us
  transfers between devices with their start and end apart: 8, of which 4 were waited for; matrix products, arithmetic and copies ran while one was open for 17% of the time, Pallas kernels for 11%

profile of v6, /device:TPU:1, one launch (start us, length us, event | category | flops | bytes accessed | tf_op | source)
XLA Modules:
  0.0 166.2 jit_solution(5773125438714935672)
XLA Ops:
  7.3 0.9 reshape.314
  8.2 0.8 fusion.24
  9.1 29.0 %all_to_all.15 = bf16[16,16,1280]{2,1,0:T(8,128)(2,1)} all-to-all(bf16[16,16,1280]{2,1,0:T(8,128)(2,1)S(1)} %bitcast.48), channel_id=1, replica_groups=mesh['zh'=2,'x'=4,'c'=2,'zl'=4,'y'=4] {'zh','c','zl'}, dimensions={0} | all-to-all | bytes 1310720 | tf_op jit(solution)/shard_map/all_to_all | solution.py:303
  38.1 0.9 select_reduce_fusion.6
  38.9 0.7 fusion.17
  39.6 0.7 fusion.20
  40.3 0.1 copy.42
  40.4 0.1 copy.43
  40.5 0.9 concatenate.33
  41.3 1.0 broadcast_in_dim.131
  42.3 5.8 %all-to-all-start.1 = ((bf16[16,4,4224]{2,1,0:T(4,128)(2,1)}), bf16[16,4,4224]{2,1,0:T(4,128)(2,1)}, u32[]{:S(2)}, u32[]{:S(2)}) async-start(bf16[16,4,4224]{2,1,0:T(4,128)(2,1)} %broadcast_in_dim.131), calls=%async_computation.1 | async-start | bytes 1081344 | tf_op jit(solution)/shard_map/all_to_all | solution.py:342
  48.1 0.7 convert_element_type.40
  48.8 1.6 fusion.3
  50.4 3.0 %constant_dynamic-update-slice_fusion.5 = (bf16[1024,4096]{1,0:T(8,128)(2,1)}, bf16[128,4096]{1,0:T(8,128)(2,1)}) fusion(f32[4096]{0:T(1024)S(1)} %convert_element_type.40, f32[128]{0:T(128)S(1)} %add_rsqrt_fusion.2, bf16[128,4096]{1,0:T(8,128)(2,1)} %param.16), kind=kLoop, calls=%fused_computation.46 | loop fusion | flops 2097151 | bytes 3162624
  53.3 0.7 collective-permute-start
  54.0 0.2 reduce-window.8
  55.4 0.2 select_reduce_fusion
  55.6 0.6 fusion
  56.3 0.3 fusion.7
  56.6 5.9 %all-to-all-done.1 = bf16[16,4,4224]{2,1,0:T(4,128)(2,1)} async-done(((bf16[16,4,4224]{2,1,0:T(4,128)(2,1)}), bf16[16,4,4224]{2,1,0:T(4,128)(2,1)}, u32[]{:S(2)}, u32[]{:S(2)}) %all-to-all-start.1) | async-done | bytes 540704 | tf_op jit(solution)/shard_map/all_to_all | solution.py:342
  62.5 1.2 reshape.318
  63.7 0.2 fusion.8
  63.9 1.2 constant_dynamic-update-slice_fusion.4
  65.1 2.3 %collective-permute-start.1 = (bf16[64,4096]{1,0:T(8,128)(2,1)}, bf16[64,4096]{1,0:T(8,128)(2,1)}, u32[]{:S(2)}, u32[]{:S(2)}) collective-permute-start(bf16[64,4096]{1,0:T(8,128)(2,1)} %get-tuple-element.39), channel_id=1, source_target_pairs={{0,16},{16,0},{1,17},{17,1},{2,18},{18,2},{3,19},{19,3},{4,20},{20... | collective-permute-start | bytes 1572872 | tf_op jit(solution)/shard_map/ppermute | solution.py:359
  67.4 2.3 %constant_dynamic-update-slice_fusion.3 = bf16[1024,4096]{1,0:T(8,128)(2,1)} fusion(bf16[1024,4096]{1,0:T(8,128)(2,1)} %get-tuple-element.38, bf16[128,4096]{1,0:T(8,128)(2,1)} %collective-permute-done), kind=kLoop, calls=%fused_computation.44 | loop fusion | bytes 2097152
  69.7 1.9 %constant_dynamic-update-slice_fusion.2 = bf16[1024,4096]{1,0:T(8,128)(2,1)} fusion(bf16[1024,4096]{1,0:T(8,128)(2,1)} %constant_dynamic-update-slice_fusion.3, bf16[64,4096]{1,0:T(8,128)(2,1)} %collective-permute-done.1), kind=kLoop, calls=%fused_computation.43 | loop fusion | bytes 1048576
  71.7 3.4 %constant_dynamic-update-slice_fusion.1 = (bf16[1024,4096]{1,0:T(8,128)(2,1)}, bf16[320,4096]{1,0:T(8,128)(2,1)}) fusion(bf16[1024,4096]{1,0:T(8,128)(2,1)} %constant_dynamic-update-slice_fusion.2, f32[4096]{0:T(1024)S(1)} %convert_element_type.40, f32[320]{0:T(512)S(1)} %add_rsqrt_fusion, bf16[320,4096]{1,0:T(8,128)(2,1)S(1)} %copy-done.4), kind=kLoop, calls=%fused_computation.42 | loop fusion | flops 5242880 | bytes 7881984
  75.1 0.1 copy.45
  75.2 0.1 and.122
  75.6 0.6 fusion.18
  76.4 0.2 fusion.14
  76.7 1.0 multiply_cosine_fusion
  77.7 0.3 pad_maximum_fusion.tab_own
  78.0 0.8 collective-permute-start.3
  78.7 0.7 pad_add_fusion.2.info
  79.5 2.6 %copy-done = bf16[84,64,512]{2,1,0:T(8,128)(2,1)S(1)} copy-done((bf16[84,64,512]{2,1,0:T(8,128)(2,1)S(1)}, bf16[84,64,512]{2,1,0:T(8,128)(2,1)}, u32[]{:S(2)}) %copy-start) | copy-done | bytes 5505048
  82.0 9.2 %take_pages.1.pages_hbm = bf16[84,64,512]{2,1,0:T(8,128)(2,1)S(1)} custom-call(s32[84]{0:T(128)S(1)} %pad_add_fusion.1.slots, bf16[84,64,512]{2,1,0:T(8,128)(2,1)S(1)} %copy-done), custom_call_target="tpu_custom_call" | custom-call | bytes 22000000 | tf_op jit(solution)/shard_map/take_pages/pallas_call | solution.py:163
  91.2 2.4 %copy-done.1 = bf16[84,64,512]{2,1,0:T(8,128)(2,1)} copy-done((bf16[84,64,512]{2,1,0:T(8,128)(2,1)}, bf16[84,64,512]{2,1,0:T(8,128)(2,1)S(1)}, u32[]{:S(2)}) %copy-start.1) | copy-done | bytes 5505048
  93.6 3.6 %constant_dynamic-update-slice_fusion.x = bf16[1024,4096]{1,0:T(8,128)(2,1)} fusion(bf16[1024,4096]{1,0:T(8,128)(2,1)} %get-tuple-element.36, bf16[320,4096]{1,0:T(8,128)(2,1)} %collective-permute-done.2), kind=kLoop, calls=%fused_computation.41 | loop fusion | bytes 5242880 | tf_op jit(solution)/shard_map/concatenate | solution.py:361
  97.2 26.5 %all-gather.2.cloned.1.call-done = bf16[4096,1280]{1,0:T(8,128)(2,1)} async-done(((bf16[256,1280]{1,0:T(8,128)(2,1)}), bf16[4096,1280]{1,0:T(8,128)(2,1)}) %all-gather.2.cloned.1.call-update) | async-done | bytes 10485776 | tf_op jit(solution)/shard_map/all_gather | solution.py:320
  123.7 12.0 %project.1 = (bf16[192,1024]{1,0:T(8,128)(2,1)S(1)}, bf16[512,256]{1,0:T(8,128)(2,1)S(1)}, bf16[320,1024]{1,0:T(8,128)(2,1)S(1)}) custom-call(bf16[16,2,2,4,16,1280]{5,4,3,2,1,0:T(8,128)(2,1)} %bitcast.52, bf16[1024,4096]{1,0:T(8,128)(2,1)} %constant_dynamic-update-slice_fusion.x, f32[512,256]{1,0:T(8,128)S(1)} %pad_maximum_fusion.tab_own, ...), custom_call_target="tpu_custom_call" | custom-call | flops 6000000000 | bytes 20000000 | tf_op jit(solution)/shard_map/project/pallas_call | solution.py:99
  135.7 0.8 collective-permute-start.4
  136.4 1.7 %collective-permute-done.4.packed = bf16[320,1024]{1,0:T(8,128)(2,1)S(1)} collective-permute-done((bf16[320,1024]{1,0:T(8,128)(2,1)S(1)}, bf16[320,1024]{1,0:T(8,128)(2,1)S(1)}, u32[]{:S(2)}, u32[]{:S(2)}) %collective-permute-start.4) | collective-permute-done | bytes 655392 | tf_op jit(solution)/shard_map/ppermute | solution.py:384
  138.1 2.4 %shared.1 = bf16[16,4,2176]{2,1,0:T(4,128)(2,1)} custom-call(s32[4]{0:T(128)S(1)} %pad_add_fusion.2.info, bf16[192,1024]{1,0:T(8,128)(2,1)S(1)} %get-tuple-element.21.q_own, bf16[320,1024]{1,0:T(8,128)(2,1)S(1)} %collective-permute-done.4.packed, bf16[512,512]{1,0:T(8,128)(2,1)S(1)} %copy-done.3), custom_call_target="tpu_custom_call" | custom-call | flops 300000000 | bytes 1000000 | tf_op jit(solution)/shard_map/shared/pallas_call | solution.py:142
  140.6 7.0 %all-to-all-start.2 = ((bf16[16,4,2176]{2,1,0:T(4,128)(2,1)}), bf16[16,4,2176]{2,1,0:T(4,128)(2,1)S(1)}, u32[]{:S(2)}, u32[]{:S(2)}) async-start(bf16[16,4,2176]{2,1,0:T(4,128)(2,1)} %shared.1), calls=%async_computation.2 | async-start | bytes 557056 | tf_op jit(solution)/shard_map/all_to_all | solution.py:386
  147.6 8.4 %local.1 = (bf16[128,2048]{1,0:T(8,128)(2,1)}, f32[64,128]{1,0:T(8,128)S(1)}, f32[64,128]{1,0:T(8,128)S(1)}) custom-call(s32[4]{0:T(128)S(1)} %pad_add_fusion.2.info, bf16[192,1024]{1,0:T(8,128)(2,1)S(1)} %get-tuple-element.21.q_own, bf16[512,256]{1,0:T(8,128)(2,1)S(1)} %get-tuple-element.22.kv_own, bf16[320,1024]{1,0:T(8,128)(2,1)S(1)} %collective-permute-done.4.packed, ...), custom_call_target="tpu_custom_call" | custom-call | flops 10000000000 | bytes 8000000 | tf_op jit(solution)/shard_map/local/pallas_call | solution.py:247
  156.1 1.7 %all-to-all-done.2.shared = bf16[16,4,2176]{2,1,0:T(4,128)(2,1)S(1)} async-done(((bf16[16,4,2176]{2,1,0:T(4,128)(2,1)}), bf16[16,4,2176]{2,1,0:T(4,128)(2,1)S(1)}, u32[]{:S(2)}, u32[]{:S(2)}) %all-to-all-start.2) | async-done | bytes 278560 | tf_op jit(solution)/shard_map/all_to_all | solution.py:386
  157.8 1.5 finish.1
  (63 shorter events, 1.3 us)
Async XLA Ops:
  7.2 47.9 %copy-start.2 = (s32[1,4]{1,0:T(1,128)S(1)}, s32[1,4]{1,0:T(1,128)}, u32[]{:S(2)}) copy-start(s32[1,4]{1,0:T(1,128)} %param.26) | copy-start | bytes 52
  7.2 48.0 %copy-start.9 = (s32[1,16]{1,0:T(1,128)S(1)}, s32[1,16]{1,0:T(1,128)}, u32[]{:S(2)}) copy-start(s32[1,16]{1,0:T(1,128)} %param.27) | copy-start | bytes 196
  7.2 47.9 %copy-start.5 = (s32[1,4]{1,0:T(1,128)S(1)}, s32[1,4]{1,0:T(1,128)}, u32[]{:S(2)}) copy-start(s32[1,4]{1,0:T(1,128)} %param.24) | copy-start | bytes 52
  7.2 47.0 %copy-start.7 = (s32[1,320]{1,0:T(1,128)S(1)}, s32[1,320]{1,0:T(1,128)}, u32[]{:S(2)}) copy-start(s32[1,320]{1,0:T(1,128)} %param.30) | copy-start | bytes 3844
  7.2 47.7 %copy-start.6 = (s32[1,4,48]{2,1,0:T(4,128)S(1)}, s32[1,4,48]{2,1,0:T(4,128)}, u32[]{:S(2)}) copy-start(s32[1,4,48]{2,1,0:T(4,128)} %param.25) | copy-start | bytes 2308
  7.2 48.1 %copy-start.8 = (s32[1,320]{1,0:T(1,128)S(1)}, s32[1,320]{1,0:T(1,128)}, u32[]{:S(2)}) copy-start(s32[1,320]{1,0:T(1,128)} %param.31) | copy-start | bytes 3844
  7.2 48.4 %copy-start.4 = (bf16[320,4096]{1,0:T(8,128)(2,1)S(1)}, bf16[320,4096]{1,0:T(8,128)(2,1)}, u32[]{:S(2)}) copy-start(bf16[320,4096]{1,0:T(8,128)(2,1)} %param.18) | copy-start | bytes 7864324
  7.2 116.5 %all-gather.2.cloned.1.call-start = ((), (), s32[]{:S(2)}) async-start(), calls=%async_computation.3 | async-start | bytes 11141120 | tf_op jit(solution)/shard_map/all_gather | solution.py:320
  42.3 20.2 %all-to-all-start.1 = ((bf16[16,4,4224]{2,1,0:T(4,128)(2,1)}), bf16[16,4,4224]{2,1,0:T(4,128)(2,1)}, u32[]{:S(2)}, u32[]{:S(2)}) async-start(bf16[16,4,4224]{2,1,0:T(4,128)(2,1)} %broadcast_in_dim.131), calls=%async_computation.1 | async-start | bytes 1081344 | tf_op jit(solution)/shard_map/all_to_all | solution.py:342
  53.3 14.1 %collective-permute-start = (bf16[128,4096]{1,0:T(8,128)(2,1)}, bf16[128,4096]{1,0:T(8,128)(2,1)}, u32[]{:S(2)}, u32[]{:S(2)}) collective-permute-start(bf16[128,4096]{1,0:T(8,128)(2,1)} %get-tuple-element.43), channel_id=1, source_target_pairs={{0,16},{16,0},{1,17},{17,1},{2,18},{18,2},{3,19},{19,3},{4,20},{20... | collective-permute-start | bytes 3145736 | tf_op jit(solution)/shard_map/ppermute | solution.py:359
  65.1 4.6 %collective-permute-start.1 = (bf16[64,4096]{1,0:T(8,128)(2,1)}, bf16[64,4096]{1,0:T(8,128)(2,1)}, u32[]{:S(2)}, u32[]{:S(2)}) collective-permute-start(bf16[64,4096]{1,0:T(8,128)(2,1)} %get-tuple-element.39), channel_id=1, source_target_pairs={{0,16},{16,0},{1,17},{17,1},{2,18},{18,2},{3,19},{19,3},{4,20},{20... | collective-permute-start | bytes 1572872 | tf_op jit(solution)/shard_map/ppermute | solution.py:359
  67.4 8.0 %copy-start.10 = (s32[1,16]{1,0:T(1,128)S(1)}, s32[1,16]{1,0:T(1,128)}, u32[]{:S(2)}) copy-start(s32[1,16]{1,0:T(1,128)} %param.29) | copy-start | bytes 196
  75.1 18.5 %collective-permute-start.2 = (bf16[320,4096]{1,0:T(8,128)(2,1)}, bf16[320,4096]{1,0:T(8,128)(2,1)}, u32[]{:S(2)}, u32[]{:S(2)}) collective-permute-start(bf16[320,4096]{1,0:T(8,128)(2,1)} %get-tuple-element.37), channel_id=1, source_target_pairs={{0,16},{16,0},{1,17},{17,1},{2,18},{18,2},{3,19},{19,3},{4,20},{20... | collective-permute-start | bytes 7864328 | tf_op jit(solution)/shard_map/ppermute | solution.py:359
  78.0 19.2 %collective-permute-start.3 = (f32[512,256]{1,0:T(8,128)S(1)}, f32[512,256]{1,0:T(8,128)S(1)}, u32[]{:S(2)}, u32[]{:S(2)}) collective-permute-start(f32[512,256]{1,0:T(8,128)S(1)} %pad_maximum_fusion.tab_own), channel_id=1, source_target_pairs={{0,16},{16,0},{1,17},{17,1},{2,18},{18,2},{3,19},{19,3},{4,20},{20... | collective-permute-start | bytes 1572872 | tf_op jit(solution)/shard_map/ppermute | solution.py:360
  79.5 2.6 %copy-start = (bf16[84,64,512]{2,1,0:T(8,128)(2,1)S(1)}, bf16[84,64,512]{2,1,0:T(8,128)(2,1)}, u32[]{:S(2)}) copy-start(bf16[84,64,512]{2,1,0:T(8,128)(2,1)} %pool.1) | copy-start | bytes 16515076
  91.2 2.4 %copy-start.1 = (bf16[84,64,512]{2,1,0:T(8,128)(2,1)}, bf16[84,64,512]{2,1,0:T(8,128)(2,1)S(1)}, u32[]{:S(2)}) copy-start(bf16[84,64,512]{2,1,0:T(8,128)(2,1)S(1)} %take_pages.1.pages_hbm) | copy-start | bytes 16515076
  123.7 14.5 %copy-start.3 = (bf16[512,512]{1,0:T(8,128)(2,1)S(1)}, bf16[512,512]{1,0:T(8,128)(2,1)}, u32[]{:S(2)}) copy-start(bf16[512,512]{1,0:T(8,128)(2,1)} %kv.1) | copy-start | bytes 1572868
  135.7 2.5 %collective-permute-start.4 = (bf16[320,1024]{1,0:T(8,128)(2,1)S(1)}, bf16[320,1024]{1,0:T(8,128)(2,1)S(1)}, u32[]{:S(2)}, u32[]{:S(2)}) collective-permute-start(bf16[320,1024]{1,0:T(8,128)(2,1)S(1)} %get-tuple-element.23), channel_id=1, source_target_pairs={{0,16},{16,0},{1,17},{17,1},{2,18},{18,2},{3,19},{19,3},{4,20},{20... | collective-permute-start | bytes 1966088 | tf_op jit(solution)/shard_map/ppermute | solution.py:384
  140.6 17.2 %all-to-all-start.2 = ((bf16[16,4,2176]{2,1,0:T(4,128)(2,1)}), bf16[16,4,2176]{2,1,0:T(4,128)(2,1)S(1)}, u32[]{:S(2)}, u32[]{:S(2)}) async-start(bf16[16,4,2176]{2,1,0:T(4,128)(2,1)} %shared.1), calls=%async_computation.2 | async-start | bytes 557056 | tf_op jit(solution)/shard_map/all_to_all | solution.py:386
Sparse Core Ops, SparseCore 0:
  38.2 85.4 all-gather.1

commit v7 on v6

--- a/solution.py
+++ b/solution.py
@@ -57,14 +57,22 @@
 def turned(values, tab):
     return values * tab[:, :HEAD_SIZE] + pltpu.roll(values, HEAD_SIZE // 2, 1) * tab[:, HEAD_SIZE:]
 
-def project_kernel(w_hbm, x, tab_own, tab_oth, q_own, kv_own, packed, w, w_sem):
+def project_kernel(w_hbm, own_pre, own_line, own_rec, other_pre, other_line, other_rec, tab_own, tab_oth, q_own, kv_own, packed, w, x, w_sem, x_sem):
+    copies = []
+    at = 0
+    for part in (own_pre, own_line, other_pre, other_line, own_rec, other_rec):
+        copies.append(pltpu.make_async_copy(part, x.at[at : at + part.shape[0]], x_sem.at[len(copies)]))
+        at += part.shape[0]
     groups = [(0, SPLIT), (SPLIT, WIDE)]
     pieces=[]
     for k,(lo,hi) in enumerate(groups):
         for xi in range(4):
             for yi in range(4):
                 pieces.append(pltpu.make_async_copy(w_hbm.at[xi*4+yi, :, :, :, :, lo:hi], w.at[:, xi, :, :, yi, :, lo:hi], w_sem.at[k, xi*4+yi]))
+    for copy in copies[:4]: copy.start()
     for copy in pieces: copy.start()
+    for copy in copies[4:]: copy.start()
+    for copy in copies[:4]: copy.wait()
     wf = w.reshape(MODEL, WIDE)
     for k,(lo,hi) in enumerate(groups):
         for copy in pieces[k*16:(k+1)*16]: copy.wait()
@@ -78,6 +86,7 @@
                     q_own[:, at] = turned(part[:QROWS], tab_own[0:QROWS,:]).astype(bf16)
                     packed[0:QROWS, at] = turned(part[QROWS:], tab_oth[0:QROWS,:]).astype(bf16)
             else:
+                for copy in copies[4:]: copy.wait()
                 acc = dot(x[...], wf[:, cols])
                 for own in (True, False):
                     tab = (tab_own if own else tab_oth)[...]
@@ -95,16 +104,16 @@
                             packed[QROWS:, b * 256 : b * 256 + 128] = keys[rows]
                             packed[QROWS:, b * 256 + 128 : (b + 1) * 256] = values[rows]
 
-def project(weights, rows, tab_own, tab_oth):
+def project(weights, own, other, tab_own, tab_oth):
     return pl.pallas_call(
         project_kernel, name="project",
         out_shape=(jax.ShapeDtypeStruct((QROWS, HALF), bf16), jax.ShapeDtypeStruct((ROWS, 2 * HEAD_SIZE), bf16), jax.ShapeDtypeStruct((QROWS + 128, HALF), bf16)),
-        in_specs=[ANY, VMEM, VMEM, VMEM], out_specs=(VMEM, VMEM, VMEM),
-        scratch_shapes=[pltpu.VMEM((2, 4, 2, 4, 4, 16, WIDE), bf16),
-            pltpu.SemaphoreType.DMA((2, 16))],
-        compiler_params=pltpu.CompilerParams(vmem_limit_bytes=44 << 20),
+        in_specs=[ANY] * 7 + [VMEM, VMEM], out_specs=(VMEM, VMEM, VMEM),
+        scratch_shapes=[pltpu.VMEM((2, 4, 2, 4, 4, 16, WIDE), bf16), pltpu.VMEM((2 * ROWS, MODEL), bf16),
+            pltpu.SemaphoreType.DMA((2, 16)), pltpu.SemaphoreType.DMA((6,))],
+        compiler_params=pltpu.CompilerParams(vmem_limit_bytes=50 << 20),
         cost_estimate=pl.CostEstimate(flops=6 * 10**9, bytes_accessed=20 * 10**6, transcendentals=0),
-    )(weights, rows, tab_own, tab_oth)
+    )(weights, *own, *other, tab_own, tab_oth)
 
 
 def shared_kernel(info, q_own, packed, kv, out, qs):
@@ -141,7 +150,7 @@
 def shared_attention(info, q_own, packed, kv):
     return pl.pallas_call(shared_kernel, name="shared", out_shape=jax.ShapeDtypeStruct((16, 4, STAT + 128), bf16),
         in_specs=[SMEM, VMEM, VMEM, VMEM], out_specs=VMEM, scratch_shapes=[pltpu.VMEM((2, LINE, HALF), bf16)],
-        compiler_params=pltpu.CompilerParams(vmem_limit_bytes=16 << 20),
+        compiler_params=pltpu.CompilerParams(vmem_limit_bytes=8 << 20),
         cost_estimate=pl.CostEstimate(flops=3 * 10**8, bytes_accessed=10**6, transcendentals=10**6))(info, q_own, packed, kv)
 
 
@@ -249,7 +258,7 @@
         out_shape=(jax.ShapeDtypeStruct((PRE, QUERY_HEADS * HEAD_SIZE), bf16), jax.ShapeDtypeStruct((64, HEAD_SIZE), f32), jax.ShapeDtypeStruct((64, HEAD_SIZE), f32)),
         in_specs=[SMEM, ANY, ANY, VMEM, VMEM, VMEM, HBM], out_specs=(VMEM, VMEM, VMEM),
         scratch_shapes=[pltpu.VMEM((2, QROWS, HALF), bf16), pltpu.VMEM((2, ROWS, 2 * HEAD_SIZE), bf16), pltpu.VMEM((DEC_SLOTS + HIST_SLOTS, PAGE_TOKENS, 4 * HEAD_SIZE), bf16), pltpu.SemaphoreType.DMA((4,))],
-        compiler_params=pltpu.CompilerParams(vmem_limit_bytes=48 << 20),
+        compiler_params=pltpu.CompilerParams(vmem_limit_bytes=50 << 20),
         cost_estimate=pl.CostEstimate(flops=10**10, bytes_accessed=8 * 10**6, transcendentals=3 * 10**6),
     )(info, q_own, kv_own, packed, bias_private, bias_new, pages)
 
@@ -290,9 +299,18 @@
 
 
 def weight_block(w_query, key_value_weight):
-    key_half = key_value_weight.reshape(16, 2, 2, HEAD_SIZE)
+    def cut(array, c, width, start=0):
+        return array[:, start + c * width : start + (c + 1) * width]
+
     halves = [
-        jnp.concatenate([w_query[:, c * HALF : (c + 1) * HALF], key_half[:, 0, c], key_half[:, 1, c]], axis=1)
+        jnp.concatenate(
+            [
+                cut(w_query, c, HALF),
+                cut(key_value_weight, c, HEAD_SIZE),
+                cut(key_value_weight, c, HEAD_SIZE, 2 * HEAD_SIZE),
+            ],
+            axis=1,
+        )
         for c in range(2)
     ]
     return jnp.stack(halves, axis=0)
@@ -358,7 +376,6 @@
     own = (normed_pre, normed_line, normed_rec)
     other = [lax.ppermute(v, "c", swap) for v in own]
     other_table = lax.ppermute(table, "c", swap)
-    rows = jnp.concatenate([own[0], own[1], other[0], other[1], own[2], other[2]], axis=0)
 
     key_pos = slot_page[:, None] * PAGE_TOKENS + jnp.arange(PAGE_TOKENS, dtype=jnp.int32)[None, :]
     valid = used[:, None] & (key_pos < small_lookup(lengths, slot_request)[:, None])
@@ -377,10 +394,10 @@
     own_prefix = small_lookup(prefix_line, place[None])[0]
     info = jnp.stack([core, own_prefix, pre_start[0], place]).astype(jnp.int32)
 
-    weights, rows, table, other_table, pages, bias_private, bias_new, info = lax.optimization_barrier(
-        (weights, rows, table, other_table, pages, bias_private, bias_new, info)
+    weights, table, other_table, pages, bias_private, bias_new, info = lax.optimization_barrier(
+        (weights, table, other_table, pages, bias_private, bias_new, info)
     )
-    q_own, kv_own, packed = project(weights, rows, table, other_table)
+    q_own, kv_own, packed = project(weights, own, other, table, other_table)
     packed = lax.ppermute(packed, "c", swap)
     shared_part = shared_attention(info, q_own, packed, shared_kv)
     shared_part = lax.all_to_all(shared_part, DP, 0, 0, tiled=True)

time: 167 us -> 163 us (0.976)
  waiting for transfers between devices: 35.9 us -> 51.8 us
  local copies, waits for them, and re-layouts: 18.2 us -> 8.5 us
  other arithmetic: 16.9 us -> 11.8 us
  Pallas kernels: 33.5 us -> 31.1 us
  starting transfers between devices: 17.4 us -> 15.1 us
    all_gather x1, waiting for transfers between devices: 26.5 us -> 47.4 us  [on_device(): lax.all_gather(column.reshape(256, WIDE), ('x', 'y'), axis=0, tiled=True)]
    unnamed x4 -> x1, other arithmetic: 7.58 us -> 0.02 us
    all_to_all x1, waiting for transfers between devices: 5.92 us -> 0.01 us  [on_device(): lax.all_to_all(jnp.broadcast_to(extra[None], (16, DEC, MODEL + 128)), DP,...]
    convert_element_type x1 -> x4, other arithmetic: 0.71 us -> 5.15 us  [rms_scaled(): return (widened * factor * gain.astype(f32)).astype(bf16)]
    unnamed x24 -> x26, local copies, waits for them, and re-layouts: 9.24 us -> 5.12 us
    concatenate x1 -> x0, local copies, waits for them, and re-layouts: 3.57 us -> none  [on_device(): jnp.concatenate([own[0], own[1], other[0], other[1], own[2], other[2]], a...]
    pallas_call x1, Pallas kernels: 12 us -> 9.56 us  [project(): pl.pallas_call(project_kernel, name='project', out_shape=(jax.ShapeDtypeS...]
    ppermute x3, starting transfers between devices: 2.99 us -> 1.27 us  [on_device(): other = [lax.ppermute(v, 'c', swap) for v in own]]
  transfers between devices with their start and end apart: 8 -> 8, of which waited for: 4 -> 4; matrix products, arithmetic and copies ran while one was open for 17% -> 9% of each run, Pallas kernels for 11% -> 11%
where the time goes in v7:
time: 163 us
  waiting for transfers between devices  51.8 us (32%)
  Pallas kernels  31.1 us (19%)
  blocking collectives  29 us (18%)
  starting transfers between devices  15.1 us (9%)
  between operations  15 us (9%)
  other arithmetic  11.8 us (7%)
  local copies, waits for them, and re-layouts  8.5 us (5%)
    all_gather x1, waiting for transfers between devices, on_device(): lax.all_gather(column.reshape(256, WIDE), ('x', 'y'), axis=0, tiled=True)  47.4 us
    all_to_all x1, blocking collectives, main_column(): return lax.all_to_all(sent, ('zh', 'c', 'zl'), 0, 0, tiled=True)  29 us
    pallas_call x1, Pallas kernels, project(): pl.pallas_call(project_kernel, name='project', out_shape=(jax.ShapeDtypeS...  9.56 us
    pallas_call x1, Pallas kernels, take_pages(): pl.pallas_call(pages_kernel, name='take_pages', out_shape=jax.ShapeDtypeS...  9.17 us
    pallas_call x1, Pallas kernels, local_attention(): pl.pallas_call(local_kernel, name='local', out_shape=(jax.ShapeDtypeStruc...  8.43 us
    all_to_all x1, starting transfers between devices, on_device(): shared_part = lax.all_to_all(shared_part, DP, 0, 0, tiled=True)  7.03 us
    all_to_all x1, starting transfers between devices, on_device(): lax.all_to_all(jnp.broadcast_to(extra[None], (16, DEC, MODEL + 128)), DP,...  5.72 us
    convert_element_type x4, other arithmetic, rms_scaled(): return (widened * factor * gain.astype(f32)).astype(bf16)  5.15 us
  transfers between devices with their start and end apart: 8, of which 4 were waited for; matrix products, arithmetic and copies ran while one was open for 9% of the time, Pallas kernels for 11%

profile of v7, /device:TPU:1, one launch (start us, length us, event | category | flops | bytes accessed | tf_op | source)
XLA Modules:
  0.0 162.7 jit_solution(11657166866754108818)
XLA Ops:
  7.3 0.7 fusion.22
  8.0 0.8 fusion.21
  8.9 29.0 %all_to_all.15 = bf16[16,16,1280]{2,1,0:T(8,128)(2,1)} all-to-all(bf16[16,16,1280]{2,1,0:T(8,128)(2,1)S(1)} %bitcast.40), channel_id=1, replica_groups=mesh['zh'=2,'x'=4,'c'=2,'zl'=4,'y'=4] {'zh','c','zl'}, dimensions={0} | all-to-all | bytes 1310720 | tf_op jit(solution)/shard_map/all_to_all | solution.py:321
  37.9 0.2 select_reduce_fusion.6
  38.1 0.1 copy.27
  38.2 0.1 copy.26
  38.3 0.1 concatenate.30
  38.4 0.9 broadcast_in_dim.131
  39.4 5.7 %all-to-all-start.1 = ((bf16[16,4,4224]{2,1,0:T(4,128)(2,1)}), bf16[16,4,4224]{2,1,0:T(4,128)(2,1)S(1)}, u32[]{:S(2)}, u32[]{:S(2)}) async-start(bf16[16,4,4224]{2,1,0:T(4,128)(2,1)} %broadcast_in_dim.131), calls=%async_computation.1 | async-start | bytes 1081344 | tf_op jit(solution)/shard_map/all_to_all | solution.py:360
  45.1 1.5 fusion.3
  46.6 2.6 %fusion.5.own_pre = bf16[128,4096]{1,0:T(8,128)(2,1)} fusion(bf16[128,4096]{1,0:T(8,128)(2,1)} %param.16, f32[4096]{0:T(1024)S(1)} %convert_element_type.43, f32[128]{0:T(128)S(1)} %add_rsqrt_fusion.2), kind=kLoop, calls=%fused_computation.9 | loop fusion | flops 2097152 | bytes 2114048 | tf_op jit(solution)/shard_map/convert_element_type | solution.py:298
  49.2 0.6 collective-permute-start.1
  49.9 0.6 fusion
  50.5 2.4 %fusion.2.own_rec = bf16[320,4096]{1,0:T(8,128)(2,1)} fusion(bf16[320,4096]{1,0:T(8,128)(2,1)S(1)} %copy-done.4, f32[4096]{0:T(1024)S(1)} %convert_element_type.43, f32[320]{0:T(512)S(1)} %add_rsqrt_fusion), kind=kLoop, calls=%fused_computation.4 | loop fusion | flops 5242880 | bytes 5260544 | tf_op jit(solution)/shard_map/convert_element_type | solution.py:298
  53.6 0.1 reshape_squeeze.3
  53.6 0.2 reduce-window.8
  53.8 0.1 convert_reduce_fusion
  53.9 0.1 select_reduce_fusion.2
  54.0 0.1 select_reduce_fusion.1
  54.2 0.1 select_reduce_fusion.4
  54.3 0.3 fusion.7
  54.6 0.1 copy.29
  54.7 0.1 and.122
  55.0 0.2 select_reduce_fusion
  55.2 2.6 %copy-done = bf16[84,64,512]{2,1,0:T(8,128)(2,1)S(1)} copy-done((bf16[84,64,512]{2,1,0:T(8,128)(2,1)S(1)}, bf16[84,64,512]{2,1,0:T(8,128)(2,1)}, u32[]{:S(2)}) %copy-start) | copy-done | bytes 5505048
  57.9 9.2 %take_pages.1.pages_hbm = bf16[84,64,512]{2,1,0:T(8,128)(2,1)S(1)} custom-call(s32[84]{0:T(128)S(1)} %pad_add_fusion.1.slots, bf16[84,64,512]{2,1,0:T(8,128)(2,1)S(1)} %copy-done), custom_call_target="tpu_custom_call" | custom-call | bytes 22000000 | tf_op jit(solution)/shard_map/take_pages/pallas_call | solution.py:172
  67.1 2.4 %copy-done.1 = bf16[84,64,512]{2,1,0:T(8,128)(2,1)} copy-done((bf16[84,64,512]{2,1,0:T(8,128)(2,1)}, bf16[84,64,512]{2,1,0:T(8,128)(2,1)S(1)}, u32[]{:S(2)}) %copy-start.1) | copy-done | bytes 5505048
  69.5 0.7 fusion.18
  70.2 0.1 and_select_fusion.bias_private
  70.3 0.1 reshape.314
  70.5 0.2 fusion.8
  70.7 0.2 fusion.10.own_line
  70.9 0.2 fusion.14
  71.1 0.6 collective-permute-start.2
  71.8 1.0 multiply_cosine_fusion
  72.8 0.3 pad_maximum_fusion.tab_own
  73.0 0.3 collective-permute-start
  73.3 0.8 pad_add_fusion.2.info
  74.3 1.0 collective-permute-done.tab_oth
  75.2 47.4 %all-gather.2.cloned.1.call-done = bf16[4096,1280]{1,0:T(8,128)(2,1)} async-done(((bf16[256,1280]{1,0:T(8,128)(2,1)}), bf16[4096,1280]{1,0:T(8,128)(2,1)}) %all-gather.2.cloned.1.call-update) | async-done | bytes 10485776 | tf_op jit(solution)/shard_map/all_gather | solution.py:338
  122.6 9.6 %project.1 = (bf16[192,1024]{1,0:T(8,128)(2,1)S(1)}, bf16[512,256]{1,0:T(8,128)(2,1)S(1)}, bf16[320,1024]{1,0:T(8,128)(2,1)S(1)}) custom-call(bf16[16,2,2,4,16,1280]{5,4,3,2,1,0:T(8,128)(2,1)} %bitcast.44, bf16[128,4096]{1,0:T(8,128)(2,1)} %fusion.5.own_pre, bf16[64,4096]{1,0:T(8,128)(2,1)S(1)} %fusion.10.own_line, bf16[320,4096]{1,0:T(8,128)(2,1)} %fusion.2.own_rec, ...), custom_call_target="tpu_custom_call" | custom-call | flops 6000000000 | bytes 20000000 | tf_op jit(solution)/shard_map/project/pallas_call | solution.py:108
  132.2 0.8 collective-permute-start.4
  132.9 1.7 %collective-permute-done.4.packed = bf16[320,1024]{1,0:T(8,128)(2,1)S(1)} collective-permute-done((bf16[320,1024]{1,0:T(8,128)(2,1)S(1)}, bf16[320,1024]{1,0:T(8,128)(2,1)S(1)}, u32[]{:S(2)}, u32[]{:S(2)}) %collective-permute-start.4) | collective-permute-done | bytes 655392 | tf_op jit(solution)/shard_map/ppermute | solution.py:401
  134.7 2.4 %shared.1 = bf16[16,4,2176]{2,1,0:T(4,128)(2,1)} custom-call(s32[4]{0:T(128)S(1)} %pad_add_fusion.2.info, bf16[192,1024]{1,0:T(8,128)(2,1)S(1)} %get-tuple-element.19.q_own, bf16[320,1024]{1,0:T(8,128)(2,1)S(1)} %collective-permute-done.4.packed, bf16[512,512]{1,0:T(8,128)(2,1)S(1)} %copy-done.3), custom_call_target="tpu_custom_call" | custom-call | flops 300000000 | bytes 1000000 | tf_op jit(solution)/shard_map/shared/pallas_call | solution.py:151
  137.1 7.0 %all-to-all-start.2 = ((bf16[16,4,2176]{2,1,0:T(4,128)(2,1)}), bf16[16,4,2176]{2,1,0:T(4,128)(2,1)S(1)}, u32[]{:S(2)}, u32[]{:S(2)}) async-start(bf16[16,4,2176]{2,1,0:T(4,128)(2,1)} %shared.1), calls=%async_computation.2 | async-start | bytes 557056 | tf_op jit(solution)/shard_map/all_to_all | solution.py:403
  144.1 8.4 %local.1 = (bf16[128,2048]{1,0:T(8,128)(2,1)}, f32[64,128]{1,0:T(8,128)S(1)}, f32[64,128]{1,0:T(8,128)S(1)}) custom-call(s32[4]{0:T(128)S(1)} %pad_add_fusion.2.info, bf16[192,1024]{1,0:T(8,128)(2,1)S(1)} %get-tuple-element.19.q_own, bf16[512,256]{1,0:T(8,128)(2,1)S(1)} %get-tuple-element.20.kv_own, bf16[320,1024]{1,0:T(8,128)(2,1)S(1)} %collective-permute-done.4.packed, ...), custom_call_target="tpu_custom_call" | custom-call | flops 10000000000 | bytes 8000000 | tf_op jit(solution)/shard_map/local/pallas_call | solution.py:256
  152.6 1.7 %all-to-all-done.2.shared = bf16[16,4,2176]{2,1,0:T(4,128)(2,1)S(1)} async-done(((bf16[16,4,2176]{2,1,0:T(4,128)(2,1)}), bf16[16,4,2176]{2,1,0:T(4,128)(2,1)S(1)}, u32[]{:S(2)}, u32[]{:S(2)}) %all-to-all-start.2) | async-done | bytes 278560 | tf_op jit(solution)/shard_map/all_to_all | solution.py:403
  154.3 1.5 finish.1
  (60 shorter events, 0.8 us)
Async XLA Ops:
  7.2 30.7 %copy-start.11 = (s32[1,16]{1,0:T(1,128)S(1)}, s32[1,16]{1,0:T(1,128)}, u32[]{:S(2)}) copy-start(s32[1,16]{1,0:T(1,128)} %param.27) | copy-start | bytes 196
  7.2 30.7 %copy-start.2 = (s32[1,4]{1,0:T(1,128)S(1)}, s32[1,4]{1,0:T(1,128)}, u32[]{:S(2)}) copy-start(s32[1,4]{1,0:T(1,128)} %param.26) | copy-start | bytes 52
  7.2 30.9 %copy-start.7 = (s32[1,4]{1,0:T(1,128)S(1)}, s32[1,4]{1,0:T(1,128)}, u32[]{:S(2)}) copy-start(s32[1,4]{1,0:T(1,128)} %param.24) | copy-start | bytes 52
  7.2 31.1 %copy-start.5 = (bf16[4,4096]{1,0:T(4,128)(2,1)S(1)}, bf16[4,4096]{1,0:T(4,128)(2,1)}, u32[]{:S(2)}) copy-start(bf16[4,4096]{1,0:T(4,128)(2,1)} %param.17) | copy-start | bytes 98308
  7.2 37.9 %copy-start.6 = (bf16[4096]{0:T(1024)(128)(2,1)S(1)}, bf16[4096]{0:T(1024)(128)(2,1)}, u32[]{:S(2)}) copy-start(bf16[4096]{0:T(1024)(128)(2,1)} %param.19) | copy-start | bytes 24580
  7.2 115.4 %all-gather.2.cloned.1.call-start = ((), (), s32[]{:S(2)}) async-start(), calls=%async_computation.3 | async-start | bytes 11141120 | tf_op jit(solution)/shard_map/all_gather | solution.py:338
  37.8 12.0 %copy-start.4 = (bf16[320,4096]{1,0:T(8,128)(2,1)S(1)}, bf16[320,4096]{1,0:T(8,128)(2,1)}, u32[]{:S(2)}) copy-start(bf16[320,4096]{1,0:T(8,128)(2,1)} %param.18) | copy-start | bytes 7864324
  39.4 31.0 %all-to-all-start.1 = ((bf16[16,4,4224]{2,1,0:T(4,128)(2,1)}), bf16[16,4,4224]{2,1,0:T(4,128)(2,1)S(1)}, u32[]{:S(2)}, u32[]{:S(2)}) async-start(bf16[16,4,4224]{2,1,0:T(4,128)(2,1)} %broadcast_in_dim.131), calls=%async_computation.1 | async-start | bytes 1081344 | tf_op jit(solution)/shard_map/all_to_all | solution.py:360
  49.2 73.4 %collective-permute-start.1 = (bf16[128,4096]{1,0:T(8,128)(2,1)}, bf16[128,4096]{1,0:T(8,128)(2,1)}, u32[]{:S(2)}, u32[]{:S(2)}) collective-permute-start(bf16[128,4096]{1,0:T(8,128)(2,1)} %fusion.5.own_pre), channel_id=1, source_target_pairs={{0,16},{16,0},{1,17},{17,1},{2,18},{18,2},{3,19},{19,3},{4,20},{20... | collective-permute-start | bytes 3145736 | tf_op jit(solution)/shard_map/ppermute | solution.py:377
  50.5 3.1 %copy-start.8 = (s32[1,4,48]{2,1,0:T(4,128)S(1)}, s32[1,4,48]{2,1,0:T(4,128)}, u32[]{:S(2)}) copy-start(s32[1,4,48]{2,1,0:T(4,128)} %param.25) | copy-start | bytes 2308
  50.5 3.3 %copy-start.9 = (s32[1,320]{1,0:T(1,128)S(1)}, s32[1,320]{1,0:T(1,128)}, u32[]{:S(2)}) copy-start(s32[1,320]{1,0:T(1,128)} %param.30) | copy-start | bytes 3844
  50.5 3.6 %copy-start.10 = (s32[1,320]{1,0:T(1,128)S(1)}, s32[1,320]{1,0:T(1,128)}, u32[]{:S(2)}) copy-start(s32[1,320]{1,0:T(1,128)} %param.31) | copy-start | bytes 3844
  50.5 4.6 %copy-start.12 = (s32[1,16]{1,0:T(1,128)S(1)}, s32[1,16]{1,0:T(1,128)}, u32[]{:S(2)}) copy-start(s32[1,16]{1,0:T(1,128)} %param.29) | copy-start | bytes 196
  52.9 69.7 %collective-permute-start.3 = (bf16[320,4096]{1,0:T(8,128)(2,1)}, bf16[320,4096]{1,0:T(8,128)(2,1)}, u32[]{:S(2)}, u32[]{:S(2)}) collective-permute-start(bf16[320,4096]{1,0:T(8,128)(2,1)} %fusion.2.own_rec), channel_id=1, source_target_pairs={{0,16},{16,0},{1,17},{17,1},{2,18},{18,2},{3,19},{19,3},{4,20},{20... | collective-permute-start | bytes 7864328 | tf_op jit(solution)/shard_map/ppermute | solution.py:377
  55.2 2.6 %copy-start = (bf16[84,64,512]{2,1,0:T(8,128)(2,1)S(1)}, bf16[84,64,512]{2,1,0:T(8,128)(2,1)}, u32[]{:S(2)}) copy-start(bf16[84,64,512]{2,1,0:T(8,128)(2,1)} %pool.1) | copy-start | bytes 16515076
  67.1 2.4 %copy-start.1 = (bf16[84,64,512]{2,1,0:T(8,128)(2,1)}, bf16[84,64,512]{2,1,0:T(8,128)(2,1)S(1)}, u32[]{:S(2)}) copy-start(bf16[84,64,512]{2,1,0:T(8,128)(2,1)S(1)} %take_pages.1.pages_hbm) | copy-start | bytes 16515076
  71.1 51.5 %collective-permute-start.2 = (bf16[64,4096]{1,0:T(8,128)(2,1)S(1)}, bf16[64,4096]{1,0:T(8,128)(2,1)S(1)}, u32[]{:S(2)}, u32[]{:S(2)}) collective-permute-start(bf16[64,4096]{1,0:T(8,128)(2,1)S(1)} %fusion.10.own_line), channel_id=1, source_target_pairs={{0,16},{16,0},{1,17},{17,1},{2,18},{18,2},{3,19},{19,3},{4,20},{20... | collective-permute-start | bytes 1572872 | tf_op jit(solution)/shard_map/ppermute | solution.py:377
  73.0 2.2 %collective-permute-start = (f32[512,256]{1,0:T(8,128)S(1)}, f32[512,256]{1,0:T(8,128)S(1)}, u32[]{:S(2)}, u32[]{:S(2)}) collective-permute-start(f32[512,256]{1,0:T(8,128)S(1)} %pad_maximum_fusion.tab_own), channel_id=1, source_target_pairs={{0,16},{16,0},{1,17},{17,1},{2,18},{18,2},{3,19},{19,3},{4,20},{20... | collective-permute-start | bytes 1572872 | tf_op jit(solution)/shard_map/ppermute | solution.py:378
  122.6 12.1 %copy-start.3 = (bf16[512,512]{1,0:T(8,128)(2,1)S(1)}, bf16[512,512]{1,0:T(8,128)(2,1)}, u32[]{:S(2)}) copy-start(bf16[512,512]{1,0:T(8,128)(2,1)} %kv.1) | copy-start | bytes 1572868
  132.2 2.5 %collective-permute-start.4 = (bf16[320,1024]{1,0:T(8,128)(2,1)S(1)}, bf16[320,1024]{1,0:T(8,128)(2,1)S(1)}, u32[]{:S(2)}, u32[]{:S(2)}) collective-permute-start(bf16[320,1024]{1,0:T(8,128)(2,1)S(1)} %get-tuple-element.21), channel_id=1, source_target_pairs={{0,16},{16,0},{1,17},{17,1},{2,18},{18,2},{3,19},{19,3},{4,20},{20... | collective-permute-start | bytes 1966088 | tf_op jit(solution)/shard_map/ppermute | solution.py:401
  137.1 17.2 %all-to-all-start.2 = ((bf16[16,4,2176]{2,1,0:T(4,128)(2,1)}), bf16[16,4,2176]{2,1,0:T(4,128)(2,1)S(1)}, u32[]{:S(2)}, u32[]{:S(2)}) async-start(bf16[16,4,2176]{2,1,0:T(4,128)(2,1)} %shared.1), calls=%async_computation.2 | async-start | bytes 557056 | tf_op jit(solution)/shard_map/all_to_all | solution.py:403
Sparse Core Ops, SparseCore 0:
  38.0 84.5 all-gather.1

commit v8 on v5

--- a/solution.py
+++ b/solution.py
@@ -60,8 +60,9 @@
 
 
 def project_kernel(
-    info, main_hbm, z0, up1, down1, up2, down2, up3, down3, up4, down4, x, tab_own, tab_oth,
-    q_own, kv_own, packed, main, side, main_sem, side_sem,
+    info, main_hbm, z0, up1, down1, up2, down2, up3, down3, up4, down4,
+    own_pre, own_line, own_rec, other_pre, other_line, other_rec, tab_own, tab_oth,
+    q_own, kv_own, packed, main, side, x, main_sem, side_sem, x_sem,
 ):
     here = info[4]
     side_copies = []
@@ -83,9 +84,14 @@
                         main_sem.at[k, xi * 4 + yi],
                     )
                 )
-    for copy in side_copies + main_copies:
+    x_copies = []
+    at = 0
+    for part in (own_pre, own_line, other_pre, other_line, own_rec, other_rec):
+        x_copies.append(pltpu.make_async_copy(part, x.at[at : at + part.shape[0]], x_sem.at[len(x_copies)]))
+        at += part.shape[0]
+    for copy in x_copies[:4] + main_copies + side_copies + x_copies[4:]:
         copy.start()
-    for copy in side_copies:
+    for copy in x_copies[:4]:
         copy.wait()
 
     def store_queries(acc, first_head):
@@ -95,6 +101,15 @@
             q_own[:, at] = turned(part[:QROWS], tab_own[0:QROWS, :]).astype(bf16)
             packed[0:QROWS, at] = turned(part[QROWS:], tab_oth[0:QROWS, :]).astype(bf16)
 
+    main_flat = main.reshape(MODEL, MAIN)
+    for k, (lo, hi) in enumerate(groups):
+        for copy in main_copies[k * 16 : (k + 1) * 16]:
+            copy.wait()
+        for c0 in range(lo, hi, 256):
+            c1 = min(c0 + 256, hi)
+            store_queries(dot(x[0 : 2 * QROWS, :], main_flat[:, c0:c1]), c0 // HEAD_SIZE)
+    for copy in side_copies + x_copies[4:]:
+        copy.wait()
     side_flat = side.reshape(MODEL, SIDE)
     acc = dot(x[...], side_flat[:, SIDE - 256 :])
     for own in (True, False):
@@ -113,16 +128,9 @@
                 packed[QROWS:, b * 256 : b * 256 + 128] = keys[rows]
                 packed[QROWS:, b * 256 + 128 : (b + 1) * 256] = values[rows]
     store_queries(dot(x[0 : 2 * QROWS, :], side_flat[:, : SIDE - 256]), MAIN // HEAD_SIZE)
-    main_flat = main.reshape(MODEL, MAIN)
-    for k, (lo, hi) in enumerate(groups):
-        for copy in main_copies[k * 16 : (k + 1) * 16]:
-            copy.wait()
-        for c0 in range(lo, hi, 256):
-            c1 = min(c0 + 256, hi)
-            store_queries(dot(x[0 : 2 * QROWS, :], main_flat[:, c0:c1]), c0 // HEAD_SIZE)
-
-
-def project(info, main, side, rows, tab_own, tab_oth):
+
+
+def project(info, main, side, own, other, tab_own, tab_oth):
     return pl.pallas_call(
         project_kernel,
         name="project",
@@ -131,17 +139,19 @@
             jax.ShapeDtypeStruct((ROWS, 2 * HEAD_SIZE), bf16),
             jax.ShapeDtypeStruct((QROWS + 128, HALF), bf16),
         ),
-        in_specs=[SMEM] + [ANY] * 10 + [VMEM] * 3,
+        in_specs=[SMEM] + [ANY] * 16 + [VMEM] * 2,
         out_specs=(VMEM, VMEM, VMEM),
         scratch_shapes=[
             pltpu.VMEM((2, 4, 2, 4, 4, 16, MAIN), bf16),
             pltpu.VMEM((2, 4, 2, 4, 4, 16, SIDE), bf16),
+            pltpu.VMEM((2 * ROWS, MODEL), bf16),
             pltpu.SemaphoreType.DMA((2, 16)),
             pltpu.SemaphoreType.DMA((9,)),
+            pltpu.SemaphoreType.DMA((6,)),
         ],
-        compiler_params=pltpu.CompilerParams(vmem_limit_bytes=46 << 20),
+        compiler_params=pltpu.CompilerParams(vmem_limit_bytes=50 << 20),
         cost_estimate=pl.CostEstimate(flops=6 * 10**9, bytes_accessed=20 * 10**6, transcendentals=0),
-    )(info, main, *side, rows, tab_own, tab_oth)
+    )(info, main, *side, *own, *other, tab_own, tab_oth)
 
 
 def shared_kernel(info, q_own, packed, kv, out, qs):
@@ -178,7 +188,7 @@
 def shared_attention(info, q_own, packed, kv):
     return pl.pallas_call(shared_kernel, name="shared", out_shape=jax.ShapeDtypeStruct((16, 4, STAT + 128), bf16),
         in_specs=[SMEM, VMEM, VMEM, VMEM], out_specs=VMEM, scratch_shapes=[pltpu.VMEM((2, LINE, HALF), bf16)],
-        compiler_params=pltpu.CompilerParams(vmem_limit_bytes=16 << 20),
+        compiler_params=pltpu.CompilerParams(vmem_limit_bytes=8 << 20),
         cost_estimate=pl.CostEstimate(flops=3 * 10**8, bytes_accessed=10**6, transcendentals=10**6))(info, q_own, packed, kv)
 
 
@@ -286,7 +296,7 @@
         out_shape=(jax.ShapeDtypeStruct((PRE, QUERY_HEADS * HEAD_SIZE), bf16), jax.ShapeDtypeStruct((64, HEAD_SIZE), f32), jax.ShapeDtypeStruct((64, HEAD_SIZE), f32)),
         in_specs=[SMEM, ANY, ANY, VMEM, VMEM, VMEM, HBM], out_specs=(VMEM, VMEM, VMEM),
         scratch_shapes=[pltpu.VMEM((2, QROWS, HALF), bf16), pltpu.VMEM((2, ROWS, 2 * HEAD_SIZE), bf16), pltpu.VMEM((DEC_SLOTS + HIST_SLOTS, PAGE_TOKENS, 4 * HEAD_SIZE), bf16), pltpu.SemaphoreType.DMA((4,))],
-        compiler_params=pltpu.CompilerParams(vmem_limit_bytes=48 << 20),
+        compiler_params=pltpu.CompilerParams(vmem_limit_bytes=50 << 20),
         cost_estimate=pl.CostEstimate(flops=10**10, bytes_accessed=8 * 10**6, transcendentals=3 * 10**6),
     )(info, q_own, kv_own, packed, bias_private, bias_new, pages)
 
@@ -336,9 +346,18 @@
 
 
 def weight_block(w_query, key_value_weight):
-    key_half = key_value_weight.reshape(16, 2, 2, HEAD_SIZE)
+    def cut(array, c, width, start=0):
+        return array[:, start + c * width : start + (c + 1) * width]
+
     halves = [
-        jnp.concatenate([w_query[:, c * HALF : (c + 1) * HALF], key_half[:, 0, c], key_half[:, 1, c]], axis=1)
+        jnp.concatenate(
+            [
+                cut(w_query, c, HALF),
+                cut(key_value_weight, c, HEAD_SIZE),
+                cut(key_value_weight, c, HEAD_SIZE, 2 * HEAD_SIZE),
+            ],
+            axis=1,
+        )
         for c in range(2)
     ]
     return jnp.stack(halves, axis=0)
@@ -380,9 +399,6 @@
     dec_pos = small_lookup(prefix_line, groups) + lengths
     parts = jnp.stack([dec_pos // 64, dec_pos % 64], axis=1).astype(bf16)
     extra = jnp.concatenate([x_dec, parts, jnp.zeros((DEC, 126), bf16)], axis=1)
-    normed_pre = rms_scaled(x_pre, norm_gain)
-    normed_rec = rms_scaled(rec_hidden, norm_gain)
-
     counts = (lengths + PAGE_TOKENS - 1) // PAGE_TOKENS
     ends = jnp.cumsum(counts)
     firsts = ends - counts
@@ -394,22 +410,22 @@
     dec_pages = small_lookup(page_table.reshape(-1), slot_request * page_table.shape[1] + slot_page)
     slots = jnp.concatenate([dec_pages, pre_table[0]], axis=0)
 
-    rest, normed_pre, slots = lax.optimization_barrier((rest, normed_pre, slots))
     plane = side_plane(rest)
     pages = take_pages(slots, cache_pool)
-    plane, pages = lax.optimization_barrier((plane, pages))
-    up1, down1 = ring_step(plane, plane)
-    up1, down1, extra = lax.optimization_barrier((up1, down1, extra))
+    plane, pages, extra, x_pre, rec_hidden = lax.optimization_barrier((plane, pages, extra, x_pre, rec_hidden))
     line = lax.all_to_all(
         jnp.broadcast_to(extra[None], (16, DEC, MODEL + 128)), DP, 0, 0, tiled=True
     ).reshape(LINE, MODEL + 128)
+    up1, down1 = ring_step(plane, plane)
+    normed_pre = rms_scaled(x_pre, norm_gain)
+    up1, down1, normed_pre = lax.optimization_barrier((up1, down1, normed_pre))
     up2, down2 = ring_step(up1, down1)
-    up2, down2, line = lax.optimization_barrier((up2, down2, line))
+    normed_rec = rms_scaled(rec_hidden, norm_gain)
+    up2, down2, normed_rec, line = lax.optimization_barrier((up2, down2, normed_rec, line))
     line_parts = line[:, MODEL : MODEL + 2].astype(jnp.int32)
     line_pos = line_parts[:, 0] * 64 + line_parts[:, 1]
     normed_line = rms_scaled(line[:, :MODEL], norm_gain)
     up3, down3 = ring_step(up2, down2)
-    up3, down3, normed_line = lax.optimization_barrier((up3, down3, normed_line))
     up4, down4 = ring_step(up3[:2], down3[2:])
     side = (plane, up1, down1, up2, down2, up3, down3, up4, down4)
 
@@ -426,7 +442,6 @@
     own = (normed_pre, normed_line, normed_rec)
     other = [lax.ppermute(v, "c", swap) for v in own]
     other_table = lax.ppermute(table, "c", swap)
-    rows = jnp.concatenate([own[0], own[1], other[0], other[1], own[2], other[2]], axis=0)
 
     key_pos = slot_page[:, None] * PAGE_TOKENS + jnp.arange(PAGE_TOKENS, dtype=jnp.int32)[None, :]
     valid = used[:, None] & (key_pos < small_lookup(lengths, slot_request)[:, None])
@@ -446,10 +461,10 @@
     depth = lax.axis_index("zh") * 4 + lax.axis_index("zl")
     info = jnp.stack([core, own_prefix, pre_start[0], place, depth]).astype(jnp.int32)
 
-    main, rows, table, other_table, bias_private, bias_new, info = lax.optimization_barrier(
-        (main, rows, table, other_table, bias_private, bias_new, info)
+    main, table, other_table, bias_private, bias_new, info = lax.optimization_barrier(
+        (main, table, other_table, bias_private, bias_new, info)
     )
-    q_own, kv_own, packed = project(info, main, side, rows, table, other_table)
+    q_own, kv_own, packed = project(info, main, side, own, other, table, other_table)
     packed = lax.ppermute(packed, "c", swap)
     shared_part = shared_attention(info, q_own, packed, shared_kv)
     shared_part = lax.all_to_all(shared_part, DP, 0, 0, tiled=True)

time: 197 us -> 165 us (0.84)
  waiting for transfers between devices: 46.8 us -> 31.7 us
  local copies, waits for them, and re-layouts: 29.5 us -> 17.7 us
  other arithmetic: 19 us -> 16.1 us
  Pallas kernels: 36.9 us -> 34.3 us
    ppermute x4, waiting for transfers between devices: 18.8 us -> 7.76 us  [ring_step(): lax.ppermute(up, AXES, along_z(1))]
    unnamed x36 -> x30, local copies, waits for them, and re-layouts: 17.4 us -> 9.63 us
    unnamed x2 -> x1, other arithmetic: 4.4 us -> 0.7 us
    concatenate x1 -> x0, local copies, waits for them, and re-layouts: 3.53 us -> none  [on_device(): jnp.concatenate([own[0], own[1], other[0], other[1], own[2], other[2]], a...]
    pallas_call x1, Pallas kernels: 15.3 us -> 12.7 us  [project(): pl.pallas_call(project_kernel, name='project', out_shape=(jax.ShapeDtypeS...]
    all_to_all x1, waiting for transfers between devices: 6.44 us -> 4.2 us  [on_device(): lax.all_to_all(jnp.broadcast_to(extra[None], (16, DEC, MODEL + 128)), DP,...]
    ppermute x4, waiting for transfers between devices: 6.62 us -> 4.61 us  [ring_step(): lax.ppermute(down, AXES, along_z(-1))]
    convert_element_type x3 -> x4, other arithmetic: 3.49 us -> 4.67 us  [rms_scaled(): return (widened * factor * gain.astype(f32)).astype(bf16)]
  transfers between devices with their start and end apart: 18 -> 18, of which waited for: 10 -> 9; matrix products, arithmetic and copies ran while one was open for 18% -> 14% of each run, Pallas kernels for 9% -> 11%
where the time goes in v8:
time: 165 us; the launch traced here: 164 us
  starting transfers between devices  48.9 us (30%)
  Pallas kernels  34.3 us (21%)
  waiting for transfers between devices  31.7 us (19%)
  local copies, waits for them, and re-layouts  17.7 us (11%)
  other arithmetic  16.1 us (10%)
  between operations  15 us (9%)
    all_to_all x1, waiting for transfers between devices, main_column(): return lax.all_to_all(sent, ('zh', 'c', 'zl'), 0, 0, tiled=True)  13.2 us
    pallas_call x1, Pallas kernels, project(): pl.pallas_call(project_kernel, name='project', out_shape=(jax.ShapeDtypeS...  12.7 us
    all_to_all x1, starting transfers between devices, main_column(): return lax.all_to_all(sent, ('zh', 'c', 'zl'), 0, 0, tiled=True)  9.98 us
    unnamed x30, local copies, waits for them, and re-layouts  9.63 us
    pallas_call x1, Pallas kernels, take_pages(): pl.pallas_call(pages_kernel, name='take_pages', out_shape=jax.ShapeDtypeS...  9.17 us
    pallas_call x1, Pallas kernels, local_attention(): pl.pallas_call(local_kernel, name='local', out_shape=(jax.ShapeDtypeStruc...  8.43 us
    ppermute x4, waiting for transfers between devices, ring_step(): lax.ppermute(up, AXES, along_z(1))  7.76 us
    ppermute x4, starting transfers between devices, ring_step(): lax.ppermute(up, AXES, along_z(1))  7.61 us
  transfers between devices with their start and end apart: 18, of which 9 were waited for; matrix products, arithmetic and copies ran while one was open for 14% of the time, Pallas kernels for 11%

profile of v8, /device:TPU:1, one launch (start us, length us, event | category | flops | bytes accessed | tf_op | source)
XLA Modules:
  0.0 164.0 jit_solution(6801314230031058921)
XLA Ops:
  7.2 0.7 fusion.22
  7.9 0.8 fusion.21
  8.7 0.8 broadcast_in_dim.133
  9.5 10.0 %all-to-all-start = ((bf16[16,16,896]{2,1,0:T(8,128)(2,1)}), bf16[16,16,896]{2,1,0:T(8,128)(2,1)S(1)}, u32[]{:S(2)}, u32[]{:S(2)}) async-start(bf16[16,16,896]{2,1,0:T(8,128)(2,1)} %bitcast.2), calls=%async_computation | async-start | bytes 917504 | tf_op jit(solution)/shard_map/all_to_all | solution.py:368
  19.6 13.2 %all-to-all-done = bf16[16,16,896]{2,1,0:T(8,128)(2,1)S(1)} async-done(((bf16[16,16,896]{2,1,0:T(8,128)(2,1)}), bf16[16,16,896]{2,1,0:T(8,128)(2,1)S(1)}, u32[]{:S(2)}, u32[]{:S(2)}) %all-to-all-start) | async-done | bytes 458784 | tf_op jit(solution)/shard_map/all_to_all | solution.py:368
  32.8 0.8 copy-done.10
  33.6 0.8 reshape_squeeze.3
  34.4 0.9 select_reduce_fusion.5
  38.2 0.7 select_reduce_fusion.2
  38.9 0.7 select_reduce_fusion.1
  40.4 0.7 select_reduce_fusion.4
  42.0 0.8 broadcast_in_dim.134
  42.7 7.3 %all-to-all-start.1 = ((bf16[32,16,384]{2,1,0:T(8,128)(2,1)}), bf16[32,16,384]{2,1,0:T(8,128)(2,1)S(1)}, u32[]{:S(2)}, u32[]{:S(2)}) async-start(bf16[32,16,384]{2,1,0:T(8,128)(2,1)} %bitcast.6), calls=%async_computation.1 | async-start | bytes 786432 | tf_op jit(solution)/shard_map/all_to_all | solution.py:373
  51.2 2.7 %copy-done = bf16[84,64,512]{2,1,0:T(8,128)(2,1)S(1)} copy-done((bf16[84,64,512]{2,1,0:T(8,128)(2,1)S(1)}, bf16[84,64,512]{2,1,0:T(8,128)(2,1)}, u32[]{:S(2)}) %copy-start) | copy-done | bytes 5505048
  53.9 9.2 %take_pages.1.pages_hbm = bf16[84,64,512]{2,1,0:T(8,128)(2,1)S(1)} custom-call(s32[84]{0:T(128)S(1)} %pad_add_fusion.1.slots, bf16[84,64,512]{2,1,0:T(8,128)(2,1)S(1)} %copy-done), custom_call_target="tpu_custom_call" | custom-call | bytes 22000000 | tf_op jit(solution)/shard_map/take_pages/pallas_call | solution.py:210
  63.1 2.4 %copy-done.1 = bf16[84,64,512]{2,1,0:T(8,128)(2,1)} copy-done((bf16[84,64,512]{2,1,0:T(8,128)(2,1)}, bf16[84,64,512]{2,1,0:T(8,128)(2,1)S(1)}, u32[]{:S(2)}) %copy-start.1) | copy-done | bytes 5505048
  65.5 2.5 %collective-permute-start.1 = (bf16[4,2,4,16,384]{4,3,2,1,0:T(8,128)(2,1)S(1)}, bf16[4,2,4,16,384]{4,3,2,1,0:T(8,128)(2,1)S(1)}, u32[]{:S(2)}, u32[]{:S(2)}) collective-permute-start(bf16[4,2,4,16,384]{4,3,2,1,0:T(8,128)(2,1)S(1)} %bitcast.39), channel_id=1, source_target_pairs={{0,140},{1,141},{2,142},{3,143},{4,0},{5,1},{6,2},{7,3},{8,4},{9,5... | collective-permute-start | bytes 1179656 | tf_op jit(solution)/shard_map/ppermute | solution.py:377
  68.5 1.0 broadcast_in_dim.143
  69.5 7.0 %all-to-all-start.2 = ((bf16[16,4,4224]{2,1,0:T(4,128)(2,1)}), bf16[16,4,4224]{2,1,0:T(4,128)(2,1)}, u32[]{:S(2)}, u32[]{:S(2)}) async-start(bf16[16,4,4224]{2,1,0:T(4,128)(2,1)} %broadcast_in_dim.143), calls=%async_computation.2 | async-start | bytes 1081344 | tf_op jit(solution)/shard_map/all_to_all | solution.py:416
  76.8 1.3 fusion.5.own_pre
  79.5 1.1 collective-permute-start.2
  80.6 1.6 collective-permute-start.3
  82.2 2.3 %fusion.2.own_rec = bf16[320,4096]{1,0:T(8,128)(2,1)} fusion(bf16[320,4096]{1,0:T(8,128)(2,1)S(1)} %copy-done.8, f32[4096]{0:T(1024)S(1)} %convert_element_type.41, f32[320]{0:T(512)S(1)} %add_rsqrt_fusion), kind=kLoop, calls=%fused_computation.4 | loop fusion | flops 5242880 | bytes 5260544 | tf_op jit(solution)/shard_map/convert_element_type | solution.py:336
  84.5 1.8 %collective-permute-start.9 = (bf16[128,4096]{1,0:T(8,128)(2,1)}, bf16[128,4096]{1,0:T(8,128)(2,1)}, u32[]{:S(2)}, u32[]{:S(2)}) collective-permute-start(bf16[128,4096]{1,0:T(8,128)(2,1)} %fusion.5.own_pre), channel_id=1, source_target_pairs={{0,16},{16,0},{1,17},{17,1},{2,18},{18,2},{3,19},{19,3},{4,20},{20... | collective-permute-start | bytes 3145736 | tf_op jit(solution)/shard_map/ppermute | solution.py:443
  86.3 4.2 %all-to-all-done.2 = bf16[16,4,4224]{2,1,0:T(4,128)(2,1)} async-done(((bf16[16,4,4224]{2,1,0:T(4,128)(2,1)}), bf16[16,4,4224]{2,1,0:T(4,128)(2,1)}, u32[]{:S(2)}, u32[]{:S(2)}) %all-to-all-start.2) | async-done | bytes 540704 | tf_op jit(solution)/shard_map/all_to_all | solution.py:416
  90.5 1.2 reshape.324
  91.7 1.8 %collective-permute-done.2.up2 = bf16[4,2,4,16,384]{4,3,2,1,0:T(8,128)(2,1)S(1)} collective-permute-done((bf16[4,2,4,16,384]{4,3,2,1,0:T(8,128)(2,1)S(1)}, bf16[4,2,4,16,384]{4,3,2,1,0:T(8,128)(2,1)S(1)}, u32[]{:S(2)}, u32[]{:S(2)}) %collective-permute-start.2) | collective-permute-done | bytes 393248 | tf_op jit(solution)/shard_map/ppermute | solution.py:377
  93.5 2.3 %collective-permute-done.3.down2 = bf16[4,2,4,16,384]{4,3,2,1,0:T(8,128)(2,1)S(1)} collective-permute-done((bf16[4,2,4,16,384]{4,3,2,1,0:T(8,128)(2,1)S(1)}, bf16[4,2,4,16,384]{4,3,2,1,0:T(8,128)(2,1)S(1)}, u32[]{:S(2)}, u32[]{:S(2)}) %collective-permute-start.3) | collective-permute-done | bytes 393248 | tf_op jit(solution)/shard_map/ppermute | solution.py:377
  95.8 3.7 %collective-permute-start.5 = (bf16[4,2,4,16,384]{4,3,2,1,0:T(8,128)(2,1)S(1)}, bf16[4,2,4,16,384]{4,3,2,1,0:T(8,128)(2,1)S(1)}, u32[]{:S(2)}, u32[]{:S(2)}) collective-permute-start(bf16[4,2,4,16,384]{4,3,2,1,0:T(8,128)(2,1)S(1)} %collective-permute-done.2.up2), channel_id=1, source_target_pairs={{0,4},{1,5},{2,6},{3,7},{4,8},{5,9},{6,10},{7,11},{8,12},{9,13},{1... | collective-permute-start | bytes 1179656 | tf_op jit(solution)/shard_map/ppermute | solution.py:377
  99.5 1.6 collective-permute-start.11
  101.4 1.0 multiply_cosine_fusion
  102.4 1.1 pad_maximum_fusion.tab_own
  103.7 1.0 fusion.10.own_line
  104.7 2.1 %collective-permute-done.5.up3 = bf16[4,2,4,16,384]{4,3,2,1,0:T(8,128)(2,1)S(1)} collective-permute-done((bf16[4,2,4,16,384]{4,3,2,1,0:T(8,128)(2,1)S(1)}, bf16[4,2,4,16,384]{4,3,2,1,0:T(8,128)(2,1)S(1)}, u32[]{:S(2)}, u32[]{:S(2)}) %collective-permute-start.5) | collective-permute-done | bytes 393248 | tf_op jit(solution)/shard_map/ppermute | solution.py:377
  106.8 2.1 %collective-permute-start.10 = (bf16[64,4096]{1,0:T(8,128)(2,1)}, bf16[64,4096]{1,0:T(8,128)(2,1)}, u32[]{:S(2)}, u32[]{:S(2)}) collective-permute-start(bf16[64,4096]{1,0:T(8,128)(2,1)} %fusion.10.own_line), channel_id=1, source_target_pairs={{0,16},{16,0},{1,17},{17,1},{2,18},{18,2},{3,19},{19,3},{4,20},{20... | collective-permute-start | bytes 1572872 | tf_op jit(solution)/shard_map/ppermute | solution.py:443
  110.3 2.3 %collective-permute-start.7 = (bf16[2,2,4,16,384]{4,3,2,1,0:T(8,128)(2,1)S(1)}, bf16[2,2,4,16,384]{4,3,2,1,0:T(8,128)(2,1)S(1)}, u32[]{:S(2)}, u32[]{:S(2)}) collective-permute-start(bf16[2,2,4,16,384]{4,3,2,1,0:T(8,128)(2,1)S(1)} %slice.58), channel_id=1, source_target_pairs={{0,4},{1,5},{2,6},{3,7},{4,8},{5,9},{6,10},{7,11},{8,12},{9,13},{1... | collective-permute-start | bytes 589832 | tf_op jit(solution)/shard_map/ppermute | solution.py:377
  113.9 3.6 %collective-permute-done.7.up4 = bf16[2,2,4,16,384]{4,3,2,1,0:T(8,128)(2,1)S(1)} collective-permute-done((bf16[2,2,4,16,384]{4,3,2,1,0:T(8,128)(2,1)S(1)}, bf16[2,2,4,16,384]{4,3,2,1,0:T(8,128)(2,1)S(1)}, u32[]{:S(2)}, u32[]{:S(2)}) %collective-permute-start.7) | collective-permute-done | bytes 196640 | tf_op jit(solution)/shard_map/ppermute | solution.py:377
  117.5 2.3 %collective-permute-done.8.down4 = bf16[2,2,4,16,384]{4,3,2,1,0:T(8,128)(2,1)S(1)} collective-permute-done((bf16[2,2,4,16,384]{4,3,2,1,0:T(8,128)(2,1)}, bf16[2,2,4,16,384]{4,3,2,1,0:T(8,128)(2,1)S(1)}, u32[]{:S(2)}, u32[]{:S(2)}) %collective-permute-start.8) | collective-permute-done | bytes 196640 | tf_op jit(solution)/shard_map/ppermute | solution.py:377
  119.7 12.7 %project.1 = (bf16[192,1024]{1,0:T(8,128)(2,1)S(1)}, bf16[512,256]{1,0:T(8,128)(2,1)S(1)}, bf16[320,1024]{1,0:T(8,128)(2,1)}) custom-call(s32[5]{0:T(128)S(1)} %stack.31.info, bf16[16,2,2,4,16,896]{5,4,3,2,1,0:T(8,128)(2,1)} %bitcast.49, bf16[4,2,4,16,384]{4,3,2,1,0:T(8,128)(2,1)S(1)} %bitcast.41, bf16[4,2,4,16,384]{4,3,2,1,0:T(8,128)(2,1)S(1)} %collective-permute-done.up1, ...), custom_call_target="tpu_custom_call" | custom-call | flops 6000000000 | bytes 20000000 | tf_op jit(solution)/shard_map/project/pallas_call | solution.py:134
  133.2 1.1 collective-permute-start.12
  134.3 1.9 %collective-permute-done.12.packed = bf16[320,1024]{1,0:T(8,128)(2,1)S(1)} collective-permute-done((bf16[320,1024]{1,0:T(8,128)(2,1)}, bf16[320,1024]{1,0:T(8,128)(2,1)S(1)}, u32[]{:S(2)}, u32[]{:S(2)}) %collective-permute-start.12) | collective-permute-done | bytes 655392 | tf_op jit(solution)/shard_map/ppermute | solution.py:468
  136.2 2.4 %shared.1 = bf16[16,4,2176]{2,1,0:T(4,128)(2,1)} custom-call(s32[5]{0:T(128)S(1)} %stack.31.info, bf16[192,1024]{1,0:T(8,128)(2,1)S(1)} %get-tuple-element.45.q_own, bf16[320,1024]{1,0:T(8,128)(2,1)S(1)} %collective-permute-done.12.packed, bf16[512,512]{1,0:T(8,128)(2,1)S(1)} %copy-done.3), custom_call_target="tpu_custom_call" | custom-call | flops 300000000 | bytes 1000000 | tf_op jit(solution)/shard_map/shared/pallas_call | solution.py:189
  138.6 0.7 copy-done.4
  139.4 5.9 %all-to-all-start.3 = ((bf16[16,4,2176]{2,1,0:T(4,128)(2,1)}), bf16[16,4,2176]{2,1,0:T(4,128)(2,1)S(1)}, u32[]{:S(2)}, u32[]{:S(2)}) async-start(bf16[16,4,2176]{2,1,0:T(4,128)(2,1)} %shared.1), calls=%async_computation.3 | async-start | bytes 557056 | tf_op jit(solution)/shard_map/all_to_all | solution.py:470
  145.3 1.0 copy-done.5
  146.2 0.9 copy-done.7
  147.2 8.4 %local.1 = (bf16[128,2048]{1,0:T(8,128)(2,1)}, f32[64,128]{1,0:T(8,128)S(1)}, f32[64,128]{1,0:T(8,128)S(1)}) custom-call(s32[5]{0:T(128)S(1)} %stack.31.info, bf16[192,1024]{1,0:T(8,128)(2,1)S(1)} %copy-done.5, bf16[512,256]{1,0:T(8,128)(2,1)S(1)} %copy-done.7, bf16[320,1024]{1,0:T(8,128)(2,1)S(1)} %collective-permute-done.12.packed, ...), custom_call_target="tpu_custom_call" | custom-call | flops 10000000000 | bytes 8000000 | tf_op jit(solution)/shard_map/local/pallas_call | solution.py:294
  155.7 1.5 finish.1
  (87 shorter events, 11.2 us)
Async XLA Ops:
  7.2 43.9 %copy-start.12 = (bf16[4096]{0:T(1024)(128)(2,1)S(1)}, bf16[4096]{0:T(1024)(128)(2,1)}, u32[]{:S(2)}) copy-start(bf16[4096]{0:T(1024)(128)(2,1)} %param.19) | copy-start | bytes 24580
  7.2 43.9 %copy-start.14 = (s32[1,16]{1,0:T(1,128)S(1)}, s32[1,16]{1,0:T(1,128)}, u32[]{:S(2)}) copy-start(s32[1,16]{1,0:T(1,128)} %param.29) | copy-start | bytes 196
  9.5 23.2 %all-to-all-start = ((bf16[16,16,896]{2,1,0:T(8,128)(2,1)}), bf16[16,16,896]{2,1,0:T(8,128)(2,1)S(1)}, u32[]{:S(2)}, u32[]{:S(2)}) async-start(bf16[16,16,896]{2,1,0:T(8,128)(2,1)} %bitcast.2), calls=%async_computation | async-start | bytes 917504 | tf_op jit(solution)/shard_map/all_to_all | solution.py:368
  19.5 94.3 %all-gather.2.cloned.1.call-start = ((), (), s32[]{:S(2)}) async-start(), calls=%async_computation.4 | async-start | bytes 7798784 | tf_op jit(solution)/shard_map/all_gather | solution.py:396
  32.8 0.8 copy-start.10
  42.7 22.8 %all-to-all-start.1 = ((bf16[32,16,384]{2,1,0:T(8,128)(2,1)}), bf16[32,16,384]{2,1,0:T(8,128)(2,1)S(1)}, u32[]{:S(2)}, u32[]{:S(2)}) async-start(bf16[32,16,384]{2,1,0:T(8,128)(2,1)} %bitcast.6), calls=%async_computation.1 | async-start | bytes 786432 | tf_op jit(solution)/shard_map/all_to_all | solution.py:373
  51.2 2.7 %copy-start = (bf16[84,64,512]{2,1,0:T(8,128)(2,1)S(1)}, bf16[84,64,512]{2,1,0:T(8,128)(2,1)}, u32[]{:S(2)}) copy-start(bf16[84,64,512]{2,1,0:T(8,128)(2,1)} %pool.1) | copy-start | bytes 16515076
  53.9 11.5 %copy-start.11 = (bf16[4,4096]{1,0:T(4,128)(2,1)S(1)}, bf16[4,4096]{1,0:T(4,128)(2,1)}, u32[]{:S(2)}) copy-start(bf16[4,4096]{1,0:T(4,128)(2,1)} %param.17) | copy-start | bytes 98308
  53.9 22.7 %copy-start.9 = (bf16[128,4096]{1,0:T(8,128)(2,1)S(1)}, bf16[128,4096]{1,0:T(8,128)(2,1)}, u32[]{:S(2)}) copy-start(bf16[128,4096]{1,0:T(8,128)(2,1)} %param.16) | copy-start | bytes 3145732
  63.0 2.4 %copy-start.1 = (bf16[84,64,512]{2,1,0:T(8,128)(2,1)}, bf16[84,64,512]{2,1,0:T(8,128)(2,1)S(1)}, u32[]{:S(2)}) copy-start(bf16[84,64,512]{2,1,0:T(8,128)(2,1)S(1)} %take_pages.1.pages_hbm) | copy-start | bytes 16515076
  65.5 13.7 %collective-permute-start.1 = (bf16[4,2,4,16,384]{4,3,2,1,0:T(8,128)(2,1)S(1)}, bf16[4,2,4,16,384]{4,3,2,1,0:T(8,128)(2,1)S(1)}, u32[]{:S(2)}, u32[]{:S(2)}) collective-permute-start(bf16[4,2,4,16,384]{4,3,2,1,0:T(8,128)(2,1)S(1)} %bitcast.39), channel_id=1, source_target_pairs={{0,140},{1,141},{2,142},{3,143},{4,0},{5,1},{6,2},{7,3},{8,4},{9,5... | collective-permute-start | bytes 1179656 | tf_op jit(solution)/shard_map/ppermute | solution.py:377
  68.0 11.5 %collective-permute-start = (bf16[4,2,4,16,384]{4,3,2,1,0:T(8,128)(2,1)S(1)}, bf16[4,2,4,16,384]{4,3,2,1,0:T(8,128)(2,1)S(1)}, u32[]{:S(2)}, u32[]{:S(2)}) collective-permute-start(bf16[4,2,4,16,384]{4,3,2,1,0:T(8,128)(2,1)S(1)} %bitcast.40), channel_id=1, source_target_pairs={{0,4},{1,5},{2,6},{3,7},{4,8},{5,9},{6,10},{7,11},{8,12},{9,13},{1... | collective-permute-start | bytes 1179656 | tf_op jit(solution)/shard_map/ppermute | solution.py:377
  69.5 21.0 %all-to-all-start.2 = ((bf16[16,4,4224]{2,1,0:T(4,128)(2,1)}), bf16[16,4,4224]{2,1,0:T(4,128)(2,1)}, u32[]{:S(2)}, u32[]{:S(2)}) async-start(bf16[16,4,4224]{2,1,0:T(4,128)(2,1)} %broadcast_in_dim.143), calls=%async_computation.2 | async-start | bytes 1081344 | tf_op jit(solution)/shard_map/all_to_all | solution.py:416
  76.5 2.1 %copy-start.8 = (bf16[320,4096]{1,0:T(8,128)(2,1)S(1)}, bf16[320,4096]{1,0:T(8,128)(2,1)}, u32[]{:S(2)}) copy-start(bf16[320,4096]{1,0:T(8,128)(2,1)} %param.18) | copy-start | bytes 7864324
  79.5 14.0 %collective-permute-start.2 = (bf16[4,2,4,16,384]{4,3,2,1,0:T(8,128)(2,1)S(1)}, bf16[4,2,4,16,384]{4,3,2,1,0:T(8,128)(2,1)S(1)}, u32[]{:S(2)}, u32[]{:S(2)}) collective-permute-start(bf16[4,2,4,16,384]{4,3,2,1,0:T(8,128)(2,1)S(1)} %collective-permute-done.up1), channel_id=1, source_target_pairs={{0,4},{1,5},{2,6},{3,7},{4,8},{5,9},{6,10},{7,11},{8,12},{9,13},{1... | collective-permute-start | bytes 1179656 | tf_op jit(solution)/shard_map/ppermute | solution.py:377
  80.6 15.2 %collective-permute-start.3 = (bf16[4,2,4,16,384]{4,3,2,1,0:T(8,128)(2,1)S(1)}, bf16[4,2,4,16,384]{4,3,2,1,0:T(8,128)(2,1)S(1)}, u32[]{:S(2)}, u32[]{:S(2)}) collective-permute-start(bf16[4,2,4,16,384]{4,3,2,1,0:T(8,128)(2,1)S(1)} %collective-permute-done.1.down1), channel_id=1, source_target_pairs={{0,140},{1,141},{2,142},{3,143},{4,0},{5,1},{6,2},{7,3},{8,4},{9,5... | collective-permute-start | bytes 1179656 | tf_op jit(solution)/shard_map/ppermute | solution.py:377
  84.5 24.3 %copy-start.13 = (s32[1,16]{1,0:T(1,128)S(1)}, s32[1,16]{1,0:T(1,128)}, u32[]{:S(2)}) copy-start(s32[1,16]{1,0:T(1,128)} %param.27) | copy-start | bytes 196
  84.5 29.4 %collective-permute-start.9 = (bf16[128,4096]{1,0:T(8,128)(2,1)}, bf16[128,4096]{1,0:T(8,128)(2,1)}, u32[]{:S(2)}, u32[]{:S(2)}) collective-permute-start(bf16[128,4096]{1,0:T(8,128)(2,1)} %fusion.5.own_pre), channel_id=1, source_target_pairs={{0,16},{16,0},{1,17},{17,1},{2,18},{18,2},{3,19},{19,3},{4,20},{20... | collective-permute-start | bytes 3145736 | tf_op jit(solution)/shard_map/ppermute | solution.py:443
  95.8 11.0 %collective-permute-start.5 = (bf16[4,2,4,16,384]{4,3,2,1,0:T(8,128)(2,1)S(1)}, bf16[4,2,4,16,384]{4,3,2,1,0:T(8,128)(2,1)S(1)}, u32[]{:S(2)}, u32[]{:S(2)}) collective-permute-start(bf16[4,2,4,16,384]{4,3,2,1,0:T(8,128)(2,1)S(1)} %collective-permute-done.2.up2), channel_id=1, source_target_pairs={{0,4},{1,5},{2,6},{3,7},{4,8},{5,9},{6,10},{7,11},{8,12},{9,13},{1... | collective-permute-start | bytes 1179656 | tf_op jit(solution)/shard_map/ppermute | solution.py:377
  99.5 10.8 %collective-permute-start.6 = (bf16[4,2,4,16,384]{4,3,2,1,0:T(8,128)(2,1)S(1)}, bf16[4,2,4,16,384]{4,3,2,1,0:T(8,128)(2,1)S(1)}, u32[]{:S(2)}, u32[]{:S(2)}) collective-permute-start(bf16[4,2,4,16,384]{4,3,2,1,0:T(8,128)(2,1)S(1)} %collective-permute-done.3.down2), channel_id=1, source_target_pairs={{0,140},{1,141},{2,142},{3,143},{4,0},{5,1},{6,2},{7,3},{8,4},{9,5... | collective-permute-start | bytes 1179656 | tf_op jit(solution)/shard_map/ppermute | solution.py:377
  99.5 20.2 %collective-permute-start.11 = (bf16[320,4096]{1,0:T(8,128)(2,1)}, bf16[320,4096]{1,0:T(8,128)(2,1)}, u32[]{:S(2)}, u32[]{:S(2)}) collective-permute-start(bf16[320,4096]{1,0:T(8,128)(2,1)} %fusion.2.own_rec), channel_id=1, source_target_pairs={{0,16},{16,0},{1,17},{17,1},{2,18},{18,2},{3,19},{19,3},{4,20},{20... | collective-permute-start | bytes 7864328 | tf_op jit(solution)/shard_map/ppermute | solution.py:443
  103.5 9.8 %collective-permute-start.4 = (f32[512,256]{1,0:T(8,128)}, f32[512,256]{1,0:T(8,128)}, u32[]{:S(2)}, u32[]{:S(2)}) collective-permute-start(f32[512,256]{1,0:T(8,128)} %pad_maximum_fusion.tab_own), channel_id=1, source_target_pairs={{0,16},{16,0},{1,17},{17,1},{2,18},{18,2},{3,19},{19,3},{4,20},{20... | collective-permute-start | bytes 1572872 | tf_op jit(solution)/shard_map/ppermute | solution.py:444
  106.8 7.1 %collective-permute-start.10 = (bf16[64,4096]{1,0:T(8,128)(2,1)}, bf16[64,4096]{1,0:T(8,128)(2,1)}, u32[]{:S(2)}, u32[]{:S(2)}) collective-permute-start(bf16[64,4096]{1,0:T(8,128)(2,1)} %fusion.10.own_line), channel_id=1, source_target_pairs={{0,16},{16,0},{1,17},{17,1},{2,18},{18,2},{3,19},{19,3},{4,20},{20... | collective-permute-start | bytes 1572872 | tf_op jit(solution)/shard_map/ppermute | solution.py:443
  110.3 7.1 %collective-permute-start.7 = (bf16[2,2,4,16,384]{4,3,2,1,0:T(8,128)(2,1)S(1)}, bf16[2,2,4,16,384]{4,3,2,1,0:T(8,128)(2,1)S(1)}, u32[]{:S(2)}, u32[]{:S(2)}) collective-permute-start(bf16[2,2,4,16,384]{4,3,2,1,0:T(8,128)(2,1)S(1)} %slice.58), channel_id=1, source_target_pairs={{0,4},{1,5},{2,6},{3,7},{4,8},{5,9},{6,10},{7,11},{8,12},{9,13},{1... | collective-permute-start | bytes 589832 | tf_op jit(solution)/shard_map/ppermute | solution.py:377
  113.3 6.4 %collective-permute-start.8 = (bf16[2,2,4,16,384]{4,3,2,1,0:T(8,128)(2,1)}, bf16[2,2,4,16,384]{4,3,2,1,0:T(8,128)(2,1)S(1)}, u32[]{:S(2)}, u32[]{:S(2)}) collective-permute-start(bf16[2,2,4,16,384]{4,3,2,1,0:T(8,128)(2,1)} %slice.59), channel_id=1, source_target_pairs={{0,140},{1,141},{2,142},{3,143},{4,0},{5,1},{6,2},{7,3},{8,4},{9,5... | collective-permute-start | bytes 589832 | tf_op jit(solution)/shard_map/ppermute | solution.py:377
  113.9 22.3 %copy-start.3 = (bf16[512,512]{1,0:T(8,128)(2,1)S(1)}, bf16[512,512]{1,0:T(8,128)(2,1)}, u32[]{:S(2)}) copy-start(bf16[512,512]{1,0:T(8,128)(2,1)} %kv.1) | copy-start | bytes 1572868
  132.5 0.7 copy-start.6
  133.2 3.0 %collective-permute-start.12 = (bf16[320,1024]{1,0:T(8,128)(2,1)}, bf16[320,1024]{1,0:T(8,128)(2,1)S(1)}, u32[]{:S(2)}, u32[]{:S(2)}) collective-permute-start(bf16[320,1024]{1,0:T(8,128)(2,1)} %get-tuple-element.47), channel_id=1, source_target_pairs={{0,16},{16,0},{1,17},{17,1},{2,18},{18,2},{3,19},{19,3},{4,20},{20... | collective-permute-start | bytes 1966088 | tf_op jit(solution)/shard_map/ppermute | solution.py:468
  138.6 0.7 copy-start.4
  139.4 16.3 %all-to-all-start.3 = ((bf16[16,4,2176]{2,1,0:T(4,128)(2,1)}), bf16[16,4,2176]{2,1,0:T(4,128)(2,1)S(1)}, u32[]{:S(2)}, u32[]{:S(2)}) async-start(bf16[16,4,2176]{2,1,0:T(4,128)(2,1)} %shared.1), calls=%async_computation.3 | async-start | bytes 557056 | tf_op jit(solution)/shard_map/all_to_all | solution.py:470
  145.2 1.0 copy-start.5
  146.2 0.9 copy-start.7
  147.2 8.5 %copy-start.2 = (s32[1,4]{1,0:T(1,128)S(1)}, s32[1,4]{1,0:T(1,128)}, u32[]{:S(2)}) copy-start(s32[1,4]{1,0:T(1,128)} %param.26) | copy-start | bytes 52
Sparse Core Ops, SparseCore 0:
  33.7 78.6 all-gather.1
